TPU v7x, 32 devices: a whole 2x2x4 slice. The times are simulated.
32 devices in a mesh: groups: 2 (over x), tm: 8 (over z, y), mp: 2 (over core).
Axes of the slice: x: 2, y: 2, z: 4, core: 2. Of those that a mesh axis runs over, the one named last changes fastest.
Arguments:
- branch_x: bfloat16 [8192, 4096], P(('groups', 'tm'), 'mp'), parts along dimension 0, may hold values from -6 to 6
- branch_y: bfloat16 [8192, 4096], P(('groups', 'tm'), 'mp'), parts along dimension 0, may hold values from -6 to 6
- queries: bfloat16 [8192, 4096], P(('groups', 'tm'), 'mp'), parts along dimension 0, may hold values from -1500 to 1500
- conv_weight: float32 [4, 4096], P(None, 'mp'), may hold values from -3 to 3
- conv_bias: float32 [4096], P('mp'), may hold values from -3 to 3
- gate_panel: bfloat16 [16, 256, 512], P('mp'), may hold values from -0.375 to 0.375
- gate_scale: float32 [16, 2, 512], P('mp'), may hold values from 0.5 to 2
- gate_bias: float32 [2, 4096], P(None, 'mp'), may hold values from -4 to 4
- decay_rate: float32 [4096], P('mp'), may hold values from 2.4414063e-05 to 0.05
- kv_panel: bfloat16 [4096, 512], P('mp'), may hold values from -0.09375 to 0.09375
- kv_scale: float32 [32, 512], P('mp'), may hold values from 0.5 to 2
- segment_ids: int32 [8192], P('groups'), parts along dimension 0, may hold values from 0 to 3, never falling along the last dimension, each value on 1 to 2048 neighbouring positions
Outputs:
- mixed: bfloat16 [8192, 4096], P(('groups', 'tm'), 'mp'), parts along dimension 0
- attended: bfloat16 [8192, 4096], P(('groups', 'tm'), 'mp'), parts along dimension 0
There are 2 independent parts, one for each index of `groups`. A program takes and returns all parts, laid end to end along the dimension named above; an argument that names none is the same for every part. Nothing has to cross between parts.
Inputs may be any that keep to these rules, and one draw needn't show every extreme that they name: `segment_ids`: never falls along the sequence; each of the 4 documents holds 1 to 2048 positions, one of them exactly 2048.
All inputs are finite; a program needn't handle non-finite values.
Results may differ from a plain program's by a relative error of at most 0.03.
Values may be sent and summed in bfloat16 or wider, within the bound.
No kernel may reach another device: no remote copies, remote signals or barrier semaphores. Data moves between devices by JAX's collectives and lax.ppermute only.
A program may use at most 128 MiB of HBM per device.

v0:
```python
import functools
import math

import jax
import jax.numpy as jnp
from jax import lax
from jax.experimental import pallas as pl
from jax.experimental.pallas import tpu as pltpu
from jax.sharding import PartitionSpec as P


HD = 256
CONV = 4
WINDOW = 2048
SCALE_ROWS = 128
DOCS = 4
SEGS = 8
MIX_GROUPS = 2
GROUP = 2
HIST = 4
LOG2E = 1.4426950408889634
LN2 = 0.6931471805599453
SINH = [-0.5 * LN2 ** (2 * k + 1) / math.factorial(2 * k + 1) for k in range(4)]
F32 = jnp.float32
BF16 = jnp.bfloat16


def ring(x, lag):
    n = lax.axis_size("tm")
    return lax.ppermute(x, "tm", [(i, (i + lag) % n) for i in range(n)])


def swap(x):
    n = lax.axis_size("tm")
    return lax.ppermute(x, "tm", [(i, i ^ 1) for i in range(n)])


def partner(x):
    return lax.ppermute(x, "mp", [(0, 1), (1, 0)])


def dequantized(panel, scale):
    rows = panel.shape[0]
    parts = []
    for g in range(rows // SCALE_ROWS):
        part = panel[g * SCALE_ROWS : (g + 1) * SCALE_ROWS, :].astype(F32)
        parts.append((part * scale[g : g + 1, :]).astype(BF16))
    return jnp.concatenate(parts, 0)


def recur_kernel(
    starts_ref,
    x_ref,
    halo_ref,
    cw_ref,
    cb_ref,
    panel_ref,
    scale_ref,
    gb_ref,
    rate_ref,
    h_ref,
    p_ref,
    ends_ref,
    tot_ref,
    keep,
    xs,
    co,
    gate,
):
    rows, width = x_ref.shape
    seg_len = rows // SEGS
    base = lax.axis_index("tm") * rows

    @pl.when(pl.program_id(0) == 0)
    def _():
        def fill(i, carry):
            pos = base + i - 2 + seg_len * lax.broadcasted_iota(jnp.int32, (SEGS, 128), 0)
            hit = pos == starts_ref[0]
            for d in range(1, DOCS):
                hit = hit | (pos == starts_ref[d])
            keep[pl.ds(pl.multiple_of(i * SEGS, SEGS), SEGS), :] = jnp.where(hit, 0.0, 1.0)
            return carry

        lax.fori_loop(0, seg_len + 2, fill, 0)

    pitch = seg_len + HIST
    for c in range(width // 128):
        lanes = slice(c * 128, (c + 1) * 128)
        xs[c, HIST + 1 : 2 * HIST, :] = halo_ref[:, lanes].astype(F32)
        for s in range(1, SEGS):
            past = x_ref[s * seg_len - 2 * HIST : s * seg_len, lanes].astype(F32)
            xs[c, s * pitch : s * pitch + 2 * HIST, :] = past
        for s in range(SEGS):
            rest = x_ref[s * seg_len : (s + 1) * seg_len, lanes].astype(F32)
            xs[c, s * pitch + 2 * HIST : (s + 1) * pitch + HIST, :] = rest

    def mask(i):
        m = keep[pl.ds(pl.multiple_of((i + 2) * SEGS, SEGS), SEGS), :]
        return jnp.concatenate([m] * (width // 128), 1)

    def row(i):
        return jnp.concatenate(
            [xs[c, pl.ds(2 * HIST + i, SEGS, stride=pitch), :] for c in range(width // 128)], 1
        )

    w = [jnp.broadcast_to(cw_ref[j : j + 1, :], (SEGS, width)) for j in range(CONV)]
    bias = jnp.broadcast_to(cb_ref[...], (SEGS, width))

    def conv_step(i, carry):
        a, b, c = carry
        x = row(i)
        m = mask(i)
        d = w[0] * x + m * c + bias
        c = w[1] * x + m * b
        b = w[2] * x + m * a
        a = w[3] * x
        return (a, b, c), d

    x3, x2, x1 = row(-3), row(-2), row(-1)
    a1 = w[3] * x1
    b1 = w[2] * x1 + mask(-1) * (w[3] * x2)
    c1 = w[1] * x1 + mask(-1) * (w[2] * x2 + mask(-2) * (w[3] * x3))

    def conv_pair(k, carry):
        carry, d0 = conv_step(2 * k, carry)
        carry, d1 = conv_step(2 * k + 1, carry)
        co[pl.ds(pl.multiple_of(k * 2 * SEGS, 2 * SEGS), 2 * SEGS), :] = jnp.concatenate([d0, d1], 0).astype(BF16)
        return carry

    lax.fori_loop(0, seg_len // 2, conv_pair, (a1, b1, c1), unroll=8)

    weight = dequantized(panel_ref[0], scale_ref[0]) * BF16(0.5)
    gate[...] = jnp.dot(co[...], weight, preferred_element_type=F32)

    bias_r = jnp.broadcast_to(gb_ref[0:1, :] * 0.5, (SEGS, width))
    bias_i = jnp.broadcast_to(gb_ref[1:2, :] * 0.5, (SEGS, width))
    rate4 = jnp.broadcast_to(rate_ref[...] * (-4.0 * LOG2E), (SEGS, width))

    def scan_step(i, conv, carry):
        h, p = carry
        at = pl.ds(pl.multiple_of(i * SEGS, SEGS), SEGS)
        m = mask(i)
        v = rate4 * (1.0 + jnp.tanh(gate[at, :width] + bias_r))
        ti = 1.0 + jnp.tanh(gate[at, width:] + bias_i)
        decay = jnp.exp2(v)
        s = v * v
        series = ((s * SINH[3] + SINH[2]) * s + SINH[1]) * s + SINH[0]
        quarter = decay * (v * series)
        half = quarter * lax.rsqrt(jnp.maximum(quarter, 1e-37))
        half = jnp.where(m > 0.0, half, 0.5)
        decay = decay * m
        h = decay * h + ti * (conv * half)
        p = p * decay
        for c in range(width // 128):
            h_ref[c, at, :] = h[:, c * 128 : (c + 1) * 128]
            p_ref[c, at, :] = p[:, c * 128 : (c + 1) * 128]
        return h, p

    def scan_pair(k, carry):
        conv = co[pl.ds(pl.multiple_of(k * 2 * SEGS, 2 * SEGS), 2 * SEGS), :].astype(F32)
        carry = scan_step(2 * k, conv[:SEGS], carry)
        return scan_step(2 * k + 1, conv[SEGS:], carry)

    h, p = lax.fori_loop(
        0,
        seg_len // 2,
        scan_pair,
        (jnp.zeros((SEGS, width), F32), jnp.ones((SEGS, width), F32)),
        unroll=8,
    )
    ends_ref[0] = p
    ends_ref[1] = h
    tp, th = p[0:1], h[0:1]
    for s in range(1, SEGS):
        th = p[s : s + 1] * th + h[s : s + 1]
        tp = tp * p[s : s + 1]
    tot_ref[0:1, :] = tp
    tot_ref[1:2, :] = th


def mix_kernel(h_ref, p_ref, ends_ref, in_ref, y_ref, panel_ref, scale_ref, mixed_ref, kv_ref, carry):
    rows, width = y_ref.shape
    seg_len = rows // SEGS

    @pl.when(pl.program_id(0) == 0)
    def _():
        kv_ref[...] = jnp.zeros_like(kv_ref)

    c = in_ref[...]
    for s in range(SEGS):
        carry[s : s + 1, :] = c
        c = ends_ref[0, s : s + 1, :] * c + ends_ref[1, s : s + 1, :]
    weight = dequantized(panel_ref[...], scale_ref[0])

    def natural(ref, g, s):
        return jnp.concatenate(
            [ref[g, pl.ds(s + k * 8 * SEGS, 8, stride=SEGS), :] for k in range(seg_len // 8)], 0
        )

    for s in range(SEGS):
        at = slice(s * seg_len, (s + 1) * seg_len)
        y = y_ref[at, :].astype(F32)
        inner = y * (0.7978845608028654 + (0.7978845608028654 * 0.044715) * (y * y))
        gelu = (0.5 * y) * (1.0 + jnp.tanh(inner))
        local_h = jnp.concatenate([natural(h_ref, g, s) for g in range(width // 128)], 1)
        local_p = jnp.concatenate([natural(p_ref, g, s) for g in range(width // 128)], 1)
        mixed_ref[at, :] = ((local_h + local_p * carry[s : s + 1, :]) * gelu).astype(BF16)
    kv_ref[...] += jnp.dot(mixed_ref[...], weight, preferred_element_type=F32)


def sum_kernel(a_ref, b_ref, own_ref, half_ref):
    both = a_ref[...] + b_ref[...]
    n = both.shape[0] // 2
    core = lax.axis_index("mp")
    for side in range(2):
        keys = both[side * n : (side + 1) * n, :HD].T.astype(BF16)
        values = both[side * n : (side + 1) * n, HD:].astype(BF16)
        own_ref[side, :HD, :] = keys
        own_ref[side, HD:, :] = values
    half_ref[...] = own_ref[core]


def attend_kernel(own, lags, has_prev, final, starts_ref, q_ref, *refs):
    refs = list(refs)
    take = lambda n: [refs.pop(0) for _ in range(n)]
    own_ref = take(1)[0] if own else None
    pairs = [take(2) for _ in lags]
    prev_acc, prev_m, prev_l = take(3) if has_prev else (None, None, None)
    out = take(1) if final else take(3)
    low, score, top = take(3)
    acc, m_ref, l_ref = take(3) if final else out
    rows = q_ref.shape[0]
    half = rows // 2
    me = lax.axis_index("tm")
    first = me * rows
    core = lax.axis_index("mp")
    turn = 2 * (me % 2) - 1
    scale = LOG2E / math.sqrt(HD)

    def lowest(t):
        d0 = jnp.maximum(t - (WINDOW - 1), 0)
        for d in range(DOCS):
            d0 = jnp.maximum(d0, jnp.where(starts_ref[d] <= t, starts_ref[d], 0))
        return d0

    @pl.when(pl.program_id(0) == 0)
    def _():
        low[...] = lowest(first + lax.broadcasted_iota(jnp.int32, (rows, 128), 0))

    lo_first = lowest(first)
    lo_last = lowest(first + rows - 1)

    def keys_of(pair, t):
        return own_ref[t, :HD, :] if pair is None else pair[t][:HD, :]

    def values_of(pair, t):
        return own_ref[t, HD:, :] if pair is None else pair[t][HD:, :]

    def score_pass(j, pair, start, masked):
        for h in range(GROUP):
            for t in range(2):
                r0 = half * t if pair is None else 0
                at = slice(r0, rows)
                s = jnp.dot(
                    q_ref[at, h * HD : (h + 1) * HD], keys_of(pair, t), preferred_element_type=F32
                )
                peak = top[h, at, :]
                for c in range(half // 128):
                    part = s[:, c * 128 : (c + 1) * 128] * scale
                    if masked:
                        side = t if pair is None else jnp.where(core == t, 0, 1)
                        kpos = lax.broadcasted_iota(jnp.int32, part.shape, 1) + (start + side * half + c * 128)
                        ok = kpos >= low[at, :]
                        if pair is None:
                            ok = ok & (kpos <= lax.broadcasted_iota(jnp.int32, part.shape, 0) + (first + r0))
                        part = jnp.where(ok, part, -1e30)
                    score[j, h, t, at, c * 128 : (c + 1) * 128] = part
                    peak = jnp.maximum(peak, part)
                top[h, at, :] = peak

    def value_pass(j, pair):
        for h in range(GROUP):
            spans = [(0, half, 1), (half, rows, 2)] if pair is None else [(0, rows, 2)]
            for r0, r1, n in spans:
                at = slice(r0, r1)
                m = m_ref[at, h * 128 : (h + 1) * 128]
                total = l_ref[at, h * 128 : (h + 1) * 128]
                ps, vs = [], []
                for t in range(n):
                    for c in range(half // 128):
                        p = jnp.exp2(score[j, h, t, at, c * 128 : (c + 1) * 128] - m)
                        total = total + p
                        ps.append(p.astype(BF16))
                    vs.append(values_of(pair, t))
                l_ref[at, h * 128 : (h + 1) * 128] = total
                acc[at, h * HD : (h + 1) * HD] += jnp.dot(
                    jnp.concatenate(ps, 1), jnp.concatenate(vs, 0), preferred_element_type=F32
                )

    tiles = [(None, first)] if own else []
    for k, (even_part, odd_part) in enumerate(lags):
        tiles.append((pairs[k], first - (even_part + odd_part * turn) * rows))
    live = [True if pair is None else (start >= 0) & (start < first) & (start + rows > lo_first) for pair, start in tiles]

    top[...] = jnp.full(top.shape, -1e30, F32)
    for j, (pair, start) in enumerate(tiles):
        if pair is None:
            score_pass(j, pair, start, True)
            continue

        @pl.when(live[j] & (start >= lo_last))
        def _(j=j, pair=pair, start=start):
            score_pass(j, pair, start, False)

        @pl.when(live[j] & (start < lo_last))
        def _(j=j, pair=pair, start=start):
            score_pass(j, pair, start, True)

    for h in range(GROUP):
        lanes = slice(h * 128, (h + 1) * 128)
        wide = slice(h * HD, (h + 1) * HD)
        m = jnp.broadcast_to(jnp.max(top[h], axis=1, keepdims=True), (rows, 128))
        if has_prev:
            m0 = prev_m[:, lanes]
            m = jnp.maximum(m, m0)
            fade = jnp.exp2(m0 - m)
            l_ref[:, lanes] = prev_l[:, lanes] * fade
            acc[:, wide] = prev_acc[:, wide] * jnp.concatenate([fade] * (HD // 128), 1)
        else:
            l_ref[:, lanes] = jnp.zeros((rows, 128), F32)
            acc[:, wide] = jnp.zeros((rows, HD), F32)
        m_ref[:, lanes] = m
    for j, (pair, start) in enumerate(tiles):
        if pair is None:
            value_pass(j, pair)
            continue

        @pl.when(live[j])
        def _(j=j, pair=pair):
            value_pass(j, pair)

    if final:
        for h in range(GROUP):
            total = jnp.sum(l_ref[:, h * 128 : (h + 1) * 128], axis=1, keepdims=True)
            share = jnp.broadcast_to(1.0 / total, (rows, 128))
            wide = slice(h * HD, (h + 1) * HD)
            out[0][:, wide] = (acc[:, wide] * jnp.concatenate([share] * (HD // 128), 1)).astype(BF16)


def recur_call(starts, x, halo, conv_weight, conv_bias, gate_panel, gate_scale, gate_bias, decay_rate):
    rows, channels = x.shape
    blocks, width, _ = gate_panel.shape
    col = lambda b, s: (0, b)
    return pl.pallas_call(
        recur_kernel,
        grid_spec=pltpu.PrefetchScalarGridSpec(
            num_scalar_prefetch=1,
            grid=(blocks,),
            in_specs=[
                pl.BlockSpec((rows, width), col),
                pl.BlockSpec((CONV - 1, width), col),
                pl.BlockSpec((CONV, width), col),
                pl.BlockSpec((1, width), col),
                pl.BlockSpec((1, width, 2 * width), lambda b, s: (b, 0, 0)),
                pl.BlockSpec((1, width // SCALE_ROWS, 2 * width), lambda b, s: (b, 0, 0)),
                pl.BlockSpec((2, width), col),
                pl.BlockSpec((1, width), col),
            ],
            out_specs=[
                pl.BlockSpec((width // 128, rows, 128), lambda b, s: (b, 0, 0)),
                pl.BlockSpec((width // 128, rows, 128), lambda b, s: (b, 0, 0)),
                pl.BlockSpec((2, SEGS, width), lambda b, s: (0, 0, b)),
                pl.BlockSpec((2, width), col),
            ],
            scratch_shapes=[
                pltpu.VMEM((rows + 2 * SEGS, 128), F32),
                pltpu.VMEM((width // 128, rows + HIST * (SEGS + 1), 128), F32),
                pltpu.VMEM((rows, width), BF16),
                pltpu.VMEM((rows, 2 * width), F32),
            ],
        ),
        out_shape=[
            jax.ShapeDtypeStruct((channels // 128, rows, 128), F32),
            jax.ShapeDtypeStruct((channels // 128, rows, 128), F32),
            jax.ShapeDtypeStruct((2, SEGS, channels), F32),
            jax.ShapeDtypeStruct((2, channels), F32),
        ],
        name="recur",
    )(starts, x, halo, conv_weight, conv_bias, gate_panel, gate_scale, gate_bias, decay_rate)


def mix_call(h, p, ends, incoming, y, kv_panel, kv_scale):
    rows, channels = y.shape
    width = MIX_GROUPS * SCALE_ROWS
    col = lambda b: (0, b)
    out = kv_panel.shape[1]
    return pl.pallas_call(
        mix_kernel,
        grid=(channels // width,),
        in_specs=[
            pl.BlockSpec((width // 128, rows, 128), lambda b: (b, 0, 0)),
            pl.BlockSpec((width // 128, rows, 128), lambda b: (b, 0, 0)),
            pl.BlockSpec((2, SEGS, width), lambda b: (0, 0, b)),
            pl.BlockSpec((1, width), col),
            pl.BlockSpec((rows, width), col),
            pl.BlockSpec((width, out), lambda b: (b, 0)),
            pl.BlockSpec((1, MIX_GROUPS, out), lambda b: (b, 0, 0)),
        ],
        out_specs=[pl.BlockSpec((rows, width), col), pl.BlockSpec((rows, out), lambda b: (0, 0))],
        out_shape=[jax.ShapeDtypeStruct((rows, channels), BF16), jax.ShapeDtypeStruct((rows, out), F32)],
        scratch_shapes=[pltpu.VMEM((SEGS, width), F32)],
        name="mix",
    )(h, p, ends, incoming, y, kv_panel, kv_scale.reshape(-1, MIX_GROUPS, out))


def sum_call(a, b):
    rows, _ = a.shape
    half = rows // 2
    return pl.pallas_call(
        sum_kernel,
        out_shape=[
            jax.ShapeDtypeStruct((2, 2 * HD, half), BF16),
            jax.ShapeDtypeStruct((2 * HD, half), BF16),
        ],
        compiler_params=pltpu.CompilerParams(vmem_limit_bytes=16 << 20),
        name="kvsum",
    )(a, b)


def attend_call(starts, q, own, halves, lags, prev, final):
    rows, width = q.shape
    heads = width // HD
    whole = lambda a: pl.BlockSpec(a.shape, lambda h, s: (0,) * a.ndim)
    per_head = lambda h, s: (0, h)
    held = [] if own is None else [own]
    held += halves
    carried = [pl.BlockSpec((rows, GROUP * n), per_head) for n in (HD, 128, 128)]
    tiles = len(lags) + (own is not None)
    if final:
        out_specs = pl.BlockSpec((rows, GROUP * HD), per_head)
        out_shape = jax.ShapeDtypeStruct((rows, width), BF16)
        extra = [pltpu.VMEM((rows, GROUP * n), F32) for n in (HD, 128, 128)]
    else:
        out_specs = carried
        out_shape = [jax.ShapeDtypeStruct((rows, heads * n), F32) for n in (HD, 128, 128)]
        extra = []
    return pl.pallas_call(
        functools.partial(attend_kernel, own is not None, lags, prev is not None, final),
        grid_spec=pltpu.PrefetchScalarGridSpec(
            num_scalar_prefetch=1,
            grid=(heads // GROUP,),
            in_specs=[pl.BlockSpec((rows, GROUP * HD), per_head)]
            + [whole(a) for a in held]
            + (carried if prev is not None else []),
            out_specs=out_specs,
            scratch_shapes=[
                pltpu.VMEM((rows, 128), jnp.int32),
                pltpu.VMEM((tiles, GROUP, 2, rows, rows // 2), F32),
                pltpu.VMEM((GROUP, rows, 128), F32),
            ]
            + extra,
        ),
        out_shape=out_shape,
        cost_estimate=pl.CostEstimate(
            flops=4 * tiles * rows * rows * width,
            bytes_accessed=4 * rows * width,
            transcendentals=tiles * rows * rows * heads,
        ),
        compiler_params=pltpu.CompilerParams(vmem_limit_bytes=32 << 20),
        name="attend_own" if own is not None else "attend_end" if final else "attend_mid",
    )(starts, q, *held, *(prev or []))


def local(
    branch_x,
    branch_y,
    queries,
    conv_weight,
    conv_bias,
    gate_panel,
    gate_scale,
    gate_bias,
    decay_rate,
    kv_panel,
    kv_scale,
    segment_ids,
):
    rows = branch_x.shape[0]
    seq = segment_ids.shape[0]
    me = lax.axis_index("tm")
    halo = ring(branch_x[rows - CONV + 1 :], 1)
    starts = jnp.sum(
        (segment_ids[None, :] < jnp.arange(DOCS, dtype=jnp.int32)[:, None]).astype(jnp.int32), axis=1
    )
    h, p, ends, tot = recur_call(
        starts,
        branch_x,
        halo,
        conv_weight,
        conv_bias[None],
        gate_panel,
        gate_scale,
        gate_bias,
        decay_rate[None],
    )
    odd = (me % 2) == 1
    near = swap(tot)
    lower = jnp.where(odd, near, tot)
    upper = jnp.where(odd, tot, near)
    level = jnp.stack([lower[0] * upper[0], upper[0] * lower[1] + upper[1]])
    levels = -(-(seq // 2) // (2 * rows))
    past = [ring(level, 2 * k) for k in range(1, levels + 1)]
    incoming = jnp.zeros_like(tot[1])
    for k in range(levels, 0, -1):
        got = past[k - 1]
        incoming = jnp.where(me >= 2 * k, got[0] * incoming + got[1], 0.0)
    incoming = jnp.where(odd, near[0] * incoming + near[1], incoming)
    mixed, partial_kv = mix_call(h, p, ends, incoming[None], branch_y, kv_panel, kv_scale)
    own, half = sum_call(partial_kv, partner(partial_kv))

    levels = -(-WINDOW // rows) // 2
    straight, attended = half, None
    for k in range(levels + 1):
        last = k == levels
        beyond = None if last else ring(straight, 2)
        crossed = swap(straight)
        if k == 0:
            attended = attend_call(starts, queries, own, [], [], None, False)
        else:
            attended = attend_call(starts, queries, None, tiles, lags, attended, False)
        tiles, lags = [crossed, partner(crossed)], [(2 * k, 1)]
        if not last:
            tiles += [beyond, partner(beyond)]
            lags.append((2 * k + 2, 0))
        straight = beyond
    attended = attend_call(starts, queries, None, tiles, lags, attended, True)
    return mixed, attended


def solution(mesh):
    in_specs = (
        P(("groups", "tm"), "mp"),
        P(("groups", "tm"), "mp"),
        P(("groups", "tm"), "mp"),
        P(None, "mp"),
        P("mp"),
        P("mp", None, None),
        P("mp", None, None),
        P(None, "mp"),
        P("mp"),
        P("mp", None),
        P("mp", None),
        P("groups"),
    )
    out_specs = (P(("groups", "tm"), "mp"), P(("groups", "tm"), "mp"))
    return jax.shard_map(local, mesh=mesh, in_specs=in_specs, out_specs=out_specs, check_vma=False)
```

profile of v0, /device:TPU:31, one launch (start us, length us, event | category | flops | bytes accessed | tf_op | source)
XLA Modules:
  0.0 91.7 jit_solution(11730286861479283806)
XLA Ops:
  0.6 0.8 slice.34
  1.5 1.3 %convert_reduce_fusion.starts_ref = s32[4]{0:T(128)} fusion(s32[4096]{0:T(1024)} %param.23), kind=kLoop, calls=%fused_computation | loop fusion | flops 49148 | bytes 16400 | tf_op jit(solution)/shard_map/reduce_sum | solution.py:492
  2.8 1.2 %collective-permute-done.halo_ref = bf16[3,2048]{1,0:T(4,128)(2,1)S(1)} collective-permute-done((bf16[3,2048]{1,0:T(4,128)(2,1)S(1)}, bf16[3,2048]{1,0:T(4,128)(2,1)S(1)}, u32[]{:S(2)}, u32[]{:S(2)}) %collective-permute-start) | collective-permute-done | bytes 12320 | tf_op jit(solution)/shard_map/ppermute | solution.py:30
  4.7 13.8 %recur.1 = (f32[16,512,128]{2,1,0:T(8,128)}, f32[16,512,128]{2,1,0:T(8,128)}, f32[2,8,2048]{2,1,0:T(8,128)}, f32[2,2048]{1,0:T(2,128)}) custom-call(s32[4]{0:T(128)} %convert_reduce_fusion.starts_ref, bf16[512,2048]{1,0:T(8,128)(2,1)} %x_ref.1, bf16[3,2048]{1,0:T(4,128)(2,1)} %copy-done.4, f32[4,2048]{1,0:T(4,128)} %cw_ref.1, f32[1,2048]{1,0:T(1,128)} %bitcast.2, ...), custom_call_target="tpu_custom_call" | custom-call | tf_op jit(solution)/shard_map/recur/pallas_call | solution.py:354
  18.5 1.2 %collective-permute-start.1 = (f32[2,2048]{1,0:T(2,128)}, f32[2,2048]{1,0:T(2,128)S(1)}, u32[]{:S(2)}, u32[]{:S(2)}) collective-permute-start(f32[2,2048]{1,0:T(2,128)} %get-tuple-element.22), channel_id=1, source_target_pairs={{0,2},{2,0},{4,6},{6,4},{8,10},{10,8},{12,14},{14,12},{1,3},{3,1},... | collective-permute-start | bytes 49160 | tf_op jit(solution)/shard_map/ppermute | solution.py:35
  19.6 1.7 %collective-permute-done.1 = f32[2,2048]{1,0:T(2,128)S(1)} collective-permute-done((f32[2,2048]{1,0:T(2,128)}, f32[2,2048]{1,0:T(2,128)S(1)}, u32[]{:S(2)}, u32[]{:S(2)}) %collective-permute-start.1) | collective-permute-done | bytes 16416 | tf_op jit(solution)/shard_map/ppermute | solution.py:35
  21.3 0.7 broadcast_select_fusion.2
  22.1 1.6 %collective-permute-start.2 = (f32[2,2048]{1,0:T(2,128)S(1)}, f32[2,2048]{1,0:T(2,128)S(1)}, u32[]{:S(2)}, u32[]{:S(2)}) collective-permute-start(f32[2,2048]{1,0:T(2,128)S(1)} %pad_maximum_fusion), channel_id=1, source_target_pairs={{0,4},{2,6},{4,8},{6,10},{8,12},{10,14},{12,0},{14,2},{1,5},{3,7},... | collective-permute-start | bytes 49160 | tf_op jit(solution)/shard_map/ppermute | solution.py:30
  23.7 0.6 reshape.8.scale_ref
  24.7 2.4 %collective-permute-done.3 = f32[2,2048]{1,0:T(2,128)S(1)} collective-permute-done((f32[2,2048]{1,0:T(2,128)S(1)}, f32[2,2048]{1,0:T(2,128)S(1)}, u32[]{:S(2)}, u32[]{:S(2)}) %collective-permute-start.3) | collective-permute-done | bytes 16416 | tf_op jit(solution)/shard_map/ppermute | solution.py:30
  27.2 0.6 broadcast_select_fusion.4.in_ref
  27.8 9.5 %mix.1 = (bf16[512,2048]{1,0:T(8,128)(2,1)}, f32[512,512]{1,0:T(8,128)}) custom-call(f32[16,512,128]{2,1,0:T(8,128)} %get-tuple-element.19.h_ref, f32[16,512,128]{2,1,0:T(8,128)} %get-tuple-element.20.p_ref, f32[2,8,2048]{2,1,0:T(8,128)} %get-tuple-element.21.ends_ref, f32[1,2048]{1,0:T(1,128)} %broadcast_select_fusion.4.in_ref, bf16[512,2048]{1,0:T(8,128)(2,1)} %y_ref.1, ...), custom_call_target="tpu_custom_call" | custom-call | tf_op jit(solution)/shard_map/mix/pallas_call | solution.py:397
  37.3 4.2 %collective-permute-start.4 = (f32[512,512]{1,0:T(8,128)}, f32[512,512]{1,0:T(8,128)S(1)}, u32[]{:S(2)}, u32[]{:S(2)}) collective-permute-start(f32[512,512]{1,0:T(8,128)} %get-tuple-element.24.a_ref), channel_id=1, source_target_pairs={{0,1},{1,0},{2,3},{3,2},{4,5},{5,4},{6,7},{7,6},{8,9},{9,8},{10,11... | collective-permute-start | bytes 3145736 | tf_op jit(solution)/shard_map/ppermute | solution.py:39
  41.5 2.5 %collective-permute-done.4.b_ref = f32[512,512]{1,0:T(8,128)S(1)} collective-permute-done((f32[512,512]{1,0:T(8,128)}, f32[512,512]{1,0:T(8,128)S(1)}, u32[]{:S(2)}, u32[]{:S(2)}) %collective-permute-start.4) | collective-permute-done | bytes 1048608 | tf_op jit(solution)/shard_map/ppermute | solution.py:39
  44.0 1.2 %copy-done.1 = f32[512,512]{1,0:T(8,128)S(1)} copy-done((f32[512,512]{1,0:T(8,128)S(1)}, f32[512,512]{1,0:T(8,128)}, u32[]{:S(2)}) %copy-start.1) | copy-done | bytes 1048600
  46.0 1.7 %collective-permute-start.12 = (bf16[512,256]{1,0:T(8,128)(2,1)S(1)}, bf16[512,256]{1,0:T(8,128)(2,1)S(1)}, u32[]{:S(2)}, u32[]{:S(2)}) collective-permute-start(bf16[512,256]{1,0:T(8,128)(2,1)S(1)} %get-tuple-element.25), channel_id=1, source_target_pairs={{0,2},{2,0},{4,6},{6,4},{8,10},{10,8},{12,14},{14,12},{1,3},{3,1},... | collective-permute-start | bytes 786440 | tf_op jit(solution)/shard_map/ppermute | solution.py:35
  47.7 5.3 %collective-permute-done.5.refs_2_ = bf16[512,256]{1,0:T(8,128)(2,1)S(1)} collective-permute-done((bf16[512,256]{1,0:T(8,128)(2,1)S(1)}, bf16[512,256]{1,0:T(8,128)(2,1)S(1)}, u32[]{:S(2)}, u32[]{:S(2)}) %collective-permute-start.5) | collective-permute-done | bytes 262176 | tf_op jit(solution)/shard_map/ppermute | solution.py:30
  53.0 2.2 %collective-permute-start.6 = (bf16[512,256]{1,0:T(8,128)(2,1)S(1)}, bf16[512,256]{1,0:T(8,128)(2,1)S(1)}, u32[]{:S(2)}, u32[]{:S(2)}) collective-permute-start(bf16[512,256]{1,0:T(8,128)(2,1)S(1)} %collective-permute-done.5.refs_2_), channel_id=1, source_target_pairs={{0,4},{2,6},{4,8},{6,10},{8,12},{10,14},{12,0},{14,2},{1,5},{3,7},... | collective-permute-start | bytes 786440 | tf_op jit(solution)/shard_map/ppermute | solution.py:30
  55.2 1.7 %collective-permute-start.9 = (bf16[512,256]{1,0:T(8,128)(2,1)S(1)}, bf16[512,256]{1,0:T(8,128)(2,1)S(1)}, u32[]{:S(2)}, u32[]{:S(2)}) collective-permute-start(bf16[512,256]{1,0:T(8,128)(2,1)S(1)} %collective-permute-done.5.refs_2_), channel_id=1, source_target_pairs={{0,2},{2,0},{4,6},{6,4},{8,10},{10,8},{12,14},{14,12},{1,3},{3,1},... | collective-permute-start | bytes 786440 | tf_op jit(solution)/shard_map/ppermute | solution.py:35
  57.0 1.8 %collective-permute-start.13 = (bf16[512,256]{1,0:T(8,128)(2,1)S(1)}, bf16[512,256]{1,0:T(8,128)(2,1)S(1)}, u32[]{:S(2)}, u32[]{:S(2)}) collective-permute-start(bf16[512,256]{1,0:T(8,128)(2,1)S(1)} %collective-permute-done.12.refs_0_), channel_id=1, source_target_pairs={{0,1},{1,0},{2,3},{3,2},{4,5},{5,4},{6,7},{7,6},{8,9},{9,8},{10,11... | collective-permute-start | bytes 786440 | tf_op jit(solution)/shard_map/ppermute | solution.py:39
  58.8 5.1 %attend_own.1 = (f32[512,2048]{1,0:T(8,128)S(1)}, f32[512,1024]{1,0:T(8,128)S(1)}, f32[512,1024]{1,0:T(8,128)S(1)}) custom-call(s32[4]{0:T(128)S(1)} %copy-done.2, bf16[512,2048]{1,0:T(8,128)(2,1)S(1)} %copy-done, bf16[2,512,256]{2,1,0:T(8,128)(2,1)S(1)} %get-tuple-element.26.refs_0_), custom_call_target="tpu_custom_call" | custom-call | flops 2147483648 | bytes 4194304 | tf_op jit(solution)/shard_map/attend_own/pallas_call | solution.py:447
  64.7 11.0 %attend_mid.2 = (f32[512,2048]{1,0:T(8,128)S(1)}, f32[512,1024]{1,0:T(8,128)S(1)}, f32[512,1024]{1,0:T(8,128)S(1)}) custom-call(s32[4]{0:T(128)S(1)} %copy-done.2, bf16[512,2048]{1,0:T(8,128)(2,1)S(1)} %copy-done, bf16[512,256]{1,0:T(8,128)(2,1)S(1)} %collective-permute-done.12.refs_0_, bf16[512,256]{1,0:T(8,128)(2,1)S(1)} %collective-permute-done.13.refs_1_, ...), custom_call_target="tpu_custom_call" | custom-call | flops 4294967296 | bytes 4194304 | tf_op jit(solution)/shard_map/attend_mid/pallas_call | solution.py:447
  76.1 11.0 %attend_mid.3 = (f32[512,2048]{1,0:T(8,128)S(1)}, f32[512,1024]{1,0:T(8,128)S(1)}, f32[512,1024]{1,0:T(8,128)S(1)}) custom-call(s32[4]{0:T(128)S(1)} %copy-done.2, bf16[512,2048]{1,0:T(8,128)(2,1)S(1)} %copy-done, bf16[512,256]{1,0:T(8,128)(2,1)S(1)} %collective-permute-done.9.refs_0_, bf16[512,256]{1,0:T(8,128)(2,1)S(1)} %collective-permute-done.10.refs_1_, ...), custom_call_target="tpu_custom_call" | custom-call | flops 4294967296 | bytes 4194304 | tf_op jit(solution)/shard_map/attend_mid/pallas_call | solution.py:447
  87.2 4.6 %attend_end.1 = bf16[512,2048]{1,0:T(8,128)(2,1)} custom-call(s32[4]{0:T(128)S(1)} %copy-done.2, bf16[512,2048]{1,0:T(8,128)(2,1)S(1)} %copy-done, bf16[512,256]{1,0:T(8,128)(2,1)S(1)} %collective-permute-done.7.refs_0_, bf16[512,256]{1,0:T(8,128)(2,1)S(1)} %collective-permute-done.8.refs_1_, f32[512,2048]{1,0:T(8,128)S(1)} %get-tuple-element.33.refs_2_, ...), custom_call_target="tpu_custom_call" | custom-call | flops 2147483648 | bytes 4194304 | tf_op jit(solution)/shard_map/attend_end/pallas_call | solution.py:447
  (30 shorter events, 3.0 us)
Async XLA Ops:
  1.4 2.6 %collective-permute-start = (bf16[3,2048]{1,0:T(4,128)(2,1)S(1)}, bf16[3,2048]{1,0:T(4,128)(2,1)S(1)}, u32[]{:S(2)}, u32[]{:S(2)}) collective-permute-start(bf16[3,2048]{1,0:T(4,128)(2,1)S(1)} %slice.34), channel_id=1, source_target_pairs={{0,2},{2,4},{4,6},{6,8},{8,10},{10,12},{12,14},{14,0},{1,3},{3,5},... | collective-permute-start | bytes 36872 | tf_op jit(solution)/shard_map/ppermute | solution.py:30
  4.0 0.6 copy-start.4
  4.7 19.0 %copy-start.3 = (f32[16,512]{1,0:T(8,128)S(1)}, f32[16,512]{1,0:T(8,128)}, u32[]{:S(2)}) copy-start(f32[16,512]{1,0:T(8,128)} %param.22) | copy-start | bytes 98308
  18.5 2.9 %collective-permute-start.1 = (f32[2,2048]{1,0:T(2,128)}, f32[2,2048]{1,0:T(2,128)S(1)}, u32[]{:S(2)}, u32[]{:S(2)}) collective-permute-start(f32[2,2048]{1,0:T(2,128)} %get-tuple-element.22), channel_id=1, source_target_pairs={{0,2},{2,0},{4,6},{6,4},{8,10},{10,8},{12,14},{14,12},{1,3},{3,1},... | collective-permute-start | bytes 49160 | tf_op jit(solution)/shard_map/ppermute | solution.py:35
  22.1 2.6 %collective-permute-start.2 = (f32[2,2048]{1,0:T(2,128)S(1)}, f32[2,2048]{1,0:T(2,128)S(1)}, u32[]{:S(2)}, u32[]{:S(2)}) collective-permute-start(f32[2,2048]{1,0:T(2,128)S(1)} %pad_maximum_fusion), channel_id=1, source_target_pairs={{0,4},{2,6},{4,8},{6,10},{8,12},{10,14},{12,0},{14,2},{1,5},{3,7},... | collective-permute-start | bytes 49160 | tf_op jit(solution)/shard_map/ppermute | solution.py:30
  23.7 3.5 %collective-permute-start.3 = (f32[2,2048]{1,0:T(2,128)S(1)}, f32[2,2048]{1,0:T(2,128)S(1)}, u32[]{:S(2)}, u32[]{:S(2)}) collective-permute-start(f32[2,2048]{1,0:T(2,128)S(1)} %pad_maximum_fusion), channel_id=1, source_target_pairs={{0,8},{2,10},{4,12},{6,14},{8,0},{10,2},{12,4},{14,6},{1,9},{3,11}... | collective-permute-start | bytes 49160 | tf_op jit(solution)/shard_map/ppermute | solution.py:30
  27.8 31.0 %copy-start.2 = (s32[4]{0:T(128)S(1)}, s32[4]{0:T(128)}, u32[]{:S(2)}) copy-start(s32[4]{0:T(128)} %convert_reduce_fusion.starts_ref) | copy-start | bytes 52
  37.3 21.5 %copy-start = (bf16[512,2048]{1,0:T(8,128)(2,1)S(1)}, bf16[512,2048]{1,0:T(8,128)(2,1)}, u32[]{:S(2)}) copy-start(bf16[512,2048]{1,0:T(8,128)(2,1)} %q_ref.7) | copy-start | bytes 6291460
  37.3 6.7 %collective-permute-start.4 = (f32[512,512]{1,0:T(8,128)}, f32[512,512]{1,0:T(8,128)S(1)}, u32[]{:S(2)}, u32[]{:S(2)}) collective-permute-start(f32[512,512]{1,0:T(8,128)} %get-tuple-element.24.a_ref), channel_id=1, source_target_pairs={{0,1},{1,0},{2,3},{3,2},{4,5},{5,4},{6,7},{7,6},{8,9},{9,8},{10,11... | collective-permute-start | bytes 3145736 | tf_op jit(solution)/shard_map/ppermute | solution.py:39
  44.0 1.2 %copy-start.1 = (f32[512,512]{1,0:T(8,128)S(1)}, f32[512,512]{1,0:T(8,128)}, u32[]{:S(2)}) copy-start(f32[512,512]{1,0:T(8,128)} %get-tuple-element.24.a_ref) | copy-start | bytes 3145732
  45.4 7.5 %collective-permute-start.5 = (bf16[512,256]{1,0:T(8,128)(2,1)S(1)}, bf16[512,256]{1,0:T(8,128)(2,1)S(1)}, u32[]{:S(2)}, u32[]{:S(2)}) collective-permute-start(bf16[512,256]{1,0:T(8,128)(2,1)S(1)} %get-tuple-element.25), channel_id=1, source_target_pairs={{0,4},{2,6},{4,8},{6,10},{8,12},{10,14},{12,0},{14,2},{1,5},{3,7},... | collective-permute-start | bytes 786440 | tf_op jit(solution)/shard_map/ppermute | solution.py:30
  46.0 11.0 %collective-permute-start.12 = (bf16[512,256]{1,0:T(8,128)(2,1)S(1)}, bf16[512,256]{1,0:T(8,128)(2,1)S(1)}, u32[]{:S(2)}, u32[]{:S(2)}) collective-permute-start(bf16[512,256]{1,0:T(8,128)(2,1)S(1)} %get-tuple-element.25), channel_id=1, source_target_pairs={{0,2},{2,0},{4,6},{6,4},{8,10},{10,8},{12,14},{14,12},{1,3},{3,1},... | collective-permute-start | bytes 786440 | tf_op jit(solution)/shard_map/ppermute | solution.py:35
  53.0 10.9 %collective-permute-start.6 = (bf16[512,256]{1,0:T(8,128)(2,1)S(1)}, bf16[512,256]{1,0:T(8,128)(2,1)S(1)}, u32[]{:S(2)}, u32[]{:S(2)}) collective-permute-start(bf16[512,256]{1,0:T(8,128)(2,1)S(1)} %collective-permute-done.5.refs_2_), channel_id=1, source_target_pairs={{0,4},{2,6},{4,8},{6,10},{8,12},{10,14},{12,0},{14,2},{1,5},{3,7},... | collective-permute-start | bytes 786440 | tf_op jit(solution)/shard_map/ppermute | solution.py:30
  55.2 9.2 %collective-permute-start.9 = (bf16[512,256]{1,0:T(8,128)(2,1)S(1)}, bf16[512,256]{1,0:T(8,128)(2,1)S(1)}, u32[]{:S(2)}, u32[]{:S(2)}) collective-permute-start(bf16[512,256]{1,0:T(8,128)(2,1)S(1)} %collective-permute-done.5.refs_2_), channel_id=1, source_target_pairs={{0,2},{2,0},{4,6},{6,4},{8,10},{10,8},{12,14},{14,12},{1,3},{3,1},... | collective-permute-start | bytes 786440 | tf_op jit(solution)/shard_map/ppermute | solution.py:35
  57.0 7.7 %collective-permute-start.13 = (bf16[512,256]{1,0:T(8,128)(2,1)S(1)}, bf16[512,256]{1,0:T(8,128)(2,1)S(1)}, u32[]{:S(2)}, u32[]{:S(2)}) collective-permute-start(bf16[512,256]{1,0:T(8,128)(2,1)S(1)} %collective-permute-done.12.refs_0_), channel_id=1, source_target_pairs={{0,1},{1,0},{2,3},{3,2},{4,5},{5,4},{6,7},{7,6},{8,9},{9,8},{10,11... | collective-permute-start | bytes 786440 | tf_op jit(solution)/shard_map/ppermute | solution.py:39
  58.8 5.9 %collective-permute-start.14 = (bf16[512,256]{1,0:T(8,128)(2,1)S(1)}, bf16[512,256]{1,0:T(8,128)(2,1)S(1)}, u32[]{:S(2)}, u32[]{:S(2)}) collective-permute-start(bf16[512,256]{1,0:T(8,128)(2,1)S(1)} %collective-permute-done.5.refs_2_), channel_id=1, source_target_pairs={{0,1},{1,0},{2,3},{3,2},{4,5},{5,4},{6,7},{7,6},{8,9},{9,8},{10,11... | collective-permute-start | bytes 786440 | tf_op jit(solution)/shard_map/ppermute | solution.py:39
  63.9 12.2 %collective-permute-start.11 = (bf16[512,256]{1,0:T(8,128)(2,1)S(1)}, bf16[512,256]{1,0:T(8,128)(2,1)S(1)}, u32[]{:S(2)}, u32[]{:S(2)}) collective-permute-start(bf16[512,256]{1,0:T(8,128)(2,1)S(1)} %collective-permute-done.6.refs_2_), channel_id=1, source_target_pairs={{0,1},{1,0},{2,3},{3,2},{4,5},{5,4},{6,7},{7,6},{8,9},{9,8},{10,11... | collective-permute-start | bytes 786440 | tf_op jit(solution)/shard_map/ppermute | solution.py:39
  64.5 11.2 %collective-permute-start.7 = (bf16[512,256]{1,0:T(8,128)(2,1)S(1)}, bf16[512,256]{1,0:T(8,128)(2,1)S(1)}, u32[]{:S(2)}, u32[]{:S(2)}) collective-permute-start(bf16[512,256]{1,0:T(8,128)(2,1)S(1)} %collective-permute-done.6.refs_2_), channel_id=1, source_target_pairs={{0,2},{2,0},{4,6},{6,4},{8,10},{10,8},{12,14},{14,12},{1,3},{3,1},... | collective-permute-start | bytes 786440 | tf_op jit(solution)/shard_map/ppermute | solution.py:35
  64.5 11.7 %collective-permute-start.10 = (bf16[512,256]{1,0:T(8,128)(2,1)S(1)}, bf16[512,256]{1,0:T(8,128)(2,1)S(1)}, u32[]{:S(2)}, u32[]{:S(2)}) collective-permute-start(bf16[512,256]{1,0:T(8,128)(2,1)S(1)} %collective-permute-done.9.refs_0_), channel_id=1, source_target_pairs={{0,1},{1,0},{2,3},{3,2},{4,5},{5,4},{6,7},{7,6},{8,9},{9,8},{10,11... | collective-permute-start | bytes 786440 | tf_op jit(solution)/shard_map/ppermute | solution.py:39
  75.7 11.5 %collective-permute-start.8 = (bf16[512,256]{1,0:T(8,128)(2,1)S(1)}, bf16[512,256]{1,0:T(8,128)(2,1)S(1)}, u32[]{:S(2)}, u32[]{:S(2)}) collective-permute-start(bf16[512,256]{1,0:T(8,128)(2,1)S(1)} %collective-permute-done.7.refs_0_), channel_id=1, source_target_pairs={{0,1},{1,0},{2,3},{3,2},{4,5},{5,4},{6,7},{7,6},{8,9},{9,8},{10,11... | collective-permute-start | bytes 786440 | tf_op jit(solution)/shard_map/ppermute | solution.py:39
where the time goes:
time: 92.5 us; the launch traced here: 91.7 us
  Pallas kernels  55.2 us (60%)
  starting transfers between devices  16.2 us (18%)
  waiting for transfers between devices  13.6 us (15%)
  local copies, waits for them, and re-layouts  3.23 us (3%)
  other arithmetic  2.75 us (3%)
    pallas_call x4, Pallas kernels, attend_call(): pl.pallas_call(functools.partial(attend_kernel, own is not None, lags, pr...  31.7 us
    pallas_call x1, Pallas kernels, recur_call(): pl.pallas_call(recur_kernel, grid_spec=pltpu.PrefetchScalarGridSpec(num_s...  13.8 us
    pallas_call x1, Pallas kernels, mix_call(): pl.pallas_call(mix_kernel, grid=(channels // width,), in_specs=[pl.BlockS...  9.46 us
    ppermute x5, waiting for transfers between devices, ring(): return lax.ppermute(x, 'tm', [(i, (i + lag) % n) for i in range(n)])  9.39 us
    ppermute x6, starting transfers between devices, partner(): return lax.ppermute(x, 'mp', [(0, 1), (1, 0)])  7.18 us
    ppermute x4, starting transfers between devices, swap(): return lax.ppermute(x, 'tm', [(i, i ^ 1) for i in range(n)])  4.67 us
    ppermute x5, starting transfers between devices, ring(): return lax.ppermute(x, 'tm', [(i, (i + lag) % n) for i in range(n)])  4.39 us
    ppermute x6, waiting for transfers between devices, partner(): return lax.ppermute(x, 'mp', [(0, 1), (1, 0)])  2.51 us
  transfers between devices with their start and end apart: 15, of which 6 were waited for; matrix products, arithmetic and copies ran while one was open for 2% of the time, Pallas kernels for 30%

commit v1 on v0

--- a/solution.py
+++ b/solution.py
@@ -15,7 +15,7 @@
 SCALE_ROWS = 128
 DOCS = 4
 SEGS = 8
-MIX_GROUPS = 2
+MIX_GROUPS = 4
 GROUP = 2
 HIST = 4
 LOG2E = 1.4426950408889634
@@ -178,19 +178,38 @@
     tot_ref[1:2, :] = th
 
 
-def mix_kernel(h_ref, p_ref, ends_ref, in_ref, y_ref, panel_ref, scale_ref, mixed_ref, kv_ref, carry):
+def level_kernel(tot_ref, near_ref, level_ref):
+    odd = lax.axis_index("tm") % 2 == 1
+    tot, near = tot_ref[...], near_ref[...]
+    lower = jnp.where(odd, near, tot)
+    upper = jnp.where(odd, tot, near)
+    level_ref[0:1, :] = lower[0:1] * upper[0:1]
+    level_ref[1:2, :] = upper[0:1] * lower[1:2] + upper[1:2]
+
+
+def mix_kernel(levels, h_ref, p_ref, ends_ref, *refs):
+    near_ref, past, rest = refs[0], refs[1 : levels + 1], refs[levels + 1 :]
+    y_ref, panel_ref, scale_ref, mixed_ref, kv_ref, carry = rest
     rows, width = y_ref.shape
+    me = lax.axis_index("tm")
     seg_len = rows // SEGS
 
     @pl.when(pl.program_id(0) == 0)
     def _():
         kv_ref[...] = jnp.zeros_like(kv_ref)
 
-    c = in_ref[...]
+    c = jnp.zeros((1, width), F32)
+    for k in range(levels, 0, -1):
+        c = jnp.where(me >= 2 * k, past[k - 1][0:1, :] * c + past[k - 1][1:2, :], 0.0)
+    c = jnp.where(me % 2 == 1, near_ref[0:1, :] * c + near_ref[1:2, :], c)
     for s in range(SEGS):
         carry[s : s + 1, :] = c
         c = ends_ref[0, s : s + 1, :] * c + ends_ref[1, s : s + 1, :]
-    weight = dequantized(panel_ref[...], scale_ref[0])
+    groups = width // SCALE_ROWS
+    table = scale_ref[...]
+    index = lax.broadcasted_iota(jnp.int32, table.shape, 0) - pl.program_id(0) * groups
+    scale = [jnp.sum(jnp.where(index == g, table, 0.0), axis=0, keepdims=True) for g in range(groups)]
+    weight = dequantized(panel_ref[...], jnp.concatenate(scale, 0))
 
     def natural(ref, g, s):
         return jnp.concatenate(
@@ -385,32 +404,46 @@
             jax.ShapeDtypeStruct((2, SEGS, channels), F32),
             jax.ShapeDtypeStruct((2, channels), F32),
         ],
+        compiler_params=pltpu.CompilerParams(vmem_limit_bytes=20 << 20),
         name="recur",
     )(starts, x, halo, conv_weight, conv_bias, gate_panel, gate_scale, gate_bias, decay_rate)
 
 
-def mix_call(h, p, ends, incoming, y, kv_panel, kv_scale):
+def level_call(tot, near):
+    return pl.pallas_call(
+        level_kernel,
+        out_shape=jax.ShapeDtypeStruct(tot.shape, F32),
+        compiler_params=pltpu.CompilerParams(vmem_limit_bytes=1 << 20),
+        name="level",
+    )(tot, near)
+
+
+def mix_call(h, p, ends, near, past, y, kv_panel, kv_scale):
     rows, channels = y.shape
     width = MIX_GROUPS * SCALE_ROWS
     col = lambda b: (0, b)
     out = kv_panel.shape[1]
+    pair = pl.BlockSpec((2, width), col)
     return pl.pallas_call(
-        mix_kernel,
+        functools.partial(mix_kernel, len(past)),
         grid=(channels // width,),
         in_specs=[
             pl.BlockSpec((width // 128, rows, 128), lambda b: (b, 0, 0)),
             pl.BlockSpec((width // 128, rows, 128), lambda b: (b, 0, 0)),
             pl.BlockSpec((2, SEGS, width), lambda b: (0, 0, b)),
-            pl.BlockSpec((1, width), col),
+        ]
+        + [pair] * (1 + len(past))
+        + [
             pl.BlockSpec((rows, width), col),
             pl.BlockSpec((width, out), lambda b: (b, 0)),
-            pl.BlockSpec((1, MIX_GROUPS, out), lambda b: (b, 0, 0)),
+            pl.BlockSpec(kv_scale.shape, lambda b: (0, 0)),
         ],
         out_specs=[pl.BlockSpec((rows, width), col), pl.BlockSpec((rows, out), lambda b: (0, 0))],
         out_shape=[jax.ShapeDtypeStruct((rows, channels), BF16), jax.ShapeDtypeStruct((rows, out), F32)],
         scratch_shapes=[pltpu.VMEM((SEGS, width), F32)],
+        compiler_params=pltpu.CompilerParams(vmem_limit_bytes=20 << 20),
         name="mix",
-    )(h, p, ends, incoming, y, kv_panel, kv_scale.reshape(-1, MIX_GROUPS, out))
+    )(h, p, ends, near, *past, y, kv_panel, kv_scale)
 
 
 def sum_call(a, b):
@@ -487,35 +520,27 @@
 ):
     rows = branch_x.shape[0]
     seq = segment_ids.shape[0]
-    me = lax.axis_index("tm")
     halo = ring(branch_x[rows - CONV + 1 :], 1)
     starts = jnp.sum(
         (segment_ids[None, :] < jnp.arange(DOCS, dtype=jnp.int32)[:, None]).astype(jnp.int32), axis=1
     )
+    stay = lambda a: pltpu.with_memory_space_constraint(a, pltpu.HBM)
     h, p, ends, tot = recur_call(
         starts,
-        branch_x,
+        stay(branch_x),
         halo,
-        conv_weight,
-        conv_bias[None],
-        gate_panel,
-        gate_scale,
-        gate_bias,
-        decay_rate[None],
+        stay(conv_weight),
+        stay(conv_bias[None]),
+        stay(gate_panel),
+        stay(gate_scale),
+        stay(gate_bias),
+        stay(decay_rate[None]),
     )
-    odd = (me % 2) == 1
     near = swap(tot)
-    lower = jnp.where(odd, near, tot)
-    upper = jnp.where(odd, tot, near)
-    level = jnp.stack([lower[0] * upper[0], upper[0] * lower[1] + upper[1]])
+    level = level_call(tot, near)
     levels = -(-(seq // 2) // (2 * rows))
     past = [ring(level, 2 * k) for k in range(1, levels + 1)]
-    incoming = jnp.zeros_like(tot[1])
-    for k in range(levels, 0, -1):
-        got = past[k - 1]
-        incoming = jnp.where(me >= 2 * k, got[0] * incoming + got[1], 0.0)
-    incoming = jnp.where(odd, near[0] * incoming + near[1], incoming)
-    mixed, partial_kv = mix_call(h, p, ends, incoming[None], branch_y, kv_panel, kv_scale)
+    mixed, partial_kv = mix_call(h, p, ends, near, past, branch_y, kv_panel, kv_scale)
     own, half = sum_call(partial_kv, partner(partial_kv))
 
     levels = -(-WINDOW // rows) // 2

time: 92.5 us -> 81.5 us (0.88)
  Pallas kernels: 55.2 us -> 48.4 us
  local copies, waits for them, and re-layouts: 3.23 us -> 0.79 us
  other arithmetic: 2.75 us -> 0.87 us
    pallas_call x1 -> x2, Pallas kernels: 9.46 us -> 4.41 us  [the longest x1 4.4 us: mix_call(): pl.pallas_call(functools.partial(mix_kernel, len(past)), grid=(channels /...]
    unnamed x10 -> x8, local copies, waits for them, and re-layouts: 1.84 us -> 0.01 us
    pallas_call x1, Pallas kernels: 13.8 us -> 12 us  [recur_call(): pl.pallas_call(recur_kernel, grid_spec=pltpu.PrefetchScalarGridSpec(num_s...]
    select_n x2 -> x0, other arithmetic: 1.36 us -> none  [the longest x1 0.73 us: local(): lower = jnp.where(odd, near, tot)]
    ppermute x5, waiting for transfers between devices: 9.39 us -> 10.5 us  [ring(): return lax.ppermute(x, 'tm', [(i, (i + lag) % n) for i in range(n)])]
  transfers between devices with their start and end apart: 15 -> 15, of which waited for: 6 -> 6; matrix products, arithmetic and copies ran while one was open for 2% -> 1% of each run, Pallas kernels for 30% -> 33%
where the time goes in v1:
time: 81.5 us; the launch traced here: 81.3 us
  Pallas kernels  48.4 us (59%)
  starting transfers between devices  16.2 us (20%)
  waiting for transfers between devices  14.3 us (18%)
  other arithmetic  0.87 us (1%)
    pallas_call x4, Pallas kernels, attend_call(): pl.pallas_call(functools.partial(attend_kernel, own is not None, lags, pr...  31.8 us
    pallas_call x1, Pallas kernels, recur_call(): pl.pallas_call(recur_kernel, grid_spec=pltpu.PrefetchScalarGridSpec(num_s...  12 us
    ppermute x5, waiting for transfers between devices, ring(): return lax.ppermute(x, 'tm', [(i, (i + lag) % n) for i in range(n)])  10.5 us
    ppermute x6, starting transfers between devices, partner(): return lax.ppermute(x, 'mp', [(0, 1), (1, 0)])  7.15 us
    ppermute x4, starting transfers between devices, swap(): return lax.ppermute(x, 'tm', [(i, i ^ 1) for i in range(n)])  4.67 us
    pallas_call x1, Pallas kernels, mix_call(): pl.pallas_call(functools.partial(mix_kernel, len(past)), grid=(channels /...  4.4 us
    ppermute x5, starting transfers between devices, ring(): return lax.ppermute(x, 'tm', [(i, (i + lag) % n) for i in range(n)])  4.39 us
    ppermute x6, waiting for transfers between devices, partner(): return lax.ppermute(x, 'mp', [(0, 1), (1, 0)])  2.3 us
  transfers between devices with their start and end apart: 15, of which 6 were waited for; matrix products, arithmetic and copies ran while one was open for 1% of the time, Pallas kernels for 33%

profile of v1, /device:TPU:31, one launch (start us, length us, event | category | flops | bytes accessed | tf_op | source)
XLA Modules:
  0.0 81.3 jit_solution(16699809692936485740)
XLA Ops:
  0.6 0.8 slice.3
  1.5 0.9 %convert_reduce_fusion.starts_ref = s32[4]{0:T(128)S(1)} fusion(s32[4096]{0:T(1024)} %param.23), kind=kLoop, calls=%fused_computation | loop fusion | flops 49148 | bytes 16400 | tf_op jit(solution)/shard_map/reduce_sum | solution.py:524
  2.3 1.7 %collective-permute-done.halo_ref = bf16[3,2048]{1,0:T(4,128)(2,1)S(1)} collective-permute-done((bf16[3,2048]{1,0:T(4,128)(2,1)S(1)}, bf16[3,2048]{1,0:T(4,128)(2,1)S(1)}, u32[]{:S(2)}, u32[]{:S(2)}) %collective-permute-start) | collective-permute-done | bytes 12320 | tf_op jit(solution)/shard_map/ppermute | solution.py:30
  4.1 12.0 %recur.1 = (f32[16,512,128]{2,1,0:T(8,128)S(1)}, f32[16,512,128]{2,1,0:T(8,128)S(1)}, f32[2,8,2048]{2,1,0:T(8,128)S(1)}, f32[2,2048]{1,0:T(2,128)S(1)}) custom-call(s32[4]{0:T(128)S(1)} %convert_reduce_fusion.starts_ref, bf16[512,2048]{1,0:T(8,128)(2,1)} %x_ref.1, bf16[3,2048]{1,0:T(4,128)(2,1)S(1)} %collective-permute-done.halo_ref, f32[4,2048]{1,0:T(4,128)} %cw_ref.1, ...), custom_call_target="tpu_custom_call" | custom-call | tf_op jit(solution)/shard_map/recur/pallas_call | solution.py:373
  16.1 1.2 %collective-permute-start.1 = (f32[2,2048]{1,0:T(2,128)S(1)}, f32[2,2048]{1,0:T(2,128)S(1)}, u32[]{:S(2)}, u32[]{:S(2)}) collective-permute-start(f32[2,2048]{1,0:T(2,128)S(1)} %get-tuple-element.22.tot_ref), channel_id=1, source_target_pairs={{0,2},{2,0},{4,6},{6,4},{8,10},{10,8},{12,14},{14,12},{1,3},{3,1},... | collective-permute-start | bytes 49160 | tf_op jit(solution)/shard_map/ppermute | solution.py:35
  17.2 1.5 %collective-permute-done.1.near_ref.refs_0_ = f32[2,2048]{1,0:T(2,128)S(1)} collective-permute-done((f32[2,2048]{1,0:T(2,128)S(1)}, f32[2,2048]{1,0:T(2,128)S(1)}, u32[]{:S(2)}, u32[]{:S(2)}) %collective-permute-start.1) | collective-permute-done | bytes 16416 | tf_op jit(solution)/shard_map/ppermute | solution.py:35
  18.7 1.6 %collective-permute-start.2 = (f32[2,2048]{1,0:T(2,128)S(1)}, f32[2,2048]{1,0:T(2,128)S(1)}, u32[]{:S(2)}, u32[]{:S(2)}) collective-permute-start(f32[2,2048]{1,0:T(2,128)S(1)} %level.1), channel_id=1, source_target_pairs={{0,4},{2,6},{4,8},{6,10},{8,12},{10,14},{12,0},{14,2},{1,5},{3,7},... | collective-permute-start | bytes 49160 | tf_op jit(solution)/shard_map/ppermute | solution.py:30
  20.3 1.1 %collective-permute-done.2.refs_1_ = f32[2,2048]{1,0:T(2,128)S(1)} collective-permute-done((f32[2,2048]{1,0:T(2,128)S(1)}, f32[2,2048]{1,0:T(2,128)S(1)}, u32[]{:S(2)}, u32[]{:S(2)}) %collective-permute-start.2) | collective-permute-done | bytes 16416 | tf_op jit(solution)/shard_map/ppermute | solution.py:30
  21.4 2.4 %collective-permute-done.3.refs_2_ = f32[2,2048]{1,0:T(2,128)S(1)} collective-permute-done((f32[2,2048]{1,0:T(2,128)S(1)}, f32[2,2048]{1,0:T(2,128)S(1)}, u32[]{:S(2)}, u32[]{:S(2)}) %collective-permute-start.3) | collective-permute-done | bytes 16416 | tf_op jit(solution)/shard_map/ppermute | solution.py:30
  23.8 4.4 %mix.1 = (bf16[512,2048]{1,0:T(8,128)(2,1)}, f32[512,512]{1,0:T(8,128)S(1)}) custom-call(f32[16,512,128]{2,1,0:T(8,128)S(1)} %get-tuple-element.19.h_ref, f32[16,512,128]{2,1,0:T(8,128)S(1)} %get-tuple-element.20.p_ref, f32[2,8,2048]{2,1,0:T(8,128)S(1)} %get-tuple-element.21.ends_ref, f32[2,2048]{1,0:T(2,128)S(1)} %collective-permute-done.1.near_ref.refs_0_, ...), custom_call_target="tpu_custom_call" | custom-call | tf_op jit(solution)/shard_map/mix/pallas_call | solution.py:427
  28.2 4.2 %collective-permute-start.4 = (f32[512,512]{1,0:T(8,128)S(1)}, f32[512,512]{1,0:T(8,128)S(1)}, u32[]{:S(2)}, u32[]{:S(2)}) collective-permute-start(f32[512,512]{1,0:T(8,128)S(1)} %get-tuple-element.24.a_ref), channel_id=1, source_target_pairs={{0,1},{1,0},{2,3},{3,2},{4,5},{5,4},{6,7},{7,6},{8,9},{9,8},{10,11... | collective-permute-start | bytes 3145736 | tf_op jit(solution)/shard_map/ppermute | solution.py:39
  32.4 2.3 %collective-permute-done.4.b_ref = f32[512,512]{1,0:T(8,128)S(1)} collective-permute-done((f32[512,512]{1,0:T(8,128)S(1)}, f32[512,512]{1,0:T(8,128)S(1)}, u32[]{:S(2)}, u32[]{:S(2)}) %collective-permute-start.4) | collective-permute-done | bytes 1048608 | tf_op jit(solution)/shard_map/ppermute | solution.py:39
  34.9 0.5 collective-permute-start.5
  35.4 1.7 %collective-permute-start.12 = (bf16[512,256]{1,0:T(8,128)(2,1)S(1)}, bf16[512,256]{1,0:T(8,128)(2,1)S(1)}, u32[]{:S(2)}, u32[]{:S(2)}) collective-permute-start(bf16[512,256]{1,0:T(8,128)(2,1)S(1)} %get-tuple-element.25), channel_id=1, source_target_pairs={{0,2},{2,0},{4,6},{6,4},{8,10},{10,8},{12,14},{14,12},{1,3},{3,1},... | collective-permute-start | bytes 786440 | tf_op jit(solution)/shard_map/ppermute | solution.py:35
  37.2 5.3 %collective-permute-done.5.refs_2_ = bf16[512,256]{1,0:T(8,128)(2,1)S(1)} collective-permute-done((bf16[512,256]{1,0:T(8,128)(2,1)S(1)}, bf16[512,256]{1,0:T(8,128)(2,1)S(1)}, u32[]{:S(2)}, u32[]{:S(2)}) %collective-permute-start.5) | collective-permute-done | bytes 262176 | tf_op jit(solution)/shard_map/ppermute | solution.py:30
  42.5 2.3 %collective-permute-start.6 = (bf16[512,256]{1,0:T(8,128)(2,1)S(1)}, bf16[512,256]{1,0:T(8,128)(2,1)S(1)}, u32[]{:S(2)}, u32[]{:S(2)}) collective-permute-start(bf16[512,256]{1,0:T(8,128)(2,1)S(1)} %collective-permute-done.5.refs_2_), channel_id=1, source_target_pairs={{0,4},{2,6},{4,8},{6,10},{8,12},{10,14},{12,0},{14,2},{1,5},{3,7},... | collective-permute-start | bytes 786440 | tf_op jit(solution)/shard_map/ppermute | solution.py:30
  44.7 1.7 %collective-permute-start.9 = (bf16[512,256]{1,0:T(8,128)(2,1)S(1)}, bf16[512,256]{1,0:T(8,128)(2,1)S(1)}, u32[]{:S(2)}, u32[]{:S(2)}) collective-permute-start(bf16[512,256]{1,0:T(8,128)(2,1)S(1)} %collective-permute-done.5.refs_2_), channel_id=1, source_target_pairs={{0,2},{2,0},{4,6},{6,4},{8,10},{10,8},{12,14},{14,12},{1,3},{3,1},... | collective-permute-start | bytes 786440 | tf_op jit(solution)/shard_map/ppermute | solution.py:35
  46.5 1.8 %collective-permute-start.13 = (bf16[512,256]{1,0:T(8,128)(2,1)S(1)}, bf16[512,256]{1,0:T(8,128)(2,1)S(1)}, u32[]{:S(2)}, u32[]{:S(2)}) collective-permute-start(bf16[512,256]{1,0:T(8,128)(2,1)S(1)} %collective-permute-done.12.refs_0_), channel_id=1, source_target_pairs={{0,1},{1,0},{2,3},{3,2},{4,5},{5,4},{6,7},{7,6},{8,9},{9,8},{10,11... | collective-permute-start | bytes 786440 | tf_op jit(solution)/shard_map/ppermute | solution.py:39
  48.3 5.1 %attend_own.1 = (f32[512,2048]{1,0:T(8,128)S(1)}, f32[512,1024]{1,0:T(8,128)S(1)}, f32[512,1024]{1,0:T(8,128)S(1)}) custom-call(s32[4]{0:T(128)S(1)} %convert_reduce_fusion.starts_ref, bf16[512,2048]{1,0:T(8,128)(2,1)S(1)} %copy-done.2, bf16[2,512,256]{2,1,0:T(8,128)(2,1)S(1)} %get-tuple-element.26.refs_0_), custom_call_target="tpu_custom_call" | custom-call | flops 2147483648 | bytes 4194304 | tf_op jit(solution)/shard_map/attend_own/pallas_call | solution.py:480
  53.4 0.6 collective-permute-start.11
  54.1 11.1 %attend_mid.2 = (f32[512,2048]{1,0:T(8,128)S(1)}, f32[512,1024]{1,0:T(8,128)S(1)}, f32[512,1024]{1,0:T(8,128)S(1)}) custom-call(s32[4]{0:T(128)S(1)} %convert_reduce_fusion.starts_ref, bf16[512,2048]{1,0:T(8,128)(2,1)S(1)} %copy-done.2, bf16[512,256]{1,0:T(8,128)(2,1)S(1)} %collective-permute-done.12.refs_0_, ...), custom_call_target="tpu_custom_call" | custom-call | flops 4294967296 | bytes 4194304 | tf_op jit(solution)/shard_map/attend_mid/pallas_call | solution.py:480
  65.2 0.4 collective-permute-start.8
  65.6 11.1 %attend_mid.3 = (f32[512,2048]{1,0:T(8,128)S(1)}, f32[512,1024]{1,0:T(8,128)S(1)}, f32[512,1024]{1,0:T(8,128)S(1)}) custom-call(s32[4]{0:T(128)S(1)} %convert_reduce_fusion.starts_ref, bf16[512,2048]{1,0:T(8,128)(2,1)S(1)} %copy-done.2, bf16[512,256]{1,0:T(8,128)(2,1)S(1)} %collective-permute-done.9.refs_0_, ...), custom_call_target="tpu_custom_call" | custom-call | flops 4294967296 | bytes 4194304 | tf_op jit(solution)/shard_map/attend_mid/pallas_call | solution.py:480
  76.7 4.6 %attend_end.1 = bf16[512,2048]{1,0:T(8,128)(2,1)} custom-call(s32[4]{0:T(128)S(1)} %convert_reduce_fusion.starts_ref, bf16[512,2048]{1,0:T(8,128)(2,1)S(1)} %copy-done.2, bf16[512,256]{1,0:T(8,128)(2,1)S(1)} %collective-permute-done.7.refs_0_, bf16[512,256]{1,0:T(8,128)(2,1)S(1)} %collective-permute-done.8.refs_1_, ...), custom_call_target="tpu_custom_call" | custom-call | flops 2147483648 | bytes 4194304 | tf_op jit(solution)/shard_map/attend_end/pallas_call | solution.py:480
  (24 shorter events, 0.5 us)
Async XLA Ops:
  1.4 2.6 %collective-permute-start = (bf16[3,2048]{1,0:T(4,128)(2,1)S(1)}, bf16[3,2048]{1,0:T(4,128)(2,1)S(1)}, u32[]{:S(2)}, u32[]{:S(2)}) collective-permute-start(bf16[3,2048]{1,0:T(4,128)(2,1)S(1)} %slice.3), channel_id=1, source_target_pairs={{0,2},{2,4},{4,6},{6,8},{8,10},{10,12},{12,14},{14,0},{1,3},{3,5},... | collective-permute-start | bytes 36872 | tf_op jit(solution)/shard_map/ppermute | solution.py:30
  4.0 19.8 %copy-start = (bf16[512,2048]{1,0:T(8,128)(2,1)S(1)}, bf16[512,2048]{1,0:T(8,128)(2,1)}, u32[]{:S(2)}) copy-start(bf16[512,2048]{1,0:T(8,128)(2,1)} %refs_3_.1) | copy-start | bytes 6291460
  4.0 19.8 %copy-start.1 = (bf16[2048,512]{1,0:T(8,128)(2,1)S(1)}, bf16[2048,512]{1,0:T(8,128)(2,1)}, u32[]{:S(2)}) copy-start(bf16[2048,512]{1,0:T(8,128)(2,1)} %refs_4_.1) | copy-start | bytes 6291460
  4.1 19.8 %copy-start.3 = (f32[16,512]{1,0:T(8,128)S(1)}, f32[16,512]{1,0:T(8,128)}, u32[]{:S(2)}) copy-start(f32[16,512]{1,0:T(8,128)} %refs_5_.1) | copy-start | bytes 98308
  16.1 2.7 %collective-permute-start.1 = (f32[2,2048]{1,0:T(2,128)S(1)}, f32[2,2048]{1,0:T(2,128)S(1)}, u32[]{:S(2)}, u32[]{:S(2)}) collective-permute-start(f32[2,2048]{1,0:T(2,128)S(1)} %get-tuple-element.22.tot_ref), channel_id=1, source_target_pairs={{0,2},{2,0},{4,6},{6,4},{8,10},{10,8},{12,14},{14,12},{1,3},{3,1},... | collective-permute-start | bytes 49160 | tf_op jit(solution)/shard_map/ppermute | solution.py:35
  18.7 2.6 %collective-permute-start.2 = (f32[2,2048]{1,0:T(2,128)S(1)}, f32[2,2048]{1,0:T(2,128)S(1)}, u32[]{:S(2)}, u32[]{:S(2)}) collective-permute-start(f32[2,2048]{1,0:T(2,128)S(1)} %level.1), channel_id=1, source_target_pairs={{0,4},{2,6},{4,8},{6,10},{8,12},{10,14},{12,0},{14,2},{1,5},{3,7},... | collective-permute-start | bytes 49160 | tf_op jit(solution)/shard_map/ppermute | solution.py:30
  20.3 3.5 %collective-permute-start.3 = (f32[2,2048]{1,0:T(2,128)S(1)}, f32[2,2048]{1,0:T(2,128)S(1)}, u32[]{:S(2)}, u32[]{:S(2)}) collective-permute-start(f32[2,2048]{1,0:T(2,128)S(1)} %level.1), channel_id=1, source_target_pairs={{0,8},{2,10},{4,12},{6,14},{8,0},{10,2},{12,4},{14,6},{1,9},{3,11}... | collective-permute-start | bytes 49160 | tf_op jit(solution)/shard_map/ppermute | solution.py:30
  28.2 20.0 %copy-start.2 = (bf16[512,2048]{1,0:T(8,128)(2,1)S(1)}, bf16[512,2048]{1,0:T(8,128)(2,1)}, u32[]{:S(2)}) copy-start(bf16[512,2048]{1,0:T(8,128)(2,1)} %q_ref.7) | copy-start | bytes 6291460
  28.2 6.5 %collective-permute-start.4 = (f32[512,512]{1,0:T(8,128)S(1)}, f32[512,512]{1,0:T(8,128)S(1)}, u32[]{:S(2)}, u32[]{:S(2)}) collective-permute-start(f32[512,512]{1,0:T(8,128)S(1)} %get-tuple-element.24.a_ref), channel_id=1, source_target_pairs={{0,1},{1,0},{2,3},{3,2},{4,5},{5,4},{6,7},{7,6},{8,9},{9,8},{10,11... | collective-permute-start | bytes 3145736 | tf_op jit(solution)/shard_map/ppermute | solution.py:39
  34.9 7.5 %collective-permute-start.5 = (bf16[512,256]{1,0:T(8,128)(2,1)S(1)}, bf16[512,256]{1,0:T(8,128)(2,1)S(1)}, u32[]{:S(2)}, u32[]{:S(2)}) collective-permute-start(bf16[512,256]{1,0:T(8,128)(2,1)S(1)} %get-tuple-element.25), channel_id=1, source_target_pairs={{0,4},{2,6},{4,8},{6,10},{8,12},{10,14},{12,0},{14,2},{1,5},{3,7},... | collective-permute-start | bytes 786440 | tf_op jit(solution)/shard_map/ppermute | solution.py:30
  35.4 11.0 %collective-permute-start.12 = (bf16[512,256]{1,0:T(8,128)(2,1)S(1)}, bf16[512,256]{1,0:T(8,128)(2,1)S(1)}, u32[]{:S(2)}, u32[]{:S(2)}) collective-permute-start(bf16[512,256]{1,0:T(8,128)(2,1)S(1)} %get-tuple-element.25), channel_id=1, source_target_pairs={{0,2},{2,0},{4,6},{6,4},{8,10},{10,8},{12,14},{14,12},{1,3},{3,1},... | collective-permute-start | bytes 786440 | tf_op jit(solution)/shard_map/ppermute | solution.py:35
  42.5 10.9 %collective-permute-start.6 = (bf16[512,256]{1,0:T(8,128)(2,1)S(1)}, bf16[512,256]{1,0:T(8,128)(2,1)S(1)}, u32[]{:S(2)}, u32[]{:S(2)}) collective-permute-start(bf16[512,256]{1,0:T(8,128)(2,1)S(1)} %collective-permute-done.5.refs_2_), channel_id=1, source_target_pairs={{0,4},{2,6},{4,8},{6,10},{8,12},{10,14},{12,0},{14,2},{1,5},{3,7},... | collective-permute-start | bytes 786440 | tf_op jit(solution)/shard_map/ppermute | solution.py:30
  44.7 9.2 %collective-permute-start.9 = (bf16[512,256]{1,0:T(8,128)(2,1)S(1)}, bf16[512,256]{1,0:T(8,128)(2,1)S(1)}, u32[]{:S(2)}, u32[]{:S(2)}) collective-permute-start(bf16[512,256]{1,0:T(8,128)(2,1)S(1)} %collective-permute-done.5.refs_2_), channel_id=1, source_target_pairs={{0,2},{2,0},{4,6},{6,4},{8,10},{10,8},{12,14},{14,12},{1,3},{3,1},... | collective-permute-start | bytes 786440 | tf_op jit(solution)/shard_map/ppermute | solution.py:35
  46.5 7.7 %collective-permute-start.13 = (bf16[512,256]{1,0:T(8,128)(2,1)S(1)}, bf16[512,256]{1,0:T(8,128)(2,1)S(1)}, u32[]{:S(2)}, u32[]{:S(2)}) collective-permute-start(bf16[512,256]{1,0:T(8,128)(2,1)S(1)} %collective-permute-done.12.refs_0_), channel_id=1, source_target_pairs={{0,1},{1,0},{2,3},{3,2},{4,5},{5,4},{6,7},{7,6},{8,9},{9,8},{10,11... | collective-permute-start | bytes 786440 | tf_op jit(solution)/shard_map/ppermute | solution.py:39
  48.2 5.9 %collective-permute-start.14 = (bf16[512,256]{1,0:T(8,128)(2,1)S(1)}, bf16[512,256]{1,0:T(8,128)(2,1)S(1)}, u32[]{:S(2)}, u32[]{:S(2)}) collective-permute-start(bf16[512,256]{1,0:T(8,128)(2,1)S(1)} %collective-permute-done.5.refs_2_), channel_id=1, source_target_pairs={{0,1},{1,0},{2,3},{3,2},{4,5},{5,4},{6,7},{7,6},{8,9},{9,8},{10,11... | collective-permute-start | bytes 786440 | tf_op jit(solution)/shard_map/ppermute | solution.py:39
  53.4 12.2 %collective-permute-start.11 = (bf16[512,256]{1,0:T(8,128)(2,1)S(1)}, bf16[512,256]{1,0:T(8,128)(2,1)S(1)}, u32[]{:S(2)}, u32[]{:S(2)}) collective-permute-start(bf16[512,256]{1,0:T(8,128)(2,1)S(1)} %collective-permute-done.6.refs_2_), channel_id=1, source_target_pairs={{0,1},{1,0},{2,3},{3,2},{4,5},{5,4},{6,7},{7,6},{8,9},{9,8},{10,11... | collective-permute-start | bytes 786440 | tf_op jit(solution)/shard_map/ppermute | solution.py:39
  54.0 11.2 %collective-permute-start.7 = (bf16[512,256]{1,0:T(8,128)(2,1)S(1)}, bf16[512,256]{1,0:T(8,128)(2,1)S(1)}, u32[]{:S(2)}, u32[]{:S(2)}) collective-permute-start(bf16[512,256]{1,0:T(8,128)(2,1)S(1)} %collective-permute-done.6.refs_2_), channel_id=1, source_target_pairs={{0,2},{2,0},{4,6},{6,4},{8,10},{10,8},{12,14},{14,12},{1,3},{3,1},... | collective-permute-start | bytes 786440 | tf_op jit(solution)/shard_map/ppermute | solution.py:35
  54.0 11.7 %collective-permute-start.10 = (bf16[512,256]{1,0:T(8,128)(2,1)S(1)}, bf16[512,256]{1,0:T(8,128)(2,1)S(1)}, u32[]{:S(2)}, u32[]{:S(2)}) collective-permute-start(bf16[512,256]{1,0:T(8,128)(2,1)S(1)} %collective-permute-done.9.refs_0_), channel_id=1, source_target_pairs={{0,1},{1,0},{2,3},{3,2},{4,5},{5,4},{6,7},{7,6},{8,9},{9,8},{10,11... | collective-permute-start | bytes 786440 | tf_op jit(solution)/shard_map/ppermute | solution.py:39
  65.2 11.5 %collective-permute-start.8 = (bf16[512,256]{1,0:T(8,128)(2,1)S(1)}, bf16[512,256]{1,0:T(8,128)(2,1)S(1)}, u32[]{:S(2)}, u32[]{:S(2)}) collective-permute-start(bf16[512,256]{1,0:T(8,128)(2,1)S(1)} %collective-permute-done.7.refs_0_), channel_id=1, source_target_pairs={{0,1},{1,0},{2,3},{3,2},{4,5},{5,4},{6,7},{7,6},{8,9},{9,8},{10,11... | collective-permute-start | bytes 786440 | tf_op jit(solution)/shard_map/ppermute | solution.py:39

commit v2 on v1

--- a/solution.py
+++ b/solution.py
@@ -239,15 +239,17 @@
     half_ref[...] = own_ref[core]
 
 
-def attend_kernel(own, lags, has_prev, final, starts_ref, q_ref, *refs):
+def attend_kernel(own, lags, final, heads, starts_ref, q_ref, *refs):
     refs = list(refs)
     take = lambda n: [refs.pop(0) for _ in range(n)]
     own_ref = take(1)[0] if own else None
     pairs = [take(2) for _ in lags]
-    prev_acc, prev_m, prev_l = take(3) if has_prev else (None, None, None)
-    out = take(1) if final else take(3)
+    prev = None if own else take(3)
+    out = take(1)[0] if final else None
+    acc, m_ref, l_ref = (None, None, None) if final else take(3)
     low, score, top = take(3)
-    acc, m_ref, l_ref = take(3) if final else out
+    if final:
+        acc, m_ref, l_ref, stage, sems = take(5)
     rows = q_ref.shape[0]
     half = rows // 2
     me = lax.axis_index("tm")
@@ -262,12 +264,12 @@
             d0 = jnp.maximum(d0, jnp.where(starts_ref[d] <= t, starts_ref[d], 0))
         return d0
 
-    @pl.when(pl.program_id(0) == 0)
-    def _():
-        low[...] = lowest(first + lax.broadcasted_iota(jnp.int32, (rows, 128), 0))
-
     lo_first = lowest(first)
     lo_last = lowest(first + rows - 1)
+    tiles = [(None, first)] if own else []
+    for k, (even_part, odd_part) in enumerate(lags):
+        tiles.append((pairs[k], first - (even_part + odd_part * turn) * rows))
+    live = [None if pair is None else (start >= 0) & (start < first) & (start + rows > lo_first) for pair, start in tiles]
 
     def keys_of(pair, t):
         return own_ref[t, :HD, :] if pair is None else pair[t][:HD, :]
@@ -275,14 +277,18 @@
     def values_of(pair, t):
         return own_ref[t, HD:, :] if pair is None else pair[t][HD:, :]
 
-    def score_pass(j, pair, start, masked):
+    def lanes(g, h, n):
+        return pl.ds(pl.multiple_of((g * GROUP + h) * n, n), n)
+
+    def kept(g, h, n):
+        return slice(h * n, (h + 1) * n) if final else lanes(g, h, n)
+
+    def score_pass(g, j, pair, start, masked):
         for h in range(GROUP):
             for t in range(2):
                 r0 = half * t if pair is None else 0
                 at = slice(r0, rows)
-                s = jnp.dot(
-                    q_ref[at, h * HD : (h + 1) * HD], keys_of(pair, t), preferred_element_type=F32
-                )
+                s = jnp.dot(q_ref[at, lanes(g, h, HD)], keys_of(pair, t), preferred_element_type=F32)
                 peak = top[h, at, :]
                 for c in range(half // 128):
                     part = s[:, c * 128 : (c + 1) * 128] * scale
@@ -297,13 +303,13 @@
                     peak = jnp.maximum(peak, part)
                 top[h, at, :] = peak
 
-    def value_pass(j, pair):
+    def value_pass(g, j, pair):
         for h in range(GROUP):
             spans = [(0, half, 1), (half, rows, 2)] if pair is None else [(0, rows, 2)]
             for r0, r1, n in spans:
                 at = slice(r0, r1)
-                m = m_ref[at, h * 128 : (h + 1) * 128]
-                total = l_ref[at, h * 128 : (h + 1) * 128]
+                m = m_ref[at, kept(g, h, 128)]
+                total = l_ref[at, kept(g, h, 128)]
                 ps, vs = [], []
                 for t in range(n):
                     for c in range(half // 128):
@@ -311,59 +317,98 @@
                         total = total + p
                         ps.append(p.astype(BF16))
                     vs.append(values_of(pair, t))
-                l_ref[at, h * 128 : (h + 1) * 128] = total
-                acc[at, h * HD : (h + 1) * HD] += jnp.dot(
+                l_ref[at, kept(g, h, 128)] = total
+                acc[at, kept(g, h, HD)] += jnp.dot(
                     jnp.concatenate(ps, 1), jnp.concatenate(vs, 0), preferred_element_type=F32
                 )
 
-    tiles = [(None, first)] if own else []
-    for k, (even_part, odd_part) in enumerate(lags):
-        tiles.append((pairs[k], first - (even_part + odd_part * turn) * rows))
-    live = [True if pair is None else (start >= 0) & (start < first) & (start + rows > lo_first) for pair, start in tiles]
-
-    top[...] = jnp.full(top.shape, -1e30, F32)
-    for j, (pair, start) in enumerate(tiles):
-        if pair is None:
-            score_pass(j, pair, start, True)
-            continue
-
-        @pl.when(live[j] & (start >= lo_last))
-        def _(j=j, pair=pair, start=start):
-            score_pass(j, pair, start, False)
-
-        @pl.when(live[j] & (start < lo_last))
-        def _(j=j, pair=pair, start=start):
-            score_pass(j, pair, start, True)
-
-    for h in range(GROUP):
-        lanes = slice(h * 128, (h + 1) * 128)
-        wide = slice(h * HD, (h + 1) * HD)
-        m = jnp.broadcast_to(jnp.max(top[h], axis=1, keepdims=True), (rows, 128))
-        if has_prev:
-            m0 = prev_m[:, lanes]
-            m = jnp.maximum(m, m0)
-            fade = jnp.exp2(m0 - m)
-            l_ref[:, lanes] = prev_l[:, lanes] * fade
-            acc[:, wide] = prev_acc[:, wide] * jnp.concatenate([fade] * (HD // 128), 1)
-        else:
-            l_ref[:, lanes] = jnp.zeros((rows, 128), F32)
-            acc[:, wide] = jnp.zeros((rows, HD), F32)
-        m_ref[:, lanes] = m
-    for j, (pair, start) in enumerate(tiles):
-        if pair is None:
-            value_pass(j, pair)
-            continue
-
-        @pl.when(live[j])
-        def _(j=j, pair=pair):
-            value_pass(j, pair)
-
-    if final:
+    def spread(x):
+        return jnp.concatenate([x] * (HD // 128), 1)
+
+    def update(g):
+        top[...] = jnp.full(top.shape, -1e30, F32)
+        for j, (pair, start) in enumerate(tiles):
+            if pair is None:
+                score_pass(g, j, pair, start, True)
+                continue
+
+            @pl.when(live[j] & (start >= lo_last))
+            def _(j=j, pair=pair, start=start):
+                score_pass(g, j, pair, start, False)
+
+            @pl.when(live[j] & (start < lo_last))
+            def _(j=j, pair=pair, start=start):
+                score_pass(g, j, pair, start, True)
+
         for h in range(GROUP):
-            total = jnp.sum(l_ref[:, h * 128 : (h + 1) * 128], axis=1, keepdims=True)
+            m = jnp.broadcast_to(jnp.max(top[h], axis=1, keepdims=True), (rows, 128))
+            if own:
+                l_ref[:, kept(g, h, 128)] = jnp.zeros((rows, 128), F32)
+                acc[:, kept(g, h, HD)] = jnp.zeros((rows, HD), F32)
+            else:
+                m0 = prev[1][:, lanes(g, h, 128)]
+                m = jnp.maximum(m, m0)
+                fade = jnp.exp2(m0 - m)
+                l_ref[:, kept(g, h, 128)] = prev[2][:, lanes(g, h, 128)] * fade
+                acc[:, kept(g, h, HD)] = prev[0][:, lanes(g, h, HD)] * spread(fade)
+            m_ref[:, kept(g, h, 128)] = m
+        for j, (pair, start) in enumerate(tiles):
+            if pair is None:
+                value_pass(g, j, pair)
+                continue
+
+            @pl.when(live[j])
+            def _(j=j, pair=pair):
+                value_pass(g, j, pair)
+
+    any_live = None if own else functools.reduce(jnp.logical_or, live)
+
+    def loop(fn):
+        def body(g, z):
+            fn(g)
+            return z
+
+        lax.fori_loop(0, heads // GROUP, body, 0)
+
+    def start_up():
+        low[...] = lowest(first + lax.broadcasted_iota(jnp.int32, (rows, 128), 0))
+
+    if own:
+        start_up()
+        loop(update)
+        return
+    if not final:
+
+        @pl.when(any_live)
+        def _():
+            start_up()
+            loop(update)
+
+        return
+
+    pl.when(any_live)(start_up)
+
+    def outgoing(g):
+        wide = pl.ds(pl.multiple_of(g * GROUP * HD, GROUP * HD), GROUP * HD)
+        return pltpu.make_async_copy(stage.at[g], out.at[:, wide], sems.at[g])
+
+    def finish(g):
+        pl.when(any_live)(lambda: update(g))
+
+        @pl.when(jnp.logical_not(any_live))
+        def _():
+            for h in range(GROUP):
+                l_ref[:, kept(g, h, 128)] = prev[2][:, lanes(g, h, 128)]
+                acc[:, kept(g, h, HD)] = prev[0][:, lanes(g, h, HD)]
+
+        for h in range(GROUP):
+            total = jnp.sum(l_ref[:, kept(g, h, 128)], axis=1, keepdims=True)
             share = jnp.broadcast_to(1.0 / total, (rows, 128))
-            wide = slice(h * HD, (h + 1) * HD)
-            out[0][:, wide] = (acc[:, wide] * jnp.concatenate([share] * (HD // 128), 1)).astype(BF16)
+            stage[g, :, h * HD : (h + 1) * HD] = (acc[:, kept(g, h, HD)] * spread(share)).astype(BF16)
+        outgoing(g).start()
+
+    loop(finish)
+    loop(lambda g: outgoing(g).wait())
 
 
 def recur_call(starts, x, halo, conv_weight, conv_bias, gate_panel, gate_scale, gate_bias, decay_rate):
@@ -463,37 +508,34 @@
 def attend_call(starts, q, own, halves, lags, prev, final):
     rows, width = q.shape
     heads = width // HD
-    whole = lambda a: pl.BlockSpec(a.shape, lambda h, s: (0,) * a.ndim)
-    per_head = lambda h, s: (0, h)
     held = [] if own is None else [own]
     held += halves
-    carried = [pl.BlockSpec((rows, GROUP * n), per_head) for n in (HD, 128, 128)]
+    held += prev or []
     tiles = len(lags) + (own is not None)
+    vmem = pl.BlockSpec(memory_space=pltpu.VMEM)
+    scratch = [
+        pltpu.VMEM((rows, 128), jnp.int32),
+        pltpu.VMEM((tiles, GROUP, 2, rows, rows // 2), F32),
+        pltpu.VMEM((GROUP, rows, 128), F32),
+    ]
+    aliases = {}
     if final:
-        out_specs = pl.BlockSpec((rows, GROUP * HD), per_head)
+        out_specs = pl.BlockSpec(memory_space=pl.ANY)
         out_shape = jax.ShapeDtypeStruct((rows, width), BF16)
-        extra = [pltpu.VMEM((rows, GROUP * n), F32) for n in (HD, 128, 128)]
+        scratch += [pltpu.VMEM((rows, GROUP * n), F32) for n in (HD, 128, 128)]
+        scratch += [pltpu.VMEM((heads // GROUP, rows, GROUP * HD), BF16), pltpu.SemaphoreType.DMA((heads // GROUP,))]
     else:
-        out_specs = carried
+        out_specs = [vmem] * 3
         out_shape = [jax.ShapeDtypeStruct((rows, heads * n), F32) for n in (HD, 128, 128)]
-        extra = []
+        if prev:
+            aliases = {2 + len(halves) + k: k for k in range(3)}
     return pl.pallas_call(
-        functools.partial(attend_kernel, own is not None, lags, prev is not None, final),
-        grid_spec=pltpu.PrefetchScalarGridSpec(
-            num_scalar_prefetch=1,
-            grid=(heads // GROUP,),
-            in_specs=[pl.BlockSpec((rows, GROUP * HD), per_head)]
-            + [whole(a) for a in held]
-            + (carried if prev is not None else []),
-            out_specs=out_specs,
-            scratch_shapes=[
-                pltpu.VMEM((rows, 128), jnp.int32),
-                pltpu.VMEM((tiles, GROUP, 2, rows, rows // 2), F32),
-                pltpu.VMEM((GROUP, rows, 128), F32),
-            ]
-            + extra,
-        ),
+        functools.partial(attend_kernel, own is not None, lags, final, heads),
+        in_specs=[pl.BlockSpec(memory_space=pltpu.SMEM), vmem] + [vmem] * len(held),
+        out_specs=out_specs,
+        scratch_shapes=scratch,
         out_shape=out_shape,
+        input_output_aliases=aliases,
         cost_estimate=pl.CostEstimate(
             flops=4 * tiles * rows * rows * width,
             bytes_accessed=4 * rows * width,
@@ -501,7 +543,7 @@
         ),
         compiler_params=pltpu.CompilerParams(vmem_limit_bytes=32 << 20),
         name="attend_own" if own is not None else "attend_end" if final else "attend_mid",
-    )(starts, q, *held, *(prev or []))
+    )(starts, q, *held)
 
 
 def local(

time: 81.5 us -> 82 us (level)
  transfers between devices with their start and end apart: 15 -> 15, of which waited for: 6 -> 6; matrix products, arithmetic and copies ran while one was open for 1% -> 1% of each run, Pallas kernels for 33% -> 36%
where the time goes in v2:
time: 82 us; the launch traced here: 81.7 us
  Pallas kernels  48.8 us (60%)
  starting transfers between devices  16.3 us (20%)
  waiting for transfers between devices  14.2 us (17%)
  other arithmetic  0.87 us (1%)
    pallas_call x4, Pallas kernels, attend_call(): pl.pallas_call(functools.partial(attend_kernel, own is not None, lags, fi...  32.2 us
    pallas_call x1, Pallas kernels, recur_call(): pl.pallas_call(recur_kernel, grid_spec=pltpu.PrefetchScalarGridSpec(num_s...  12 us
    ppermute x5, waiting for transfers between devices, ring(): return lax.ppermute(x, 'tm', [(i, (i + lag) % n) for i in range(n)])  10.5 us
    ppermute x6, starting transfers between devices, partner(): return lax.ppermute(x, 'mp', [(0, 1), (1, 0)])  7.11 us
    ppermute x4, starting transfers between devices, swap(): return lax.ppermute(x, 'tm', [(i, i ^ 1) for i in range(n)])  4.71 us
    ppermute x5, starting transfers between devices, ring(): return lax.ppermute(x, 'tm', [(i, (i + lag) % n) for i in range(n)])  4.43 us
    pallas_call x1, Pallas kernels, mix_call(): pl.pallas_call(functools.partial(mix_kernel, len(past)), grid=(channels /...  4.4 us
    ppermute x6, waiting for transfers between devices, partner(): return lax.ppermute(x, 'mp', [(0, 1), (1, 0)])  2.3 us
  transfers between devices with their start and end apart: 15, of which 6 were waited for; matrix products, arithmetic and copies ran while one was open for 1% of the time, Pallas kernels for 36%

profile of v2, /device:TPU:31, one launch (start us, length us, event | category | flops | bytes accessed | tf_op | source)
XLA Modules:
  0.0 81.7 jit_solution(14247292981336284848)
XLA Ops:
  0.6 0.8 slice.3
  1.5 0.9 %convert_reduce_fusion.starts_ref = s32[4]{0:T(128)S(1)} fusion(s32[4096]{0:T(1024)} %param.23), kind=kLoop, calls=%fused_computation | loop fusion | flops 49148 | bytes 16400 | tf_op jit(solution)/shard_map/reduce_sum | solution.py:566
  2.3 1.7 %collective-permute-done.halo_ref = bf16[3,2048]{1,0:T(4,128)(2,1)S(1)} collective-permute-done((bf16[3,2048]{1,0:T(4,128)(2,1)S(1)}, bf16[3,2048]{1,0:T(4,128)(2,1)S(1)}, u32[]{:S(2)}, u32[]{:S(2)}) %collective-permute-start) | collective-permute-done | bytes 12320 | tf_op jit(solution)/shard_map/ppermute | solution.py:30
  4.1 12.0 %recur.1 = (f32[16,512,128]{2,1,0:T(8,128)S(1)}, f32[16,512,128]{2,1,0:T(8,128)S(1)}, f32[2,8,2048]{2,1,0:T(8,128)S(1)}, f32[2,2048]{1,0:T(2,128)S(1)}) custom-call(s32[4]{0:T(128)S(1)} %convert_reduce_fusion.starts_ref, bf16[512,2048]{1,0:T(8,128)(2,1)} %x_ref.1, bf16[3,2048]{1,0:T(4,128)(2,1)S(1)} %collective-permute-done.halo_ref, f32[4,2048]{1,0:T(4,128)} %cw_ref.1, ...), custom_call_target="tpu_custom_call" | custom-call | tf_op jit(solution)/shard_map/recur/pallas_call | solution.py:418
  16.1 1.2 %collective-permute-start.1 = (f32[2,2048]{1,0:T(2,128)S(1)}, f32[2,2048]{1,0:T(2,128)S(1)}, u32[]{:S(2)}, u32[]{:S(2)}) collective-permute-start(f32[2,2048]{1,0:T(2,128)S(1)} %get-tuple-element.22.tot_ref), channel_id=1, source_target_pairs={{0,2},{2,0},{4,6},{6,4},{8,10},{10,8},{12,14},{14,12},{1,3},{3,1},... | collective-permute-start | bytes 49160 | tf_op jit(solution)/shard_map/ppermute | solution.py:35
  17.3 1.4 %collective-permute-done.1.near_ref.refs_0_ = f32[2,2048]{1,0:T(2,128)S(1)} collective-permute-done((f32[2,2048]{1,0:T(2,128)S(1)}, f32[2,2048]{1,0:T(2,128)S(1)}, u32[]{:S(2)}, u32[]{:S(2)}) %collective-permute-start.1) | collective-permute-done | bytes 16416 | tf_op jit(solution)/shard_map/ppermute | solution.py:35
  18.7 1.6 %collective-permute-start.2 = (f32[2,2048]{1,0:T(2,128)S(1)}, f32[2,2048]{1,0:T(2,128)S(1)}, u32[]{:S(2)}, u32[]{:S(2)}) collective-permute-start(f32[2,2048]{1,0:T(2,128)S(1)} %level.1), channel_id=1, source_target_pairs={{0,4},{2,6},{4,8},{6,10},{8,12},{10,14},{12,0},{14,2},{1,5},{3,7},... | collective-permute-start | bytes 49160 | tf_op jit(solution)/shard_map/ppermute | solution.py:30
  20.3 1.0 %collective-permute-done.2.refs_1_ = f32[2,2048]{1,0:T(2,128)S(1)} collective-permute-done((f32[2,2048]{1,0:T(2,128)S(1)}, f32[2,2048]{1,0:T(2,128)S(1)}, u32[]{:S(2)}, u32[]{:S(2)}) %collective-permute-start.2) | collective-permute-done | bytes 16416 | tf_op jit(solution)/shard_map/ppermute | solution.py:30
  21.4 2.5 %collective-permute-done.3.refs_2_ = f32[2,2048]{1,0:T(2,128)S(1)} collective-permute-done((f32[2,2048]{1,0:T(2,128)S(1)}, f32[2,2048]{1,0:T(2,128)S(1)}, u32[]{:S(2)}, u32[]{:S(2)}) %collective-permute-start.3) | collective-permute-done | bytes 16416 | tf_op jit(solution)/shard_map/ppermute | solution.py:30
  23.8 4.4 %mix.1 = (bf16[512,2048]{1,0:T(8,128)(2,1)}, f32[512,512]{1,0:T(8,128)S(1)}) custom-call(f32[16,512,128]{2,1,0:T(8,128)S(1)} %get-tuple-element.19.h_ref, f32[16,512,128]{2,1,0:T(8,128)S(1)} %get-tuple-element.20.p_ref, f32[2,8,2048]{2,1,0:T(8,128)S(1)} %get-tuple-element.21.ends_ref, f32[2,2048]{1,0:T(2,128)S(1)} %collective-permute-done.1.near_ref.refs_0_, ...), custom_call_target="tpu_custom_call" | custom-call | tf_op jit(solution)/shard_map/mix/pallas_call | solution.py:472
  28.2 4.2 %collective-permute-start.4 = (f32[512,512]{1,0:T(8,128)S(1)}, f32[512,512]{1,0:T(8,128)S(1)}, u32[]{:S(2)}, u32[]{:S(2)}) collective-permute-start(f32[512,512]{1,0:T(8,128)S(1)} %get-tuple-element.24.a_ref), channel_id=1, source_target_pairs={{0,1},{1,0},{2,3},{3,2},{4,5},{5,4},{6,7},{7,6},{8,9},{9,8},{10,11... | collective-permute-start | bytes 3145736 | tf_op jit(solution)/shard_map/ppermute | solution.py:39
  32.4 2.3 %collective-permute-done.4.b_ref = f32[512,512]{1,0:T(8,128)S(1)} collective-permute-done((f32[512,512]{1,0:T(8,128)S(1)}, f32[512,512]{1,0:T(8,128)S(1)}, u32[]{:S(2)}, u32[]{:S(2)}) %collective-permute-start.4) | collective-permute-done | bytes 1048608 | tf_op jit(solution)/shard_map/ppermute | solution.py:39
  34.9 0.5 collective-permute-start.5
  35.4 1.7 %collective-permute-start.12 = (bf16[512,256]{1,0:T(8,128)(2,1)S(1)}, bf16[512,256]{1,0:T(8,128)(2,1)S(1)}, u32[]{:S(2)}, u32[]{:S(2)}) collective-permute-start(bf16[512,256]{1,0:T(8,128)(2,1)S(1)} %get-tuple-element.25), channel_id=1, source_target_pairs={{0,2},{2,0},{4,6},{6,4},{8,10},{10,8},{12,14},{14,12},{1,3},{3,1},... | collective-permute-start | bytes 786440 | tf_op jit(solution)/shard_map/ppermute | solution.py:35
  37.2 5.3 %collective-permute-done.5.refs_2_ = bf16[512,256]{1,0:T(8,128)(2,1)S(1)} collective-permute-done((bf16[512,256]{1,0:T(8,128)(2,1)S(1)}, bf16[512,256]{1,0:T(8,128)(2,1)S(1)}, u32[]{:S(2)}, u32[]{:S(2)}) %collective-permute-start.5) | collective-permute-done | bytes 262176 | tf_op jit(solution)/shard_map/ppermute | solution.py:30
  42.5 2.3 %collective-permute-start.6 = (bf16[512,256]{1,0:T(8,128)(2,1)S(1)}, bf16[512,256]{1,0:T(8,128)(2,1)S(1)}, u32[]{:S(2)}, u32[]{:S(2)}) collective-permute-start(bf16[512,256]{1,0:T(8,128)(2,1)S(1)} %collective-permute-done.5.refs_2_), channel_id=1, source_target_pairs={{0,4},{2,6},{4,8},{6,10},{8,12},{10,14},{12,0},{14,2},{1,5},{3,7},... | collective-permute-start | bytes 786440 | tf_op jit(solution)/shard_map/ppermute | solution.py:30
  44.7 1.7 %collective-permute-start.9 = (bf16[512,256]{1,0:T(8,128)(2,1)S(1)}, bf16[512,256]{1,0:T(8,128)(2,1)S(1)}, u32[]{:S(2)}, u32[]{:S(2)}) collective-permute-start(bf16[512,256]{1,0:T(8,128)(2,1)S(1)} %collective-permute-done.5.refs_2_), channel_id=1, source_target_pairs={{0,2},{2,0},{4,6},{6,4},{8,10},{10,8},{12,14},{14,12},{1,3},{3,1},... | collective-permute-start | bytes 786440 | tf_op jit(solution)/shard_map/ppermute | solution.py:35
  46.5 1.8 %collective-permute-start.13 = (bf16[512,256]{1,0:T(8,128)(2,1)S(1)}, bf16[512,256]{1,0:T(8,128)(2,1)S(1)}, u32[]{:S(2)}, u32[]{:S(2)}) collective-permute-start(bf16[512,256]{1,0:T(8,128)(2,1)S(1)} %collective-permute-done.12.refs_0_), channel_id=1, source_target_pairs={{0,1},{1,0},{2,3},{3,2},{4,5},{5,4},{6,7},{7,6},{8,9},{9,8},{10,11... | collective-permute-start | bytes 786440 | tf_op jit(solution)/shard_map/ppermute | solution.py:39
  48.3 6.2 %attend_own.1 = (f32[512,2048]{1,0:T(8,128)S(1)}, f32[512,1024]{1,0:T(8,128)S(1)}, f32[512,1024]{1,0:T(8,128)S(1)}) custom-call(s32[4]{0:T(128)S(1)} %convert_reduce_fusion.starts_ref, bf16[512,2048]{1,0:T(8,128)(2,1)S(1)} %copy-done.2, bf16[2,512,256]{2,1,0:T(8,128)(2,1)S(1)} %get-tuple-element.26.refs_0_), custom_call_target="tpu_custom_call" | custom-call | flops 2147483648 | bytes 4194304 | tf_op jit(solution)/shard_map/attend_own/pallas_call | solution.py:532
  54.5 0.6 collective-permute-start.11
  55.2 11.5 %attend_mid.2 = (f32[512,2048]{1,0:T(8,128)S(1)}, f32[512,1024]{1,0:T(8,128)S(1)}, f32[512,1024]{1,0:T(8,128)S(1)}) custom-call(s32[4]{0:T(128)S(1)} %convert_reduce_fusion.starts_ref, bf16[512,2048]{1,0:T(8,128)(2,1)S(1)} %copy-done.2, ...), custom_call_target="tpu_custom_call", output_to_operand_aliasing={{0}: (6, {}), {1}: (7, {}), {2}: (8, {})} | custom-call | flops 4294967296 | bytes 4194304 | tf_op jit(solution)/shard_map/attend_mid/pallas_call | solution.py:532
  66.7 0.4 collective-permute-start.8
  67.2 11.5 %attend_mid.3 = (f32[512,2048]{1,0:T(8,128)S(1)}, f32[512,1024]{1,0:T(8,128)S(1)}, f32[512,1024]{1,0:T(8,128)S(1)}) custom-call(s32[4]{0:T(128)S(1)} %convert_reduce_fusion.starts_ref, bf16[512,2048]{1,0:T(8,128)(2,1)S(1)} %copy-done.2, ...), custom_call_target="tpu_custom_call", output_to_operand_aliasing={{0}: (6, {}), {1}: (7, {}), {2}: (8, {})} | custom-call | flops 4294967296 | bytes 4194304 | tf_op jit(solution)/shard_map/attend_mid/pallas_call | solution.py:532
  78.7 3.0 %attend_end.1 = bf16[512,2048]{1,0:T(8,128)(2,1)} custom-call(s32[4]{0:T(128)S(1)} %convert_reduce_fusion.starts_ref, bf16[512,2048]{1,0:T(8,128)(2,1)S(1)} %copy-done.2, bf16[512,256]{1,0:T(8,128)(2,1)S(1)} %collective-permute-done.7.refs_0_, bf16[512,256]{1,0:T(8,128)(2,1)S(1)} %collective-permute-done.8.refs_1_, ...), custom_call_target="tpu_custom_call" | custom-call | flops 2147483648 | bytes 4194304 | tf_op jit(solution)/shard_map/attend_end/pallas_call | solution.py:532
  (24 shorter events, 0.5 us)
Async XLA Ops:
  1.4 2.6 %collective-permute-start = (bf16[3,2048]{1,0:T(4,128)(2,1)S(1)}, bf16[3,2048]{1,0:T(4,128)(2,1)S(1)}, u32[]{:S(2)}, u32[]{:S(2)}) collective-permute-start(bf16[3,2048]{1,0:T(4,128)(2,1)S(1)} %slice.3), channel_id=1, source_target_pairs={{0,2},{2,4},{4,6},{6,8},{8,10},{10,12},{12,14},{14,0},{1,3},{3,5},... | collective-permute-start | bytes 36872 | tf_op jit(solution)/shard_map/ppermute | solution.py:30
  4.0 19.8 %copy-start = (bf16[512,2048]{1,0:T(8,128)(2,1)S(1)}, bf16[512,2048]{1,0:T(8,128)(2,1)}, u32[]{:S(2)}) copy-start(bf16[512,2048]{1,0:T(8,128)(2,1)} %refs_3_.1) | copy-start | bytes 6291460
  4.0 19.8 %copy-start.1 = (bf16[2048,512]{1,0:T(8,128)(2,1)S(1)}, bf16[2048,512]{1,0:T(8,128)(2,1)}, u32[]{:S(2)}) copy-start(bf16[2048,512]{1,0:T(8,128)(2,1)} %refs_4_.1) | copy-start | bytes 6291460
  4.1 19.8 %copy-start.3 = (f32[16,512]{1,0:T(8,128)S(1)}, f32[16,512]{1,0:T(8,128)}, u32[]{:S(2)}) copy-start(f32[16,512]{1,0:T(8,128)} %refs_5_.1) | copy-start | bytes 98308
  16.1 2.7 %collective-permute-start.1 = (f32[2,2048]{1,0:T(2,128)S(1)}, f32[2,2048]{1,0:T(2,128)S(1)}, u32[]{:S(2)}, u32[]{:S(2)}) collective-permute-start(f32[2,2048]{1,0:T(2,128)S(1)} %get-tuple-element.22.tot_ref), channel_id=1, source_target_pairs={{0,2},{2,0},{4,6},{6,4},{8,10},{10,8},{12,14},{14,12},{1,3},{3,1},... | collective-permute-start | bytes 49160 | tf_op jit(solution)/shard_map/ppermute | solution.py:35
  18.7 2.6 %collective-permute-start.2 = (f32[2,2048]{1,0:T(2,128)S(1)}, f32[2,2048]{1,0:T(2,128)S(1)}, u32[]{:S(2)}, u32[]{:S(2)}) collective-permute-start(f32[2,2048]{1,0:T(2,128)S(1)} %level.1), channel_id=1, source_target_pairs={{0,4},{2,6},{4,8},{6,10},{8,12},{10,14},{12,0},{14,2},{1,5},{3,7},... | collective-permute-start | bytes 49160 | tf_op jit(solution)/shard_map/ppermute | solution.py:30
  20.3 3.5 %collective-permute-start.3 = (f32[2,2048]{1,0:T(2,128)S(1)}, f32[2,2048]{1,0:T(2,128)S(1)}, u32[]{:S(2)}, u32[]{:S(2)}) collective-permute-start(f32[2,2048]{1,0:T(2,128)S(1)} %level.1), channel_id=1, source_target_pairs={{0,8},{2,10},{4,12},{6,14},{8,0},{10,2},{12,4},{14,6},{1,9},{3,11}... | collective-permute-start | bytes 49160 | tf_op jit(solution)/shard_map/ppermute | solution.py:30
  28.2 20.0 %copy-start.2 = (bf16[512,2048]{1,0:T(8,128)(2,1)S(1)}, bf16[512,2048]{1,0:T(8,128)(2,1)}, u32[]{:S(2)}) copy-start(bf16[512,2048]{1,0:T(8,128)(2,1)} %q_ref.7) | copy-start | bytes 6291460
  28.2 6.5 %collective-permute-start.4 = (f32[512,512]{1,0:T(8,128)S(1)}, f32[512,512]{1,0:T(8,128)S(1)}, u32[]{:S(2)}, u32[]{:S(2)}) collective-permute-start(f32[512,512]{1,0:T(8,128)S(1)} %get-tuple-element.24.a_ref), channel_id=1, source_target_pairs={{0,1},{1,0},{2,3},{3,2},{4,5},{5,4},{6,7},{7,6},{8,9},{9,8},{10,11... | collective-permute-start | bytes 3145736 | tf_op jit(solution)/shard_map/ppermute | solution.py:39
  34.9 7.5 %collective-permute-start.5 = (bf16[512,256]{1,0:T(8,128)(2,1)S(1)}, bf16[512,256]{1,0:T(8,128)(2,1)S(1)}, u32[]{:S(2)}, u32[]{:S(2)}) collective-permute-start(bf16[512,256]{1,0:T(8,128)(2,1)S(1)} %get-tuple-element.25), channel_id=1, source_target_pairs={{0,4},{2,6},{4,8},{6,10},{8,12},{10,14},{12,0},{14,2},{1,5},{3,7},... | collective-permute-start | bytes 786440 | tf_op jit(solution)/shard_map/ppermute | solution.py:30
  35.4 11.0 %collective-permute-start.12 = (bf16[512,256]{1,0:T(8,128)(2,1)S(1)}, bf16[512,256]{1,0:T(8,128)(2,1)S(1)}, u32[]{:S(2)}, u32[]{:S(2)}) collective-permute-start(bf16[512,256]{1,0:T(8,128)(2,1)S(1)} %get-tuple-element.25), channel_id=1, source_target_pairs={{0,2},{2,0},{4,6},{6,4},{8,10},{10,8},{12,14},{14,12},{1,3},{3,1},... | collective-permute-start | bytes 786440 | tf_op jit(solution)/shard_map/ppermute | solution.py:35
  42.5 12.0 %collective-permute-start.6 = (bf16[512,256]{1,0:T(8,128)(2,1)S(1)}, bf16[512,256]{1,0:T(8,128)(2,1)S(1)}, u32[]{:S(2)}, u32[]{:S(2)}) collective-permute-start(bf16[512,256]{1,0:T(8,128)(2,1)S(1)} %collective-permute-done.5.refs_2_), channel_id=1, source_target_pairs={{0,4},{2,6},{4,8},{6,10},{8,12},{10,14},{12,0},{14,2},{1,5},{3,7},... | collective-permute-start | bytes 786440 | tf_op jit(solution)/shard_map/ppermute | solution.py:30
  44.7 10.3 %collective-permute-start.9 = (bf16[512,256]{1,0:T(8,128)(2,1)S(1)}, bf16[512,256]{1,0:T(8,128)(2,1)S(1)}, u32[]{:S(2)}, u32[]{:S(2)}) collective-permute-start(bf16[512,256]{1,0:T(8,128)(2,1)S(1)} %collective-permute-done.5.refs_2_), channel_id=1, source_target_pairs={{0,2},{2,0},{4,6},{6,4},{8,10},{10,8},{12,14},{14,12},{1,3},{3,1},... | collective-permute-start | bytes 786440 | tf_op jit(solution)/shard_map/ppermute | solution.py:35
  46.5 8.7 %collective-permute-start.13 = (bf16[512,256]{1,0:T(8,128)(2,1)S(1)}, bf16[512,256]{1,0:T(8,128)(2,1)S(1)}, u32[]{:S(2)}, u32[]{:S(2)}) collective-permute-start(bf16[512,256]{1,0:T(8,128)(2,1)S(1)} %collective-permute-done.12.refs_0_), channel_id=1, source_target_pairs={{0,1},{1,0},{2,3},{3,2},{4,5},{5,4},{6,7},{7,6},{8,9},{9,8},{10,11... | collective-permute-start | bytes 786440 | tf_op jit(solution)/shard_map/ppermute | solution.py:39
  48.2 7.0 %collective-permute-start.14 = (bf16[512,256]{1,0:T(8,128)(2,1)S(1)}, bf16[512,256]{1,0:T(8,128)(2,1)S(1)}, u32[]{:S(2)}, u32[]{:S(2)}) collective-permute-start(bf16[512,256]{1,0:T(8,128)(2,1)S(1)} %collective-permute-done.5.refs_2_), channel_id=1, source_target_pairs={{0,1},{1,0},{2,3},{3,2},{4,5},{5,4},{6,7},{7,6},{8,9},{9,8},{10,11... | collective-permute-start | bytes 786440 | tf_op jit(solution)/shard_map/ppermute | solution.py:39
  54.5 12.7 %collective-permute-start.11 = (bf16[512,256]{1,0:T(8,128)(2,1)S(1)}, bf16[512,256]{1,0:T(8,128)(2,1)S(1)}, u32[]{:S(2)}, u32[]{:S(2)}) collective-permute-start(bf16[512,256]{1,0:T(8,128)(2,1)S(1)} %collective-permute-done.6.refs_2_), channel_id=1, source_target_pairs={{0,1},{1,0},{2,3},{3,2},{4,5},{5,4},{6,7},{7,6},{8,9},{9,8},{10,11... | collective-permute-start | bytes 786440 | tf_op jit(solution)/shard_map/ppermute | solution.py:39
  55.0 11.7 %collective-permute-start.7 = (bf16[512,256]{1,0:T(8,128)(2,1)S(1)}, bf16[512,256]{1,0:T(8,128)(2,1)S(1)}, u32[]{:S(2)}, u32[]{:S(2)}) collective-permute-start(bf16[512,256]{1,0:T(8,128)(2,1)S(1)} %collective-permute-done.6.refs_2_), channel_id=1, source_target_pairs={{0,2},{2,0},{4,6},{6,4},{8,10},{10,8},{12,14},{14,12},{1,3},{3,1},... | collective-permute-start | bytes 786440 | tf_op jit(solution)/shard_map/ppermute | solution.py:35
  55.0 12.1 %collective-permute-start.10 = (bf16[512,256]{1,0:T(8,128)(2,1)S(1)}, bf16[512,256]{1,0:T(8,128)(2,1)S(1)}, u32[]{:S(2)}, u32[]{:S(2)}) collective-permute-start(bf16[512,256]{1,0:T(8,128)(2,1)S(1)} %collective-permute-done.9.refs_0_), channel_id=1, source_target_pairs={{0,1},{1,0},{2,3},{3,2},{4,5},{5,4},{6,7},{7,6},{8,9},{9,8},{10,11... | collective-permute-start | bytes 786440 | tf_op jit(solution)/shard_map/ppermute | solution.py:39
  66.7 12.0 %collective-permute-start.8 = (bf16[512,256]{1,0:T(8,128)(2,1)S(1)}, bf16[512,256]{1,0:T(8,128)(2,1)S(1)}, u32[]{:S(2)}, u32[]{:S(2)}) collective-permute-start(bf16[512,256]{1,0:T(8,128)(2,1)S(1)} %collective-permute-done.7.refs_0_), channel_id=1, source_target_pairs={{0,1},{1,0},{2,3},{3,2},{4,5},{5,4},{6,7},{7,6},{8,9},{9,8},{10,11... | collective-permute-start | bytes 786440 | tf_op jit(solution)/shard_map/ppermute | solution.py:39

commit v3 on v2

--- a/solution.py
+++ b/solution.py
@@ -250,6 +250,7 @@
     low, score, top = take(3)
     if final:
         acc, m_ref, l_ref, stage, sems = take(5)
+    prob, l_new, excess = (None, None, None) if own else take(3)
     rows = q_ref.shape[0]
     half = rows // 2
     me = lax.axis_index("tm")
@@ -361,8 +362,6 @@
             def _(j=j, pair=pair):
                 value_pass(g, j, pair)
 
-    any_live = None if own else functools.reduce(jnp.logical_or, live)
-
     def loop(fn):
         def body(g, z):
             fn(g)
@@ -377,34 +376,104 @@
         start_up()
         loop(update)
         return
+
+    def exp_pass(g, j, pair, start, masked):
+        for h in range(GROUP):
+            m = prev[1][:, lanes(g, h, 128)]
+            total = l_new[:, lanes(g, h, 128)]
+            worst = excess[...]
+            for t in range(2):
+                s = jnp.dot(q_ref[:, lanes(g, h, HD)], keys_of(pair, t), preferred_element_type=F32)
+                for c in range(half // 128):
+                    part = s[:, c * 128 : (c + 1) * 128] * scale
+                    if masked:
+                        side = jnp.where(core == t, 0, 1)
+                        kpos = lax.broadcasted_iota(jnp.int32, part.shape, 1) + (start + side * half + c * 128)
+                        part = jnp.where(kpos >= low[...], part, -1e30)
+                    part = part - m
+                    worst = jnp.maximum(worst, part)
+                    p = jnp.exp2(part)
+                    total = total + p
+                    at = t * half + c * 128
+                    prob[j, g * GROUP + h, :, at : at + 128] = p.astype(BF16)
+            l_new[:, lanes(g, h, 128)] = total
+            excess[...] = worst
+
+    def weighted(g, h, j, pair):
+        values = jnp.concatenate([values_of(pair, t) for t in range(2)], 0)
+        return jnp.dot(prob[j, g * GROUP + h], values, preferred_element_type=F32)
+
+    def exp_all(g):
+        for j, (pair, start) in enumerate(tiles):
+
+            @pl.when(live[j] & (start >= lo_last))
+            def _(j=j, pair=pair, start=start):
+                exp_pass(g, j, pair, start, False)
+
+            @pl.when(live[j] & (start < lo_last))
+            def _(j=j, pair=pair, start=start):
+                exp_pass(g, j, pair, start, True)
+
+    any_live = functools.reduce(jnp.logical_or, live)
+
+    @pl.when(any_live)
+    def _():
+        start_up()
+        l_new[...] = prev[2][...]
+        excess[...] = jnp.full(excess.shape, -1e30, F32)
+        loop(exp_all)
+
+    within = jnp.max(excess[...]) <= 64.0
+    fast = any_live & within
+    slow = any_live & jnp.logical_not(within)
+
     if not final:
 
-        @pl.when(any_live)
+        def add_all(g):
+            for j, (pair, start) in enumerate(tiles):
+
+                @pl.when(live[j])
+                def _(j=j, pair=pair):
+                    for h in range(GROUP):
+                        acc[:, lanes(g, h, HD)] += weighted(g, h, j, pair)
+
+        @pl.when(fast)
         def _():
-            start_up()
+            l_ref[...] = l_new[...]
+            loop(add_all)
+
+        @pl.when(slow)
+        def _():
             loop(update)
 
         return
-
-    pl.when(any_live)(start_up)
 
     def outgoing(g):
         wide = pl.ds(pl.multiple_of(g * GROUP * HD, GROUP * HD), GROUP * HD)
         return pltpu.make_async_copy(stage.at[g], out.at[:, wide], sems.at[g])
 
+    def settle(g, h, top_sum, below):
+        share = jnp.broadcast_to(1.0 / jnp.sum(below, axis=1, keepdims=True), (rows, 128))
+        stage[g, :, h * HD : (h + 1) * HD] = (top_sum * spread(share)).astype(BF16)
+
     def finish(g):
-        pl.when(any_live)(lambda: update(g))
+        @pl.when(fast)
+        def _():
+            for h in range(GROUP):
+                sums = prev[0][:, lanes(g, h, HD)] + weighted(g, h, 0, tiles[0][0])
+                settle(g, h, sums, l_new[:, lanes(g, h, 128)])
+
+        @pl.when(slow)
+        def _():
+            update(g)
+            for h in range(GROUP):
+                settle(g, h, acc[:, kept(g, h, HD)], l_ref[:, kept(g, h, 128)])
 
         @pl.when(jnp.logical_not(any_live))
         def _():
             for h in range(GROUP):
-                l_ref[:, kept(g, h, 128)] = prev[2][:, lanes(g, h, 128)]
-                acc[:, kept(g, h, HD)] = prev[0][:, lanes(g, h, HD)]
-
-        for h in range(GROUP):
-            total = jnp.sum(l_ref[:, kept(g, h, 128)], axis=1, keepdims=True)
-            share = jnp.broadcast_to(1.0 / total, (rows, 128))
-            stage[g, :, h * HD : (h + 1) * HD] = (acc[:, kept(g, h, HD)] * spread(share)).astype(BF16)
+                settle(g, h, prev[0][:, lanes(g, h, HD)], prev[2][:, lanes(g, h, 128)])
+
         outgoing(g).start()
 
     loop(finish)
@@ -524,7 +593,13 @@
         out_shape = jax.ShapeDtypeStruct((rows, width), BF16)
         scratch += [pltpu.VMEM((rows, GROUP * n), F32) for n in (HD, 128, 128)]
         scratch += [pltpu.VMEM((heads // GROUP, rows, GROUP * HD), BF16), pltpu.SemaphoreType.DMA((heads // GROUP,))]
-    else:
+    if own is None:
+        scratch += [
+            pltpu.VMEM((tiles, heads, rows, rows), BF16),
+            pltpu.VMEM((rows, heads * 128), F32),
+            pltpu.VMEM((rows, 128), F32),
+        ]
+    if not final:
         out_specs = [vmem] * 3
         out_shape = [jax.ShapeDtypeStruct((rows, heads * n), F32) for n in (HD, 128, 128)]
         if prev:

time: 82 us -> 95.4 us (1.16)
  the two profiles are of different devices: /device:TPU:31 before, /device:TPU:17 now
where the time goes in v3:
time: 95.4 us; the launch traced here: 95.1 us
  Pallas kernels  62.2 us (65%)
  starting transfers between devices  15.7 us (16%)
  waiting for transfers between devices  14.6 us (15%)
    pallas_call x4, Pallas kernels, attend_call(): pl.pallas_call(functools.partial(attend_kernel, own is not None, lags, fi...  45.6 us
    pallas_call x1, Pallas kernels, recur_call(): pl.pallas_call(recur_kernel, grid_spec=pltpu.PrefetchScalarGridSpec(num_s...  12 us
    ppermute x5, waiting for transfers between devices, ring(): return lax.ppermute(x, 'tm', [(i, (i + lag) % n) for i in range(n)])  10.1 us
    ppermute x6, starting transfers between devices, partner(): return lax.ppermute(x, 'mp', [(0, 1), (1, 0)])  7.07 us
    ppermute x5, starting transfers between devices, ring(): return lax.ppermute(x, 'tm', [(i, (i + lag) % n) for i in range(n)])  6.52 us
    pallas_call x1, Pallas kernels, mix_call(): pl.pallas_call(functools.partial(mix_kernel, len(past)), grid=(channels /...  4.4 us
    ppermute x6, waiting for transfers between devices, partner(): return lax.ppermute(x, 'mp', [(0, 1), (1, 0)])  2.3 us
    ppermute x4, waiting for transfers between devices, swap(): return lax.ppermute(x, 'tm', [(i, i ^ 1) for i in range(n)])  2.26 us
  transfers between devices with their start and end apart: 15, of which 6 were waited for; matrix products, arithmetic and copies ran while one was open for 1% of the time, Pallas kernels for 37%

profile of v3, /device:TPU:17, one launch (start us, length us, event | category | flops | bytes accessed | tf_op | source)
XLA Modules:
  0.0 95.1 jit_solution(7365046730773290759)
XLA Ops:
  0.6 0.8 slice.3
  1.4 1.3 %collective-permute-start = (bf16[3,2048]{1,0:T(4,128)(2,1)S(1)}, bf16[3,2048]{1,0:T(4,128)(2,1)S(1)}, u32[]{:S(2)}, u32[]{:S(2)}) collective-permute-start(bf16[3,2048]{1,0:T(4,128)(2,1)S(1)} %slice.3), channel_id=1, source_target_pairs={{0,2},{2,4},{4,6},{6,8},{8,10},{10,12},{12,14},{14,0},{1,3},{3,5},... | collective-permute-start | bytes 36872 | tf_op jit(solution)/shard_map/ppermute | solution.py:30
  2.7 0.9 convert_reduce_fusion.starts_ref
  3.6 1.4 %collective-permute-done.halo_ref = bf16[3,2048]{1,0:T(4,128)(2,1)S(1)} collective-permute-done((bf16[3,2048]{1,0:T(4,128)(2,1)S(1)}, bf16[3,2048]{1,0:T(4,128)(2,1)S(1)}, u32[]{:S(2)}, u32[]{:S(2)}) %collective-permute-start) | collective-permute-done | bytes 12320 | tf_op jit(solution)/shard_map/ppermute | solution.py:30
  5.0 12.0 %recur.1 = (f32[16,512,128]{2,1,0:T(8,128)S(1)}, f32[16,512,128]{2,1,0:T(8,128)S(1)}, f32[2,8,2048]{2,1,0:T(8,128)S(1)}, f32[2,2048]{1,0:T(2,128)S(1)}) custom-call(s32[4]{0:T(128)S(1)} %convert_reduce_fusion.starts_ref, bf16[512,2048]{1,0:T(8,128)(2,1)} %x_ref.1, bf16[3,2048]{1,0:T(4,128)(2,1)S(1)} %collective-permute-done.halo_ref, f32[4,2048]{1,0:T(4,128)} %cw_ref.1, ...), custom_call_target="tpu_custom_call" | custom-call | tf_op jit(solution)/shard_map/recur/pallas_call | solution.py:487
  17.0 0.4 collective-permute-start.1
  17.4 2.2 %collective-permute-done.1.near_ref.refs_0_ = f32[2,2048]{1,0:T(2,128)S(1)} collective-permute-done((f32[2,2048]{1,0:T(2,128)S(1)}, f32[2,2048]{1,0:T(2,128)S(1)}, u32[]{:S(2)}, u32[]{:S(2)}) %collective-permute-start.1) | collective-permute-done | bytes 16416 | tf_op jit(solution)/shard_map/ppermute | solution.py:35
  19.7 1.3 %collective-permute-start.2 = (f32[2,2048]{1,0:T(2,128)S(1)}, f32[2,2048]{1,0:T(2,128)S(1)}, u32[]{:S(2)}, u32[]{:S(2)}) collective-permute-start(f32[2,2048]{1,0:T(2,128)S(1)} %level.1), channel_id=1, source_target_pairs={{0,4},{2,6},{4,8},{6,10},{8,12},{10,14},{12,0},{14,2},{1,5},{3,7},... | collective-permute-start | bytes 49160 | tf_op jit(solution)/shard_map/ppermute | solution.py:30
  21.0 0.7 collective-permute-start.3
  21.7 0.6 collective-permute-done.2.refs_1_
  22.3 2.2 %collective-permute-done.3.refs_2_ = f32[2,2048]{1,0:T(2,128)S(1)} collective-permute-done((f32[2,2048]{1,0:T(2,128)S(1)}, f32[2,2048]{1,0:T(2,128)S(1)}, u32[]{:S(2)}, u32[]{:S(2)}) %collective-permute-start.3) | collective-permute-done | bytes 16416 | tf_op jit(solution)/shard_map/ppermute | solution.py:30
  24.5 4.4 %mix.1 = (bf16[512,2048]{1,0:T(8,128)(2,1)}, f32[512,512]{1,0:T(8,128)S(1)}) custom-call(f32[16,512,128]{2,1,0:T(8,128)S(1)} %get-tuple-element.19.h_ref, f32[16,512,128]{2,1,0:T(8,128)S(1)} %get-tuple-element.20.p_ref, f32[2,8,2048]{2,1,0:T(8,128)S(1)} %get-tuple-element.21.ends_ref, f32[2,2048]{1,0:T(2,128)S(1)} %collective-permute-done.1.near_ref.refs_0_, ...), custom_call_target="tpu_custom_call" | custom-call | tf_op jit(solution)/shard_map/mix/pallas_call | solution.py:541
  28.9 4.4 %collective-permute-start.4 = (f32[512,512]{1,0:T(8,128)S(1)}, f32[512,512]{1,0:T(8,128)S(1)}, u32[]{:S(2)}, u32[]{:S(2)}) collective-permute-start(f32[512,512]{1,0:T(8,128)S(1)} %get-tuple-element.24.a_ref), channel_id=1, source_target_pairs={{0,1},{1,0},{2,3},{3,2},{4,5},{5,4},{6,7},{7,6},{8,9},{9,8},{10,11... | collective-permute-start | bytes 3145736 | tf_op jit(solution)/shard_map/ppermute | solution.py:39
  33.3 2.3 %collective-permute-done.4.b_ref = f32[512,512]{1,0:T(8,128)S(1)} collective-permute-done((f32[512,512]{1,0:T(8,128)S(1)}, f32[512,512]{1,0:T(8,128)S(1)}, u32[]{:S(2)}, u32[]{:S(2)}) %collective-permute-start.4) | collective-permute-done | bytes 1048608 | tf_op jit(solution)/shard_map/ppermute | solution.py:39
  35.8 1.6 %collective-permute-start.5 = (bf16[512,256]{1,0:T(8,128)(2,1)S(1)}, bf16[512,256]{1,0:T(8,128)(2,1)S(1)}, u32[]{:S(2)}, u32[]{:S(2)}) collective-permute-start(bf16[512,256]{1,0:T(8,128)(2,1)S(1)} %get-tuple-element.25), channel_id=1, source_target_pairs={{0,4},{2,6},{4,8},{6,10},{8,12},{10,14},{12,0},{14,2},{1,5},{3,7},... | collective-permute-start | bytes 786440 | tf_op jit(solution)/shard_map/ppermute | solution.py:30
  37.4 5.9 %collective-permute-done.5.refs_2_ = bf16[512,256]{1,0:T(8,128)(2,1)S(1)} collective-permute-done((bf16[512,256]{1,0:T(8,128)(2,1)S(1)}, bf16[512,256]{1,0:T(8,128)(2,1)S(1)}, u32[]{:S(2)}, u32[]{:S(2)}) %collective-permute-start.5) | collective-permute-done | bytes 262176 | tf_op jit(solution)/shard_map/ppermute | solution.py:30
  43.4 1.5 %collective-permute-start.6 = (bf16[512,256]{1,0:T(8,128)(2,1)S(1)}, bf16[512,256]{1,0:T(8,128)(2,1)S(1)}, u32[]{:S(2)}, u32[]{:S(2)}) collective-permute-start(bf16[512,256]{1,0:T(8,128)(2,1)S(1)} %collective-permute-done.5.refs_2_), channel_id=1, source_target_pairs={{0,4},{2,6},{4,8},{6,10},{8,12},{10,14},{12,0},{14,2},{1,5},{3,7},... | collective-permute-start | bytes 786440 | tf_op jit(solution)/shard_map/ppermute | solution.py:30
  44.9 1.5 %collective-permute-start.13 = (bf16[512,256]{1,0:T(8,128)(2,1)S(1)}, bf16[512,256]{1,0:T(8,128)(2,1)S(1)}, u32[]{:S(2)}, u32[]{:S(2)}) collective-permute-start(bf16[512,256]{1,0:T(8,128)(2,1)S(1)} %collective-permute-done.12.refs_0_), channel_id=1, source_target_pairs={{0,1},{1,0},{2,3},{3,2},{4,5},{5,4},{6,7},{7,6},{8,9},{9,8},{10,11... | collective-permute-start | bytes 786440 | tf_op jit(solution)/shard_map/ppermute | solution.py:39
  46.5 6.2 %attend_own.1 = (f32[512,2048]{1,0:T(8,128)S(1)}, f32[512,1024]{1,0:T(8,128)S(1)}, f32[512,1024]{1,0:T(8,128)S(1)}) custom-call(s32[4]{0:T(128)S(1)} %convert_reduce_fusion.starts_ref, bf16[512,2048]{1,0:T(8,128)(2,1)S(1)} %copy-done.2, bf16[2,512,256]{2,1,0:T(8,128)(2,1)S(1)} %get-tuple-element.26.refs_0_), custom_call_target="tpu_custom_call" | custom-call | flops 2147483648 | bytes 4194304 | tf_op jit(solution)/shard_map/attend_own/pallas_call | solution.py:607
  52.7 0.5 collective-permute-start.11
  53.2 1.7 %collective-permute-start.7 = (bf16[512,256]{1,0:T(8,128)(2,1)S(1)}, bf16[512,256]{1,0:T(8,128)(2,1)S(1)}, u32[]{:S(2)}, u32[]{:S(2)}) collective-permute-start(bf16[512,256]{1,0:T(8,128)(2,1)S(1)} %collective-permute-done.6.refs_2_), channel_id=1, source_target_pairs={{0,2},{2,0},{4,6},{6,4},{8,10},{10,8},{12,14},{14,12},{1,3},{3,1},... | collective-permute-start | bytes 786440 | tf_op jit(solution)/shard_map/ppermute | solution.py:35
  55.3 10.5 %attend_mid.2 = (f32[512,2048]{1,0:T(8,128)S(1)}, f32[512,1024]{1,0:T(8,128)S(1)}, f32[512,1024]{1,0:T(8,128)S(1)}) custom-call(s32[4]{0:T(128)S(1)} %convert_reduce_fusion.starts_ref, bf16[512,2048]{1,0:T(8,128)(2,1)S(1)} %copy-done.2, ...), custom_call_target="tpu_custom_call", output_to_operand_aliasing={{0}: (6, {}), {1}: (7, {}), {2}: (8, {})} | custom-call | flops 4294967296 | bytes 4194304 | tf_op jit(solution)/shard_map/attend_mid/pallas_call | solution.py:607
  66.0 18.1 %attend_mid.3 = (f32[512,2048]{1,0:T(8,128)S(1)}, f32[512,1024]{1,0:T(8,128)S(1)}, f32[512,1024]{1,0:T(8,128)S(1)}) custom-call(s32[4]{0:T(128)S(1)} %convert_reduce_fusion.starts_ref, bf16[512,2048]{1,0:T(8,128)(2,1)S(1)} %copy-done.2, ...), custom_call_target="tpu_custom_call", output_to_operand_aliasing={{0}: (6, {}), {1}: (7, {}), {2}: (8, {})} | custom-call | flops 4294967296 | bytes 4194304 | tf_op jit(solution)/shard_map/attend_mid/pallas_call | solution.py:607
  84.1 10.8 %attend_end.1 = bf16[512,2048]{1,0:T(8,128)(2,1)} custom-call(s32[4]{0:T(128)S(1)} %convert_reduce_fusion.starts_ref, bf16[512,2048]{1,0:T(8,128)(2,1)S(1)} %copy-done.2, bf16[512,256]{1,0:T(8,128)(2,1)S(1)} %collective-permute-done.7.refs_0_, bf16[512,256]{1,0:T(8,128)(2,1)S(1)} %collective-permute-done.8.refs_1_, ...), custom_call_target="tpu_custom_call" | custom-call | flops 2147483648 | bytes 4194304 | tf_op jit(solution)/shard_map/attend_end/pallas_call | solution.py:607
  (24 shorter events, 0.9 us)
Async XLA Ops:
  1.4 3.5 %collective-permute-start = (bf16[3,2048]{1,0:T(4,128)(2,1)S(1)}, bf16[3,2048]{1,0:T(4,128)(2,1)S(1)}, u32[]{:S(2)}, u32[]{:S(2)}) collective-permute-start(bf16[3,2048]{1,0:T(4,128)(2,1)S(1)} %slice.3), channel_id=1, source_target_pairs={{0,2},{2,4},{4,6},{6,8},{8,10},{10,12},{12,14},{14,0},{1,3},{3,5},... | collective-permute-start | bytes 36872 | tf_op jit(solution)/shard_map/ppermute | solution.py:30
  4.9 19.6 %copy-start = (bf16[512,2048]{1,0:T(8,128)(2,1)S(1)}, bf16[512,2048]{1,0:T(8,128)(2,1)}, u32[]{:S(2)}) copy-start(bf16[512,2048]{1,0:T(8,128)(2,1)} %refs_3_.1) | copy-start | bytes 6291460
  4.9 19.6 %copy-start.1 = (bf16[2048,512]{1,0:T(8,128)(2,1)S(1)}, bf16[2048,512]{1,0:T(8,128)(2,1)}, u32[]{:S(2)}) copy-start(bf16[2048,512]{1,0:T(8,128)(2,1)} %refs_4_.1) | copy-start | bytes 6291460
  4.9 19.6 %copy-start.3 = (f32[16,512]{1,0:T(8,128)S(1)}, f32[16,512]{1,0:T(8,128)}, u32[]{:S(2)}) copy-start(f32[16,512]{1,0:T(8,128)} %refs_5_.1) | copy-start | bytes 98308
  17.0 2.7 %collective-permute-start.1 = (f32[2,2048]{1,0:T(2,128)S(1)}, f32[2,2048]{1,0:T(2,128)S(1)}, u32[]{:S(2)}, u32[]{:S(2)}) collective-permute-start(f32[2,2048]{1,0:T(2,128)S(1)} %get-tuple-element.22.tot_ref), channel_id=1, source_target_pairs={{0,2},{2,0},{4,6},{6,4},{8,10},{10,8},{12,14},{14,12},{1,3},{3,1},... | collective-permute-start | bytes 49160 | tf_op jit(solution)/shard_map/ppermute | solution.py:35
  19.7 2.6 %collective-permute-start.2 = (f32[2,2048]{1,0:T(2,128)S(1)}, f32[2,2048]{1,0:T(2,128)S(1)}, u32[]{:S(2)}, u32[]{:S(2)}) collective-permute-start(f32[2,2048]{1,0:T(2,128)S(1)} %level.1), channel_id=1, source_target_pairs={{0,4},{2,6},{4,8},{6,10},{8,12},{10,14},{12,0},{14,2},{1,5},{3,7},... | collective-permute-start | bytes 49160 | tf_op jit(solution)/shard_map/ppermute | solution.py:30
  21.0 3.5 %collective-permute-start.3 = (f32[2,2048]{1,0:T(2,128)S(1)}, f32[2,2048]{1,0:T(2,128)S(1)}, u32[]{:S(2)}, u32[]{:S(2)}) collective-permute-start(f32[2,2048]{1,0:T(2,128)S(1)} %level.1), channel_id=1, source_target_pairs={{0,8},{2,10},{4,12},{6,14},{8,0},{10,2},{12,4},{14,6},{1,9},{3,11}... | collective-permute-start | bytes 49160 | tf_op jit(solution)/shard_map/ppermute | solution.py:30
  28.9 17.6 %copy-start.2 = (bf16[512,2048]{1,0:T(8,128)(2,1)S(1)}, bf16[512,2048]{1,0:T(8,128)(2,1)}, u32[]{:S(2)}) copy-start(bf16[512,2048]{1,0:T(8,128)(2,1)} %q_ref.7) | copy-start | bytes 6291460
  28.9 6.7 %collective-permute-start.4 = (f32[512,512]{1,0:T(8,128)S(1)}, f32[512,512]{1,0:T(8,128)S(1)}, u32[]{:S(2)}, u32[]{:S(2)}) collective-permute-start(f32[512,512]{1,0:T(8,128)S(1)} %get-tuple-element.24.a_ref), channel_id=1, source_target_pairs={{0,1},{1,0},{2,3},{3,2},{4,5},{5,4},{6,7},{7,6},{8,9},{9,8},{10,11... | collective-permute-start | bytes 3145736 | tf_op jit(solution)/shard_map/ppermute | solution.py:39
  35.8 7.5 %collective-permute-start.5 = (bf16[512,256]{1,0:T(8,128)(2,1)S(1)}, bf16[512,256]{1,0:T(8,128)(2,1)S(1)}, u32[]{:S(2)}, u32[]{:S(2)}) collective-permute-start(bf16[512,256]{1,0:T(8,128)(2,1)S(1)} %get-tuple-element.25), channel_id=1, source_target_pairs={{0,4},{2,6},{4,8},{6,10},{8,12},{10,14},{12,0},{14,2},{1,5},{3,7},... | collective-permute-start | bytes 786440 | tf_op jit(solution)/shard_map/ppermute | solution.py:30
  37.4 7.5 %collective-permute-start.12 = (bf16[512,256]{1,0:T(8,128)(2,1)S(1)}, bf16[512,256]{1,0:T(8,128)(2,1)S(1)}, u32[]{:S(2)}, u32[]{:S(2)}) collective-permute-start(bf16[512,256]{1,0:T(8,128)(2,1)S(1)} %get-tuple-element.25), channel_id=1, source_target_pairs={{0,2},{2,0},{4,6},{6,4},{8,10},{10,8},{12,14},{14,12},{1,3},{3,1},... | collective-permute-start | bytes 786440 | tf_op jit(solution)/shard_map/ppermute | solution.py:35
  43.4 9.3 %collective-permute-start.6 = (bf16[512,256]{1,0:T(8,128)(2,1)S(1)}, bf16[512,256]{1,0:T(8,128)(2,1)S(1)}, u32[]{:S(2)}, u32[]{:S(2)}) collective-permute-start(bf16[512,256]{1,0:T(8,128)(2,1)S(1)} %collective-permute-done.5.refs_2_), channel_id=1, source_target_pairs={{0,4},{2,6},{4,8},{6,10},{8,12},{10,14},{12,0},{14,2},{1,5},{3,7},... | collective-permute-start | bytes 786440 | tf_op jit(solution)/shard_map/ppermute | solution.py:30
  44.9 10.0 %collective-permute-start.9 = (bf16[512,256]{1,0:T(8,128)(2,1)S(1)}, bf16[512,256]{1,0:T(8,128)(2,1)S(1)}, u32[]{:S(2)}, u32[]{:S(2)}) collective-permute-start(bf16[512,256]{1,0:T(8,128)(2,1)S(1)} %collective-permute-done.5.refs_2_), channel_id=1, source_target_pairs={{0,2},{2,0},{4,6},{6,4},{8,10},{10,8},{12,14},{14,12},{1,3},{3,1},... | collective-permute-start | bytes 786440 | tf_op jit(solution)/shard_map/ppermute | solution.py:35
  44.9 10.4 %collective-permute-start.13 = (bf16[512,256]{1,0:T(8,128)(2,1)S(1)}, bf16[512,256]{1,0:T(8,128)(2,1)S(1)}, u32[]{:S(2)}, u32[]{:S(2)}) collective-permute-start(bf16[512,256]{1,0:T(8,128)(2,1)S(1)} %collective-permute-done.12.refs_0_), channel_id=1, source_target_pairs={{0,1},{1,0},{2,3},{3,2},{4,5},{5,4},{6,7},{7,6},{8,9},{9,8},{10,11... | collective-permute-start | bytes 786440 | tf_op jit(solution)/shard_map/ppermute | solution.py:39
  46.4 8.9 %collective-permute-start.14 = (bf16[512,256]{1,0:T(8,128)(2,1)S(1)}, bf16[512,256]{1,0:T(8,128)(2,1)S(1)}, u32[]{:S(2)}, u32[]{:S(2)}) collective-permute-start(bf16[512,256]{1,0:T(8,128)(2,1)S(1)} %collective-permute-done.5.refs_2_), channel_id=1, source_target_pairs={{0,1},{1,0},{2,3},{3,2},{4,5},{5,4},{6,7},{7,6},{8,9},{9,8},{10,11... | collective-permute-start | bytes 786440 | tf_op jit(solution)/shard_map/ppermute | solution.py:39
  52.7 13.3 %collective-permute-start.11 = (bf16[512,256]{1,0:T(8,128)(2,1)S(1)}, bf16[512,256]{1,0:T(8,128)(2,1)S(1)}, u32[]{:S(2)}, u32[]{:S(2)}) collective-permute-start(bf16[512,256]{1,0:T(8,128)(2,1)S(1)} %collective-permute-done.6.refs_2_), channel_id=1, source_target_pairs={{0,1},{1,0},{2,3},{3,2},{4,5},{5,4},{6,7},{7,6},{8,9},{9,8},{10,11... | collective-permute-start | bytes 786440 | tf_op jit(solution)/shard_map/ppermute | solution.py:39
  53.2 12.6 %collective-permute-start.7 = (bf16[512,256]{1,0:T(8,128)(2,1)S(1)}, bf16[512,256]{1,0:T(8,128)(2,1)S(1)}, u32[]{:S(2)}, u32[]{:S(2)}) collective-permute-start(bf16[512,256]{1,0:T(8,128)(2,1)S(1)} %collective-permute-done.6.refs_2_), channel_id=1, source_target_pairs={{0,2},{2,0},{4,6},{6,4},{8,10},{10,8},{12,14},{14,12},{1,3},{3,1},... | collective-permute-start | bytes 786440 | tf_op jit(solution)/shard_map/ppermute | solution.py:35
  55.0 11.1 %collective-permute-start.10 = (bf16[512,256]{1,0:T(8,128)(2,1)S(1)}, bf16[512,256]{1,0:T(8,128)(2,1)S(1)}, u32[]{:S(2)}, u32[]{:S(2)}) collective-permute-start(bf16[512,256]{1,0:T(8,128)(2,1)S(1)} %collective-permute-done.9.refs_0_), channel_id=1, source_target_pairs={{0,1},{1,0},{2,3},{3,2},{4,5},{5,4},{6,7},{7,6},{8,9},{9,8},{10,11... | collective-permute-start | bytes 786440 | tf_op jit(solution)/shard_map/ppermute | solution.py:39
  65.8 18.3 %collective-permute-start.8 = (bf16[512,256]{1,0:T(8,128)(2,1)S(1)}, bf16[512,256]{1,0:T(8,128)(2,1)S(1)}, u32[]{:S(2)}, u32[]{:S(2)}) collective-permute-start(bf16[512,256]{1,0:T(8,128)(2,1)S(1)} %collective-permute-done.7.refs_0_), channel_id=1, source_target_pairs={{0,1},{1,0},{2,3},{3,2},{4,5},{5,4},{6,7},{7,6},{8,9},{9,8},{10,11... | collective-permute-start | bytes 786440 | tf_op jit(solution)/shard_map/ppermute | solution.py:39

commit v4 on v3

--- a/solution.py
+++ b/solution.py
@@ -124,13 +124,16 @@
     def conv_pair(k, carry):
         carry, d0 = conv_step(2 * k, carry)
         carry, d1 = conv_step(2 * k + 1, carry)
-        co[pl.ds(pl.multiple_of(k * 2 * SEGS, 2 * SEGS), 2 * SEGS), :] = jnp.concatenate([d0, d1], 0).astype(BF16)
+        d = jnp.concatenate([d0, d1], 0).astype(BF16)
+        for c in range(width // 128):
+            co[c, pl.ds(pl.multiple_of(k * 2 * SEGS, 2 * SEGS), 2 * SEGS), :] = d[:, c * 128 : (c + 1) * 128]
         return carry
 
     lax.fori_loop(0, seg_len // 2, conv_pair, (a1, b1, c1), unroll=8)
 
     weight = dequantized(panel_ref[0], scale_ref[0]) * BF16(0.5)
-    gate[...] = jnp.dot(co[...], weight, preferred_element_type=F32)
+    conv_out = jnp.concatenate([co[c] for c in range(width // 128)], 1)
+    gate[...] = jnp.dot(conv_out, weight, preferred_element_type=F32)
 
     bias_r = jnp.broadcast_to(gb_ref[0:1, :] * 0.5, (SEGS, width))
     bias_i = jnp.broadcast_to(gb_ref[1:2, :] * 0.5, (SEGS, width))
@@ -157,7 +160,8 @@
         return h, p
 
     def scan_pair(k, carry):
-        conv = co[pl.ds(pl.multiple_of(k * 2 * SEGS, 2 * SEGS), 2 * SEGS), :].astype(F32)
+        at = pl.ds(pl.multiple_of(k * 2 * SEGS, 2 * SEGS), 2 * SEGS)
+        conv = jnp.concatenate([co[c, at, :].astype(F32) for c in range(width // 128)], 1)
         carry = scan_step(2 * k, conv[:SEGS], carry)
         return scan_step(2 * k + 1, conv[SEGS:], carry)
 
@@ -250,7 +254,7 @@
     low, score, top = take(3)
     if final:
         acc, m_ref, l_ref, stage, sems = take(5)
-    prob, l_new, excess = (None, None, None) if own else take(3)
+    prob, l_new = (None, None) if own else take(2)
     rows = q_ref.shape[0]
     half = rows // 2
     me = lax.axis_index("tm")
@@ -381,7 +385,6 @@
         for h in range(GROUP):
             m = prev[1][:, lanes(g, h, 128)]
             total = l_new[:, lanes(g, h, 128)]
-            worst = excess[...]
             for t in range(2):
                 s = jnp.dot(q_ref[:, lanes(g, h, HD)], keys_of(pair, t), preferred_element_type=F32)
                 for c in range(half // 128):
@@ -390,18 +393,15 @@
                         side = jnp.where(core == t, 0, 1)
                         kpos = lax.broadcasted_iota(jnp.int32, part.shape, 1) + (start + side * half + c * 128)
                         part = jnp.where(kpos >= low[...], part, -1e30)
-                    part = part - m
-                    worst = jnp.maximum(worst, part)
-                    p = jnp.exp2(part)
+                    p = jnp.exp2(part - m)
                     total = total + p
-                    at = t * half + c * 128
-                    prob[j, g * GROUP + h, :, at : at + 128] = p.astype(BF16)
+                    prob[j, g * GROUP + h, (t * half) // 128 + c] = p.astype(BF16)
             l_new[:, lanes(g, h, 128)] = total
-            excess[...] = worst
 
     def weighted(g, h, j, pair):
         values = jnp.concatenate([values_of(pair, t) for t in range(2)], 0)
-        return jnp.dot(prob[j, g * GROUP + h], values, preferred_element_type=F32)
+        shares = jnp.concatenate([prob[j, g * GROUP + h, c] for c in range(rows // 128)], 1)
+        return jnp.dot(shares, values, preferred_element_type=F32)
 
     def exp_all(g):
         for j, (pair, start) in enumerate(tiles):
@@ -420,10 +420,9 @@
     def _():
         start_up()
         l_new[...] = prev[2][...]
-        excess[...] = jnp.full(excess.shape, -1e30, F32)
         loop(exp_all)
 
-    within = jnp.max(excess[...]) <= 64.0
+    within = jnp.max(l_new[...]) <= 2.0**64
     fast = any_live & within
     slow = any_live & jnp.logical_not(within)
 
@@ -508,7 +507,7 @@
             scratch_shapes=[
                 pltpu.VMEM((rows + 2 * SEGS, 128), F32),
                 pltpu.VMEM((width // 128, rows + HIST * (SEGS + 1), 128), F32),
-                pltpu.VMEM((rows, width), BF16),
+                pltpu.VMEM((width // 128, rows, 128), BF16),
                 pltpu.VMEM((rows, 2 * width), F32),
             ],
         ),
@@ -595,9 +594,8 @@
         scratch += [pltpu.VMEM((heads // GROUP, rows, GROUP * HD), BF16), pltpu.SemaphoreType.DMA((heads // GROUP,))]
     if own is None:
         scratch += [
-            pltpu.VMEM((tiles, heads, rows, rows), BF16),
+            pltpu.VMEM((tiles, heads, rows // 128, rows, 128), BF16),
             pltpu.VMEM((rows, heads * 128), F32),
-            pltpu.VMEM((rows, 128), F32),
         ]
     if not final:
         out_specs = [vmem] * 3

time: 95.4 us -> 95.3 us (level)
  transfers between devices with their start and end apart: 15 -> 15, of which waited for: 6 -> 6; matrix products, arithmetic and copies ran while one was open for 1% -> 1% of each run, Pallas kernels for 37% -> 36%
where the time goes in v4:
time: 95.3 us; the launch traced here: 95.1 us
  Pallas kernels  62.1 us (65%)
  starting transfers between devices  15.8 us (17%)
  waiting for transfers between devices  14.6 us (15%)
    pallas_call x4, Pallas kernels, attend_call(): pl.pallas_call(functools.partial(attend_kernel, own is not None, lags, fi...  45.4 us
    pallas_call x1, Pallas kernels, recur_call(): pl.pallas_call(recur_kernel, grid_spec=pltpu.PrefetchScalarGridSpec(num_s...  12.1 us
    ppermute x5, waiting for transfers between devices, ring(): return lax.ppermute(x, 'tm', [(i, (i + lag) % n) for i in range(n)])  10 us
    ppermute x6, starting transfers between devices, partner(): return lax.ppermute(x, 'mp', [(0, 1), (1, 0)])  7.07 us
    ppermute x5, starting transfers between devices, ring(): return lax.ppermute(x, 'tm', [(i, (i + lag) % n) for i in range(n)])  6.61 us
    pallas_call x1, Pallas kernels, mix_call(): pl.pallas_call(functools.partial(mix_kernel, len(past)), grid=(channels /...  4.4 us
    ppermute x6, waiting for transfers between devices, partner(): return lax.ppermute(x, 'mp', [(0, 1), (1, 0)])  2.3 us
    ppermute x4, waiting for transfers between devices, swap(): return lax.ppermute(x, 'tm', [(i, i ^ 1) for i in range(n)])  2.25 us
  transfers between devices with their start and end apart: 15, of which 6 were waited for; matrix products, arithmetic and copies ran while one was open for 1% of the time, Pallas kernels for 36%

profile of v4, /device:TPU:17, one launch (start us, length us, event | category | flops | bytes accessed | tf_op | source)
XLA Modules:
  0.0 95.1 jit_solution(10604746198408282424)
XLA Ops:
  0.6 0.8 slice.3
  1.4 1.3 %collective-permute-start = (bf16[3,2048]{1,0:T(4,128)(2,1)S(1)}, bf16[3,2048]{1,0:T(4,128)(2,1)S(1)}, u32[]{:S(2)}, u32[]{:S(2)}) collective-permute-start(bf16[3,2048]{1,0:T(4,128)(2,1)S(1)} %slice.3), channel_id=1, source_target_pairs={{0,2},{2,4},{4,6},{6,8},{8,10},{10,12},{12,14},{14,0},{1,3},{3,5},... | collective-permute-start | bytes 36872 | tf_op jit(solution)/shard_map/ppermute | solution.py:30
  2.7 0.9 convert_reduce_fusion.starts_ref
  3.6 1.4 %collective-permute-done.halo_ref = bf16[3,2048]{1,0:T(4,128)(2,1)S(1)} collective-permute-done((bf16[3,2048]{1,0:T(4,128)(2,1)S(1)}, bf16[3,2048]{1,0:T(4,128)(2,1)S(1)}, u32[]{:S(2)}, u32[]{:S(2)}) %collective-permute-start) | collective-permute-done | bytes 12320 | tf_op jit(solution)/shard_map/ppermute | solution.py:30
  5.0 12.1 %recur.1 = (f32[16,512,128]{2,1,0:T(8,128)S(1)}, f32[16,512,128]{2,1,0:T(8,128)S(1)}, f32[2,8,2048]{2,1,0:T(8,128)S(1)}, f32[2,2048]{1,0:T(2,128)S(1)}) custom-call(s32[4]{0:T(128)S(1)} %convert_reduce_fusion.starts_ref, bf16[512,2048]{1,0:T(8,128)(2,1)} %x_ref.1, bf16[3,2048]{1,0:T(4,128)(2,1)S(1)} %collective-permute-done.halo_ref, f32[4,2048]{1,0:T(4,128)} %cw_ref.1, ...), custom_call_target="tpu_custom_call" | custom-call | tf_op jit(solution)/shard_map/recur/pallas_call | solution.py:486
  17.1 0.4 collective-permute-start.1
  17.5 2.2 %collective-permute-done.1.near_ref.refs_0_ = f32[2,2048]{1,0:T(2,128)S(1)} collective-permute-done((f32[2,2048]{1,0:T(2,128)S(1)}, f32[2,2048]{1,0:T(2,128)S(1)}, u32[]{:S(2)}, u32[]{:S(2)}) %collective-permute-start.1) | collective-permute-done | bytes 16416 | tf_op jit(solution)/shard_map/ppermute | solution.py:35
  19.8 1.4 %collective-permute-start.2 = (f32[2,2048]{1,0:T(2,128)S(1)}, f32[2,2048]{1,0:T(2,128)S(1)}, u32[]{:S(2)}, u32[]{:S(2)}) collective-permute-start(f32[2,2048]{1,0:T(2,128)S(1)} %level.1), channel_id=1, source_target_pairs={{0,4},{2,6},{4,8},{6,10},{8,12},{10,14},{12,0},{14,2},{1,5},{3,7},... | collective-permute-start | bytes 49160 | tf_op jit(solution)/shard_map/ppermute | solution.py:30
  21.1 0.8 collective-permute-start.3
  21.9 0.5 collective-permute-done.2.refs_1_
  22.4 2.2 %collective-permute-done.3.refs_2_ = f32[2,2048]{1,0:T(2,128)S(1)} collective-permute-done((f32[2,2048]{1,0:T(2,128)S(1)}, f32[2,2048]{1,0:T(2,128)S(1)}, u32[]{:S(2)}, u32[]{:S(2)}) %collective-permute-start.3) | collective-permute-done | bytes 16416 | tf_op jit(solution)/shard_map/ppermute | solution.py:30
  24.6 4.4 %mix.1 = (bf16[512,2048]{1,0:T(8,128)(2,1)}, f32[512,512]{1,0:T(8,128)S(1)}) custom-call(f32[16,512,128]{2,1,0:T(8,128)S(1)} %get-tuple-element.19.h_ref, f32[16,512,128]{2,1,0:T(8,128)S(1)} %get-tuple-element.20.p_ref, f32[2,8,2048]{2,1,0:T(8,128)S(1)} %get-tuple-element.21.ends_ref, f32[2,2048]{1,0:T(2,128)S(1)} %collective-permute-done.1.near_ref.refs_0_, ...), custom_call_target="tpu_custom_call" | custom-call | tf_op jit(solution)/shard_map/mix/pallas_call | solution.py:540
  29.0 4.4 %collective-permute-start.4 = (f32[512,512]{1,0:T(8,128)S(1)}, f32[512,512]{1,0:T(8,128)S(1)}, u32[]{:S(2)}, u32[]{:S(2)}) collective-permute-start(f32[512,512]{1,0:T(8,128)S(1)} %get-tuple-element.24.a_ref), channel_id=1, source_target_pairs={{0,1},{1,0},{2,3},{3,2},{4,5},{5,4},{6,7},{7,6},{8,9},{9,8},{10,11... | collective-permute-start | bytes 3145736 | tf_op jit(solution)/shard_map/ppermute | solution.py:39
  33.4 2.3 %collective-permute-done.4.b_ref = f32[512,512]{1,0:T(8,128)S(1)} collective-permute-done((f32[512,512]{1,0:T(8,128)S(1)}, f32[512,512]{1,0:T(8,128)S(1)}, u32[]{:S(2)}, u32[]{:S(2)}) %collective-permute-start.4) | collective-permute-done | bytes 1048608 | tf_op jit(solution)/shard_map/ppermute | solution.py:39
  35.9 1.6 %collective-permute-start.5 = (bf16[512,256]{1,0:T(8,128)(2,1)S(1)}, bf16[512,256]{1,0:T(8,128)(2,1)S(1)}, u32[]{:S(2)}, u32[]{:S(2)}) collective-permute-start(bf16[512,256]{1,0:T(8,128)(2,1)S(1)} %get-tuple-element.25), channel_id=1, source_target_pairs={{0,4},{2,6},{4,8},{6,10},{8,12},{10,14},{12,0},{14,2},{1,5},{3,7},... | collective-permute-start | bytes 786440 | tf_op jit(solution)/shard_map/ppermute | solution.py:30
  37.6 5.9 %collective-permute-done.5.refs_2_ = bf16[512,256]{1,0:T(8,128)(2,1)S(1)} collective-permute-done((bf16[512,256]{1,0:T(8,128)(2,1)S(1)}, bf16[512,256]{1,0:T(8,128)(2,1)S(1)}, u32[]{:S(2)}, u32[]{:S(2)}) %collective-permute-start.5) | collective-permute-done | bytes 262176 | tf_op jit(solution)/shard_map/ppermute | solution.py:30
  43.5 1.6 %collective-permute-start.6 = (bf16[512,256]{1,0:T(8,128)(2,1)S(1)}, bf16[512,256]{1,0:T(8,128)(2,1)S(1)}, u32[]{:S(2)}, u32[]{:S(2)}) collective-permute-start(bf16[512,256]{1,0:T(8,128)(2,1)S(1)} %collective-permute-done.5.refs_2_), channel_id=1, source_target_pairs={{0,4},{2,6},{4,8},{6,10},{8,12},{10,14},{12,0},{14,2},{1,5},{3,7},... | collective-permute-start | bytes 786440 | tf_op jit(solution)/shard_map/ppermute | solution.py:30
  45.0 1.5 %collective-permute-start.13 = (bf16[512,256]{1,0:T(8,128)(2,1)S(1)}, bf16[512,256]{1,0:T(8,128)(2,1)S(1)}, u32[]{:S(2)}, u32[]{:S(2)}) collective-permute-start(bf16[512,256]{1,0:T(8,128)(2,1)S(1)} %collective-permute-done.12.refs_0_), channel_id=1, source_target_pairs={{0,1},{1,0},{2,3},{3,2},{4,5},{5,4},{6,7},{7,6},{8,9},{9,8},{10,11... | collective-permute-start | bytes 786440 | tf_op jit(solution)/shard_map/ppermute | solution.py:39
  46.6 6.2 %attend_own.1 = (f32[512,2048]{1,0:T(8,128)S(1)}, f32[512,1024]{1,0:T(8,128)S(1)}, f32[512,1024]{1,0:T(8,128)S(1)}) custom-call(s32[4]{0:T(128)S(1)} %convert_reduce_fusion.starts_ref, bf16[512,2048]{1,0:T(8,128)(2,1)S(1)} %copy-done.2, bf16[2,512,256]{2,1,0:T(8,128)(2,1)S(1)} %get-tuple-element.26.refs_0_), custom_call_target="tpu_custom_call" | custom-call | flops 2147483648 | bytes 4194304 | tf_op jit(solution)/shard_map/attend_own/pallas_call | solution.py:605
  52.8 0.5 collective-permute-start.11
  53.3 1.7 %collective-permute-start.7 = (bf16[512,256]{1,0:T(8,128)(2,1)S(1)}, bf16[512,256]{1,0:T(8,128)(2,1)S(1)}, u32[]{:S(2)}, u32[]{:S(2)}) collective-permute-start(bf16[512,256]{1,0:T(8,128)(2,1)S(1)} %collective-permute-done.6.refs_2_), channel_id=1, source_target_pairs={{0,2},{2,0},{4,6},{6,4},{8,10},{10,8},{12,14},{14,12},{1,3},{3,1},... | collective-permute-start | bytes 786440 | tf_op jit(solution)/shard_map/ppermute | solution.py:35
  55.4 10.5 %attend_mid.2 = (f32[512,2048]{1,0:T(8,128)S(1)}, f32[512,1024]{1,0:T(8,128)S(1)}, f32[512,1024]{1,0:T(8,128)S(1)}) custom-call(s32[4]{0:T(128)S(1)} %convert_reduce_fusion.starts_ref, bf16[512,2048]{1,0:T(8,128)(2,1)S(1)} %copy-done.2, ...), custom_call_target="tpu_custom_call", output_to_operand_aliasing={{0}: (6, {}), {1}: (7, {}), {2}: (8, {})} | custom-call | flops 4294967296 | bytes 4194304 | tf_op jit(solution)/shard_map/attend_mid/pallas_call | solution.py:605
  66.2 17.8 %attend_mid.3 = (f32[512,2048]{1,0:T(8,128)S(1)}, f32[512,1024]{1,0:T(8,128)S(1)}, f32[512,1024]{1,0:T(8,128)S(1)}) custom-call(s32[4]{0:T(128)S(1)} %convert_reduce_fusion.starts_ref, bf16[512,2048]{1,0:T(8,128)(2,1)S(1)} %copy-done.2, ...), custom_call_target="tpu_custom_call", output_to_operand_aliasing={{0}: (6, {}), {1}: (7, {}), {2}: (8, {})} | custom-call | flops 4294967296 | bytes 4194304 | tf_op jit(solution)/shard_map/attend_mid/pallas_call | solution.py:605
  84.0 10.9 %attend_end.1 = bf16[512,2048]{1,0:T(8,128)(2,1)} custom-call(s32[4]{0:T(128)S(1)} %convert_reduce_fusion.starts_ref, bf16[512,2048]{1,0:T(8,128)(2,1)S(1)} %copy-done.2, bf16[512,256]{1,0:T(8,128)(2,1)S(1)} %collective-permute-done.7.refs_0_, bf16[512,256]{1,0:T(8,128)(2,1)S(1)} %collective-permute-done.8.refs_1_, ...), custom_call_target="tpu_custom_call" | custom-call | flops 2147483648 | bytes 4194304 | tf_op jit(solution)/shard_map/attend_end/pallas_call | solution.py:605
  (24 shorter events, 0.9 us)
Async XLA Ops:
  1.4 3.5 %collective-permute-start = (bf16[3,2048]{1,0:T(4,128)(2,1)S(1)}, bf16[3,2048]{1,0:T(4,128)(2,1)S(1)}, u32[]{:S(2)}, u32[]{:S(2)}) collective-permute-start(bf16[3,2048]{1,0:T(4,128)(2,1)S(1)} %slice.3), channel_id=1, source_target_pairs={{0,2},{2,4},{4,6},{6,8},{8,10},{10,12},{12,14},{14,0},{1,3},{3,5},... | collective-permute-start | bytes 36872 | tf_op jit(solution)/shard_map/ppermute | solution.py:30
  4.9 19.7 %copy-start = (bf16[512,2048]{1,0:T(8,128)(2,1)S(1)}, bf16[512,2048]{1,0:T(8,128)(2,1)}, u32[]{:S(2)}) copy-start(bf16[512,2048]{1,0:T(8,128)(2,1)} %refs_3_.1) | copy-start | bytes 6291460
  4.9 19.7 %copy-start.1 = (bf16[2048,512]{1,0:T(8,128)(2,1)S(1)}, bf16[2048,512]{1,0:T(8,128)(2,1)}, u32[]{:S(2)}) copy-start(bf16[2048,512]{1,0:T(8,128)(2,1)} %refs_4_.1) | copy-start | bytes 6291460
  4.9 19.7 %copy-start.3 = (f32[16,512]{1,0:T(8,128)S(1)}, f32[16,512]{1,0:T(8,128)}, u32[]{:S(2)}) copy-start(f32[16,512]{1,0:T(8,128)} %refs_5_.1) | copy-start | bytes 98308
  17.1 2.7 %collective-permute-start.1 = (f32[2,2048]{1,0:T(2,128)S(1)}, f32[2,2048]{1,0:T(2,128)S(1)}, u32[]{:S(2)}, u32[]{:S(2)}) collective-permute-start(f32[2,2048]{1,0:T(2,128)S(1)} %get-tuple-element.22.tot_ref), channel_id=1, source_target_pairs={{0,2},{2,0},{4,6},{6,4},{8,10},{10,8},{12,14},{14,12},{1,3},{3,1},... | collective-permute-start | bytes 49160 | tf_op jit(solution)/shard_map/ppermute | solution.py:35
  19.8 2.6 %collective-permute-start.2 = (f32[2,2048]{1,0:T(2,128)S(1)}, f32[2,2048]{1,0:T(2,128)S(1)}, u32[]{:S(2)}, u32[]{:S(2)}) collective-permute-start(f32[2,2048]{1,0:T(2,128)S(1)} %level.1), channel_id=1, source_target_pairs={{0,4},{2,6},{4,8},{6,10},{8,12},{10,14},{12,0},{14,2},{1,5},{3,7},... | collective-permute-start | bytes 49160 | tf_op jit(solution)/shard_map/ppermute | solution.py:30
  21.1 3.5 %collective-permute-start.3 = (f32[2,2048]{1,0:T(2,128)S(1)}, f32[2,2048]{1,0:T(2,128)S(1)}, u32[]{:S(2)}, u32[]{:S(2)}) collective-permute-start(f32[2,2048]{1,0:T(2,128)S(1)} %level.1), channel_id=1, source_target_pairs={{0,8},{2,10},{4,12},{6,14},{8,0},{10,2},{12,4},{14,6},{1,9},{3,11}... | collective-permute-start | bytes 49160 | tf_op jit(solution)/shard_map/ppermute | solution.py:30
  29.0 17.6 %copy-start.2 = (bf16[512,2048]{1,0:T(8,128)(2,1)S(1)}, bf16[512,2048]{1,0:T(8,128)(2,1)}, u32[]{:S(2)}) copy-start(bf16[512,2048]{1,0:T(8,128)(2,1)} %q_ref.7) | copy-start | bytes 6291460
  29.0 6.7 %collective-permute-start.4 = (f32[512,512]{1,0:T(8,128)S(1)}, f32[512,512]{1,0:T(8,128)S(1)}, u32[]{:S(2)}, u32[]{:S(2)}) collective-permute-start(f32[512,512]{1,0:T(8,128)S(1)} %get-tuple-element.24.a_ref), channel_id=1, source_target_pairs={{0,1},{1,0},{2,3},{3,2},{4,5},{5,4},{6,7},{7,6},{8,9},{9,8},{10,11... | collective-permute-start | bytes 3145736 | tf_op jit(solution)/shard_map/ppermute | solution.py:39
  35.9 7.5 %collective-permute-start.5 = (bf16[512,256]{1,0:T(8,128)(2,1)S(1)}, bf16[512,256]{1,0:T(8,128)(2,1)S(1)}, u32[]{:S(2)}, u32[]{:S(2)}) collective-permute-start(bf16[512,256]{1,0:T(8,128)(2,1)S(1)} %get-tuple-element.25), channel_id=1, source_target_pairs={{0,4},{2,6},{4,8},{6,10},{8,12},{10,14},{12,0},{14,2},{1,5},{3,7},... | collective-permute-start | bytes 786440 | tf_op jit(solution)/shard_map/ppermute | solution.py:30
  37.5 7.5 %collective-permute-start.12 = (bf16[512,256]{1,0:T(8,128)(2,1)S(1)}, bf16[512,256]{1,0:T(8,128)(2,1)S(1)}, u32[]{:S(2)}, u32[]{:S(2)}) collective-permute-start(bf16[512,256]{1,0:T(8,128)(2,1)S(1)} %get-tuple-element.25), channel_id=1, source_target_pairs={{0,2},{2,0},{4,6},{6,4},{8,10},{10,8},{12,14},{14,12},{1,3},{3,1},... | collective-permute-start | bytes 786440 | tf_op jit(solution)/shard_map/ppermute | solution.py:35
  43.5 9.4 %collective-permute-start.6 = (bf16[512,256]{1,0:T(8,128)(2,1)S(1)}, bf16[512,256]{1,0:T(8,128)(2,1)S(1)}, u32[]{:S(2)}, u32[]{:S(2)}) collective-permute-start(bf16[512,256]{1,0:T(8,128)(2,1)S(1)} %collective-permute-done.5.refs_2_), channel_id=1, source_target_pairs={{0,4},{2,6},{4,8},{6,10},{8,12},{10,14},{12,0},{14,2},{1,5},{3,7},... | collective-permute-start | bytes 786440 | tf_op jit(solution)/shard_map/ppermute | solution.py:30
  45.0 10.0 %collective-permute-start.9 = (bf16[512,256]{1,0:T(8,128)(2,1)S(1)}, bf16[512,256]{1,0:T(8,128)(2,1)S(1)}, u32[]{:S(2)}, u32[]{:S(2)}) collective-permute-start(bf16[512,256]{1,0:T(8,128)(2,1)S(1)} %collective-permute-done.5.refs_2_), channel_id=1, source_target_pairs={{0,2},{2,0},{4,6},{6,4},{8,10},{10,8},{12,14},{14,12},{1,3},{3,1},... | collective-permute-start | bytes 786440 | tf_op jit(solution)/shard_map/ppermute | solution.py:35
  45.0 10.4 %collective-permute-start.13 = (bf16[512,256]{1,0:T(8,128)(2,1)S(1)}, bf16[512,256]{1,0:T(8,128)(2,1)S(1)}, u32[]{:S(2)}, u32[]{:S(2)}) collective-permute-start(bf16[512,256]{1,0:T(8,128)(2,1)S(1)} %collective-permute-done.12.refs_0_), channel_id=1, source_target_pairs={{0,1},{1,0},{2,3},{3,2},{4,5},{5,4},{6,7},{7,6},{8,9},{9,8},{10,11... | collective-permute-start | bytes 786440 | tf_op jit(solution)/shard_map/ppermute | solution.py:39
  46.6 8.9 %collective-permute-start.14 = (bf16[512,256]{1,0:T(8,128)(2,1)S(1)}, bf16[512,256]{1,0:T(8,128)(2,1)S(1)}, u32[]{:S(2)}, u32[]{:S(2)}) collective-permute-start(bf16[512,256]{1,0:T(8,128)(2,1)S(1)} %collective-permute-done.5.refs_2_), channel_id=1, source_target_pairs={{0,1},{1,0},{2,3},{3,2},{4,5},{5,4},{6,7},{7,6},{8,9},{9,8},{10,11... | collective-permute-start | bytes 786440 | tf_op jit(solution)/shard_map/ppermute | solution.py:39
  52.8 13.4 %collective-permute-start.11 = (bf16[512,256]{1,0:T(8,128)(2,1)S(1)}, bf16[512,256]{1,0:T(8,128)(2,1)S(1)}, u32[]{:S(2)}, u32[]{:S(2)}) collective-permute-start(bf16[512,256]{1,0:T(8,128)(2,1)S(1)} %collective-permute-done.6.refs_2_), channel_id=1, source_target_pairs={{0,1},{1,0},{2,3},{3,2},{4,5},{5,4},{6,7},{7,6},{8,9},{9,8},{10,11... | collective-permute-start | bytes 786440 | tf_op jit(solution)/shard_map/ppermute | solution.py:39
  53.3 12.6 %collective-permute-start.7 = (bf16[512,256]{1,0:T(8,128)(2,1)S(1)}, bf16[512,256]{1,0:T(8,128)(2,1)S(1)}, u32[]{:S(2)}, u32[]{:S(2)}) collective-permute-start(bf16[512,256]{1,0:T(8,128)(2,1)S(1)} %collective-permute-done.6.refs_2_), channel_id=1, source_target_pairs={{0,2},{2,0},{4,6},{6,4},{8,10},{10,8},{12,14},{14,12},{1,3},{3,1},... | collective-permute-start | bytes 786440 | tf_op jit(solution)/shard_map/ppermute | solution.py:35
  55.1 11.1 %collective-permute-start.10 = (bf16[512,256]{1,0:T(8,128)(2,1)S(1)}, bf16[512,256]{1,0:T(8,128)(2,1)S(1)}, u32[]{:S(2)}, u32[]{:S(2)}) collective-permute-start(bf16[512,256]{1,0:T(8,128)(2,1)S(1)} %collective-permute-done.9.refs_0_), channel_id=1, source_target_pairs={{0,1},{1,0},{2,3},{3,2},{4,5},{5,4},{6,7},{7,6},{8,9},{9,8},{10,11... | collective-permute-start | bytes 786440 | tf_op jit(solution)/shard_map/ppermute | solution.py:39
  66.0 18.0 %collective-permute-start.8 = (bf16[512,256]{1,0:T(8,128)(2,1)S(1)}, bf16[512,256]{1,0:T(8,128)(2,1)S(1)}, u32[]{:S(2)}, u32[]{:S(2)}) collective-permute-start(bf16[512,256]{1,0:T(8,128)(2,1)S(1)} %collective-permute-done.7.refs_0_), channel_id=1, source_target_pairs={{0,1},{1,0},{2,3},{3,2},{4,5},{5,4},{6,7},{7,6},{8,9},{9,8},{10,11... | collective-permute-start | bytes 786440 | tf_op jit(solution)/shard_map/ppermute | solution.py:39

commit v5 on v4

--- a/solution.py
+++ b/solution.py
@@ -50,12 +50,108 @@
 
 def recur_kernel(
     starts_ref,
+    x_hbm,
+    halo_all,
+    cw_hbm,
+    cb_hbm,
+    panel_hbm,
+    scale_hbm,
+    gb_hbm,
+    rate_hbm,
+    h_ref,
+    p_ref,
+    ends_ref,
+    tot_ref,
+    keep,
+    xs,
+    co,
+    gate,
+    x_buf,
+    panel_buf,
+    cw_all,
+    cb_all,
+    scale_all,
+    gb_all,
+    rate_all,
+    sems,
+    small_sems,
+):
+    blocks, width, _ = panel_hbm.shape
+    rows = x_hbm.shape[0]
+    seg_len = rows // SEGS
+    base = lax.axis_index("tm") * rows
+
+    def fetch_x(b):
+        at = pl.ds(pl.multiple_of(b * width, width), width)
+        return pltpu.make_async_copy(x_hbm.at[:, at], x_buf.at[b % 2], sems.at[0, b % 2])
+
+    def fetch_panel(b):
+        return pltpu.make_async_copy(panel_hbm.at[b], panel_buf.at[b % 2], sems.at[1, b % 2])
+
+    fetch_x(0).start()
+    fetch_panel(0).start()
+    sources = (cw_hbm, cb_hbm, scale_hbm, gb_hbm, rate_hbm)
+    targets = (cw_all, cb_all, scale_all, gb_all, rate_all)
+    smalls = [
+        pltpu.make_async_copy(src, dst, small_sems.at[k]) for k, (src, dst) in enumerate(zip(sources, targets))
+    ]
+    for copy in smalls:
+        copy.start()
+
+    def fill(i, carry):
+        pos = base + i - 2 + seg_len * lax.broadcasted_iota(jnp.int32, (SEGS, 128), 0)
+        hit = pos == starts_ref[0]
+        for d in range(1, DOCS):
+            hit = hit | (pos == starts_ref[d])
+        keep[pl.ds(pl.multiple_of(i * SEGS, SEGS), SEGS), :] = jnp.where(hit, 0.0, 1.0)
+        return carry
+
+    lax.fori_loop(0, seg_len + 2, fill, 0)
+    for copy in smalls:
+        copy.wait()
+
+    def block(b, z):
+        fetch_x(b).wait()
+        fetch_panel(b).wait()
+
+        @pl.when(b + 1 < blocks)
+        def _():
+            fetch_x(b + 1).start()
+            fetch_panel(b + 1).start()
+
+        wide = pl.ds(pl.multiple_of(b * width, width), width)
+        recur_block(
+            b,
+            x_buf.at[b % 2],
+            halo_all.at[:, wide],
+            cw_all.at[:, wide],
+            cb_all.at[:, wide],
+            panel_buf[b % 2],
+            scale_all[b],
+            gb_all.at[:, wide],
+            rate_all.at[:, wide],
+            h_ref,
+            p_ref,
+            ends_ref.at[:, :, wide],
+            tot_ref.at[:, wide],
+            keep,
+            xs,
+            co,
+            gate,
+        )
+        return z
+
+    lax.fori_loop(0, blocks, block, 0)
+
+
+def recur_block(
+    b,
     x_ref,
     halo_ref,
     cw_ref,
     cb_ref,
-    panel_ref,
-    scale_ref,
+    panel,
+    scale,
     gb_ref,
     rate_ref,
     h_ref,
@@ -69,20 +165,6 @@
 ):
     rows, width = x_ref.shape
     seg_len = rows // SEGS
-    base = lax.axis_index("tm") * rows
-
-    @pl.when(pl.program_id(0) == 0)
-    def _():
-        def fill(i, carry):
-            pos = base + i - 2 + seg_len * lax.broadcasted_iota(jnp.int32, (SEGS, 128), 0)
-            hit = pos == starts_ref[0]
-            for d in range(1, DOCS):
-                hit = hit | (pos == starts_ref[d])
-            keep[pl.ds(pl.multiple_of(i * SEGS, SEGS), SEGS), :] = jnp.where(hit, 0.0, 1.0)
-            return carry
-
-        lax.fori_loop(0, seg_len + 2, fill, 0)
-
     pitch = seg_len + HIST
     for c in range(width // 128):
         lanes = slice(c * 128, (c + 1) * 128)
@@ -131,7 +213,7 @@
 
     lax.fori_loop(0, seg_len // 2, conv_pair, (a1, b1, c1), unroll=8)
 
-    weight = dequantized(panel_ref[0], scale_ref[0]) * BF16(0.5)
+    weight = dequantized(panel, scale) * BF16(0.5)
     conv_out = jnp.concatenate([co[c] for c in range(width // 128)], 1)
     gate[...] = jnp.dot(conv_out, weight, preferred_element_type=F32)
 
@@ -155,8 +237,8 @@
         h = decay * h + ti * (conv * half)
         p = p * decay
         for c in range(width // 128):
-            h_ref[c, at, :] = h[:, c * 128 : (c + 1) * 128]
-            p_ref[c, at, :] = p[:, c * 128 : (c + 1) * 128]
+            h_ref[b * (width // 128) + c, at, :] = h[:, c * 128 : (c + 1) * 128]
+            p_ref[b * (width // 128) + c, at, :] = p[:, c * 128 : (c + 1) * 128]
         return h, p
 
     def scan_pair(k, carry):
@@ -191,44 +273,69 @@
     level_ref[1:2, :] = upper[0:1] * lower[1:2] + upper[1:2]
 
 
-def mix_kernel(levels, h_ref, p_ref, ends_ref, *refs):
-    near_ref, past, rest = refs[0], refs[1 : levels + 1], refs[levels + 1 :]
-    y_ref, panel_ref, scale_ref, mixed_ref, kv_ref, carry = rest
-    rows, width = y_ref.shape
+def ready_kernel(h_ref, p_ref, y_ref, panel_ref, scale_ref, hg_ref, pg_ref, w_ref):
+    rows, channels = y_ref.shape
+    seg_len = rows // SEGS
+    width = MIX_GROUPS * SCALE_ROWS
+
+    def natural(ref, c, s):
+        return jnp.concatenate(
+            [ref[c, pl.ds(s + k * 8 * SEGS, 8, stride=SEGS), :] for k in range(seg_len // 8)], 0
+        )
+
+    def body(g, z):
+        wide = pl.ds(pl.multiple_of(g * width, width), width)
+        table = scale_ref[...]
+        index = lax.broadcasted_iota(jnp.int32, table.shape, 0) - g * MIX_GROUPS
+        scale = [jnp.sum(jnp.where(index == k, table, 0.0), axis=0, keepdims=True) for k in range(MIX_GROUPS)]
+        w_ref[wide, :] = dequantized(panel_ref[wide, :], jnp.concatenate(scale, 0))
+        for s in range(SEGS):
+            at = slice(s * seg_len, (s + 1) * seg_len)
+            y = y_ref[at, wide].astype(F32)
+            inner = y * (0.7978845608028654 + (0.7978845608028654 * 0.044715) * (y * y))
+            gelu = (0.5 * y) * (1.0 + jnp.tanh(inner))
+            for c in range(width // 128):
+                lanes = pl.ds(pl.multiple_of(g * width + c * 128, 128), 128)
+                part = gelu[:, c * 128 : (c + 1) * 128]
+                hg_ref[at, lanes] = natural(h_ref, g * (width // 128) + c, s) * part
+                pg_ref[at, lanes] = natural(p_ref, g * (width // 128) + c, s) * part
+        return z
+
+    lax.fori_loop(0, channels // width, body, 0)
+
+
+def mix_kernel(levels, hg_ref, pg_ref, w_ref, ends_ref, near_ref, *refs):
+    past, (mixed_hbm, kv_ref, stage, sems) = refs[:levels], refs[levels:]
+    rows, channels = hg_ref.shape
+    seg_len = rows // SEGS
+    width = MIX_GROUPS * SCALE_ROWS
     me = lax.axis_index("tm")
-    seg_len = rows // SEGS
-
-    @pl.when(pl.program_id(0) == 0)
-    def _():
-        kv_ref[...] = jnp.zeros_like(kv_ref)
-
-    c = jnp.zeros((1, width), F32)
-    for k in range(levels, 0, -1):
-        c = jnp.where(me >= 2 * k, past[k - 1][0:1, :] * c + past[k - 1][1:2, :], 0.0)
-    c = jnp.where(me % 2 == 1, near_ref[0:1, :] * c + near_ref[1:2, :], c)
-    for s in range(SEGS):
-        carry[s : s + 1, :] = c
-        c = ends_ref[0, s : s + 1, :] * c + ends_ref[1, s : s + 1, :]
-    groups = width // SCALE_ROWS
-    table = scale_ref[...]
-    index = lax.broadcasted_iota(jnp.int32, table.shape, 0) - pl.program_id(0) * groups
-    scale = [jnp.sum(jnp.where(index == g, table, 0.0), axis=0, keepdims=True) for g in range(groups)]
-    weight = dequantized(panel_ref[...], jnp.concatenate(scale, 0))
-
-    def natural(ref, g, s):
-        return jnp.concatenate(
-            [ref[g, pl.ds(s + k * 8 * SEGS, 8, stride=SEGS), :] for k in range(seg_len // 8)], 0
-        )
-
-    for s in range(SEGS):
-        at = slice(s * seg_len, (s + 1) * seg_len)
-        y = y_ref[at, :].astype(F32)
-        inner = y * (0.7978845608028654 + (0.7978845608028654 * 0.044715) * (y * y))
-        gelu = (0.5 * y) * (1.0 + jnp.tanh(inner))
-        local_h = jnp.concatenate([natural(h_ref, g, s) for g in range(width // 128)], 1)
-        local_p = jnp.concatenate([natural(p_ref, g, s) for g in range(width // 128)], 1)
-        mixed_ref[at, :] = ((local_h + local_p * carry[s : s + 1, :]) * gelu).astype(BF16)
-    kv_ref[...] += jnp.dot(mixed_ref[...], weight, preferred_element_type=F32)
+    kv_ref[...] = jnp.zeros_like(kv_ref)
+
+    def outgoing(g):
+        wide = pl.ds(pl.multiple_of(g * width, width), width)
+        return pltpu.make_async_copy(stage.at[g], mixed_hbm.at[:, wide], sems.at[g])
+
+    def body(g, z):
+        wide = pl.ds(pl.multiple_of(g * width, width), width)
+        c = jnp.zeros((1, width), F32)
+        for k in range(levels, 0, -1):
+            c = jnp.where(me >= 2 * k, past[k - 1][0:1, wide] * c + past[k - 1][1:2, wide], 0.0)
+        c = jnp.where(me % 2 == 1, near_ref[0:1, wide] * c + near_ref[1:2, wide], c)
+        for s in range(SEGS):
+            at = slice(s * seg_len, (s + 1) * seg_len)
+            stage[g, at, :] = (hg_ref[at, wide] + pg_ref[at, wide] * c).astype(BF16)
+            c = ends_ref[0, s : s + 1, wide] * c + ends_ref[1, s : s + 1, wide]
+        outgoing(g).start()
+        kv_ref[...] += jnp.dot(stage[g], w_ref[wide, :], preferred_element_type=F32)
+        return z
+
+    def drain(g, z):
+        outgoing(g).wait()
+        return z
+
+    lax.fori_loop(0, channels // width, body, 0)
+    lax.fori_loop(0, channels // width, drain, 0)
 
 
 def sum_kernel(a_ref, b_ref, own_ref, half_ref):
@@ -479,38 +586,26 @@
     loop(lambda g: outgoing(g).wait())
 
 
-def recur_call(starts, x, halo, conv_weight, conv_bias, gate_panel, gate_scale, gate_bias, decay_rate):
+def recur_call(starts, x, halo, *params):
     rows, channels = x.shape
-    blocks, width, _ = gate_panel.shape
-    col = lambda b, s: (0, b)
+    _, width, _ = params[2].shape
+    conv_weight, conv_bias, _, gate_scale, gate_bias, decay_rate = params
+    vmem = pl.BlockSpec(memory_space=pltpu.VMEM)
+    hbm = pl.BlockSpec(memory_space=pl.ANY)
     return pl.pallas_call(
         recur_kernel,
-        grid_spec=pltpu.PrefetchScalarGridSpec(
-            num_scalar_prefetch=1,
-            grid=(blocks,),
-            in_specs=[
-                pl.BlockSpec((rows, width), col),
-                pl.BlockSpec((CONV - 1, width), col),
-                pl.BlockSpec((CONV, width), col),
-                pl.BlockSpec((1, width), col),
-                pl.BlockSpec((1, width, 2 * width), lambda b, s: (b, 0, 0)),
-                pl.BlockSpec((1, width // SCALE_ROWS, 2 * width), lambda b, s: (b, 0, 0)),
-                pl.BlockSpec((2, width), col),
-                pl.BlockSpec((1, width), col),
-            ],
-            out_specs=[
-                pl.BlockSpec((width // 128, rows, 128), lambda b, s: (b, 0, 0)),
-                pl.BlockSpec((width // 128, rows, 128), lambda b, s: (b, 0, 0)),
-                pl.BlockSpec((2, SEGS, width), lambda b, s: (0, 0, b)),
-                pl.BlockSpec((2, width), col),
-            ],
-            scratch_shapes=[
-                pltpu.VMEM((rows + 2 * SEGS, 128), F32),
-                pltpu.VMEM((width // 128, rows + HIST * (SEGS + 1), 128), F32),
-                pltpu.VMEM((width // 128, rows, 128), BF16),
-                pltpu.VMEM((rows, 2 * width), F32),
-            ],
-        ),
+        in_specs=[pl.BlockSpec(memory_space=pltpu.SMEM), hbm, vmem] + [hbm] * 6,
+        out_specs=[vmem] * 4,
+        scratch_shapes=[
+            pltpu.VMEM((rows + 2 * SEGS, 128), F32),
+            pltpu.VMEM((width // 128, rows + HIST * (SEGS + 1), 128), F32),
+            pltpu.VMEM((width // 128, rows, 128), BF16),
+            pltpu.VMEM((rows, 2 * width), F32),
+            pltpu.VMEM((2, rows, width), BF16),
+            pltpu.VMEM((2, width, 2 * width), BF16),
+        ]
+        + [pltpu.VMEM(a.shape, F32) for a in (conv_weight, conv_bias, gate_scale, gate_bias, decay_rate)]
+        + [pltpu.SemaphoreType.DMA((2, 2)), pltpu.SemaphoreType.DMA((5,))],
         out_shape=[
             jax.ShapeDtypeStruct((channels // 128, rows, 128), F32),
             jax.ShapeDtypeStruct((channels // 128, rows, 128), F32),
@@ -519,7 +614,7 @@
         ],
         compiler_params=pltpu.CompilerParams(vmem_limit_bytes=20 << 20),
         name="recur",
-    )(starts, x, halo, conv_weight, conv_bias, gate_panel, gate_scale, gate_bias, decay_rate)
+    )(starts, x, halo, *params)
 
 
 def level_call(tot, near):
@@ -531,32 +626,38 @@
     )(tot, near)
 
 
-def mix_call(h, p, ends, near, past, y, kv_panel, kv_scale):
+def ready_call(h, p, y, kv_panel, kv_scale):
     rows, channels = y.shape
+    vmem = pl.BlockSpec(memory_space=pltpu.VMEM)
+    flat = jax.ShapeDtypeStruct((rows, channels), F32)
+    return pl.pallas_call(
+        ready_kernel,
+        in_specs=[vmem] * 5,
+        out_specs=[vmem] * 3,
+        out_shape=[flat, flat, jax.ShapeDtypeStruct(kv_panel.shape, BF16)],
+        cost_estimate=pl.CostEstimate(flops=1 << 24, bytes_accessed=1 << 22, transcendentals=rows * channels),
+        compiler_params=pltpu.CompilerParams(vmem_limit_bytes=4 << 20),
+        name="ready",
+    )(h, p, y, kv_panel, kv_scale)
+
+
+def mix_call(hg, pg, weight, ends, near, past):
+    rows, channels = hg.shape
+    out = weight.shape[1]
     width = MIX_GROUPS * SCALE_ROWS
-    col = lambda b: (0, b)
-    out = kv_panel.shape[1]
-    pair = pl.BlockSpec((2, width), col)
+    vmem = pl.BlockSpec(memory_space=pltpu.VMEM)
     return pl.pallas_call(
         functools.partial(mix_kernel, len(past)),
-        grid=(channels // width,),
-        in_specs=[
-            pl.BlockSpec((width // 128, rows, 128), lambda b: (b, 0, 0)),
-            pl.BlockSpec((width // 128, rows, 128), lambda b: (b, 0, 0)),
-            pl.BlockSpec((2, SEGS, width), lambda b: (0, 0, b)),
-        ]
-        + [pair] * (1 + len(past))
-        + [
-            pl.BlockSpec((rows, width), col),
-            pl.BlockSpec((width, out), lambda b: (b, 0)),
-            pl.BlockSpec(kv_scale.shape, lambda b: (0, 0)),
+        in_specs=[vmem] * (5 + len(past)),
+        out_specs=[pl.BlockSpec(memory_space=pl.ANY), vmem],
+        out_shape=[jax.ShapeDtypeStruct((rows, channels), BF16), jax.ShapeDtypeStruct((rows, out), F32)],
+        scratch_shapes=[
+            pltpu.VMEM((channels // width, rows, width), BF16),
+            pltpu.SemaphoreType.DMA((channels // width,)),
         ],
-        out_specs=[pl.BlockSpec((rows, width), col), pl.BlockSpec((rows, out), lambda b: (0, 0))],
-        out_shape=[jax.ShapeDtypeStruct((rows, channels), BF16), jax.ShapeDtypeStruct((rows, out), F32)],
-        scratch_shapes=[pltpu.VMEM((SEGS, width), F32)],
-        compiler_params=pltpu.CompilerParams(vmem_limit_bytes=20 << 20),
+        compiler_params=pltpu.CompilerParams(vmem_limit_bytes=8 << 20),
         name="mix",
-    )(h, p, ends, near, *past, y, kv_panel, kv_scale)
+    )(hg, pg, weight, ends, near, *past)
 
 
 def sum_call(a, b):
@@ -652,10 +753,11 @@
         stay(decay_rate[None]),
     )
     near = swap(tot)
+    hg, pg, weight = ready_call(h, p, branch_y, kv_panel, kv_scale)
     level = level_call(tot, near)
     levels = -(-(seq // 2) // (2 * rows))
     past = [ring(level, 2 * k) for k in range(1, levels + 1)]
-    mixed, partial_kv = mix_call(h, p, ends, near, past, branch_y, kv_panel, kv_scale)
+    mixed, partial_kv = mix_call(hg, pg, weight, ends, near, past)
     own, half = sum_call(partial_kv, partner(partial_kv))
 
     levels = -(-WINDOW // rows) // 2

time: 95.3 us -> 92.9 us (0.975)
  waiting for transfers between devices: 14.6 us -> 11.9 us
    ppermute x5, waiting for transfers between devices: 10 us -> 7.3 us  [ring(): return lax.ppermute(x, 'tm', [(i, (i + lag) % n) for i in range(n)])]
    pallas_call x2 -> x3, Pallas kernels: 16.5 us -> 17 us  [the longest x1 11.5 us: recur_call(): pl.pallas_call(recur_kernel, in_specs=[pl.BlockSpec(memory_space=pltpu.SM...]
  transfers between devices with their start and end apart: 15 -> 15, of which waited for: 6 -> 4; matrix products, arithmetic and copies ran while one was open for 1% -> 1% of each run, Pallas kernels for 36% -> 40%
where the time goes in v5:
time: 92.9 us; the launch traced here: 92.6 us
  Pallas kernels  62.5 us (67%)
  starting transfers between devices  15.7 us (17%)
  waiting for transfers between devices  11.9 us (13%)
    pallas_call x4, Pallas kernels, attend_call(): pl.pallas_call(functools.partial(attend_kernel, own is not None, lags, fi...  45.3 us
    pallas_call x1, Pallas kernels, recur_call(): pl.pallas_call(recur_kernel, in_specs=[pl.BlockSpec(memory_space=pltpu.SM...  11.5 us
    ppermute x5, waiting for transfers between devices, ring(): return lax.ppermute(x, 'tm', [(i, (i + lag) % n) for i in range(n)])  7.3 us
    ppermute x6, starting transfers between devices, partner(): return lax.ppermute(x, 'mp', [(0, 1), (1, 0)])  6.91 us
    ppermute x5, starting transfers between devices, ring(): return lax.ppermute(x, 'tm', [(i, (i + lag) % n) for i in range(n)])  6.6 us
    pallas_call x1, Pallas kernels, ready_call(): pl.pallas_call(ready_kernel, in_specs=[vmem] * 5, out_specs=[vmem] * 3, o...  2.92 us
    pallas_call x1, Pallas kernels, mix_call(): pl.pallas_call(functools.partial(mix_kernel, len(past)), in_specs=[vmem]...  2.6 us
    ppermute x6, waiting for transfers between devices, partner(): return lax.ppermute(x, 'mp', [(0, 1), (1, 0)])  2.3 us
  transfers between devices with their start and end apart: 15, of which 4 were waited for; matrix products, arithmetic and copies ran while one was open for 1% of the time, Pallas kernels for 40%

profile of v5, /device:TPU:17, one launch (start us, length us, event | category | flops | bytes accessed | tf_op | source)
XLA Modules:
  0.0 92.6 jit_solution(8173967472921410586)
XLA Ops:
  0.6 0.8 slice.3
  1.4 1.3 %collective-permute-start = (bf16[3,2048]{1,0:T(4,128)(2,1)S(1)}, bf16[3,2048]{1,0:T(4,128)(2,1)S(1)}, u32[]{:S(2)}, u32[]{:S(2)}) collective-permute-start(bf16[3,2048]{1,0:T(4,128)(2,1)S(1)} %slice.3), channel_id=1, source_target_pairs={{0,2},{2,4},{4,6},{6,8},{8,10},{10,12},{12,14},{14,0},{1,3},{3,5},... | collective-permute-start | bytes 36872 | tf_op jit(solution)/shard_map/ppermute | solution.py:30
  2.7 0.9 convert_reduce_fusion.starts_ref
  3.6 1.4 %collective-permute-done.halo_all = bf16[3,2048]{1,0:T(4,128)(2,1)S(1)} collective-permute-done((bf16[3,2048]{1,0:T(4,128)(2,1)S(1)}, bf16[3,2048]{1,0:T(4,128)(2,1)S(1)}, u32[]{:S(2)}, u32[]{:S(2)}) %collective-permute-start) | collective-permute-done | bytes 12320 | tf_op jit(solution)/shard_map/ppermute | solution.py:30
  5.0 11.5 %recur.1 = (f32[16,512,128]{2,1,0:T(8,128)S(1)}, f32[16,512,128]{2,1,0:T(8,128)S(1)}, f32[2,8,2048]{2,1,0:T(8,128)S(1)}, f32[2,2048]{1,0:T(2,128)S(1)}) custom-call(s32[4]{0:T(128)S(1)} %convert_reduce_fusion.starts_ref, bf16[512,2048]{1,0:T(8,128)(2,1)} %x_hbm.1, bf16[3,2048]{1,0:T(4,128)(2,1)S(1)} %collective-permute-done.halo_all, f32[4,2048]{1,0:T(4,128)} %cw_hbm.1, ...), custom_call_target="tpu_custom_call" | custom-call | tf_op jit(solution)/shard_map/recur/pallas_call | solution.py:595
  16.4 0.4 collective-permute-start.1
  16.9 2.2 %collective-permute-done.1.near_ref = f32[2,2048]{1,0:T(2,128)S(1)} collective-permute-done((f32[2,2048]{1,0:T(2,128)S(1)}, f32[2,2048]{1,0:T(2,128)S(1)}, u32[]{:S(2)}, u32[]{:S(2)}) %collective-permute-start.1) | collective-permute-done | bytes 16416 | tf_op jit(solution)/shard_map/ppermute | solution.py:35
  19.1 1.3 %collective-permute-start.2 = (f32[2,2048]{1,0:T(2,128)S(1)}, f32[2,2048]{1,0:T(2,128)S(1)}, u32[]{:S(2)}, u32[]{:S(2)}) collective-permute-start(f32[2,2048]{1,0:T(2,128)S(1)} %level.1), channel_id=1, source_target_pairs={{0,4},{2,6},{4,8},{6,10},{8,12},{10,14},{12,0},{14,2},{1,5},{3,7},... | collective-permute-start | bytes 49160 | tf_op jit(solution)/shard_map/ppermute | solution.py:30
  20.5 0.8 collective-permute-start.3
  21.2 2.9 %ready.1 = (f32[512,2048]{1,0:T(8,128)S(1)}, f32[512,2048]{1,0:T(8,128)S(1)}, bf16[2048,512]{1,0:T(8,128)(2,1)S(1)}) custom-call(f32[16,512,128]{2,1,0:T(8,128)S(1)} %get-tuple-element.22.h_ref, f32[16,512,128]{2,1,0:T(8,128)S(1)} %get-tuple-element.23.p_ref, bf16[512,2048]{1,0:T(8,128)(2,1)S(1)} %copy-done.1, bf16[2048,512]{1,0:T(8,128)(2,1)S(1)} %copy-done.2, ...), custom_call_target="tpu_custom_call" | custom-call | flops 16777216 | bytes 4194304 | tf_op jit(solution)/shard_map/ready/pallas_call | solution.py:633
  24.2 2.6 %mix.1 = (bf16[512,2048]{1,0:T(8,128)(2,1)}, f32[512,512]{1,0:T(8,128)S(1)}) custom-call(f32[512,2048]{1,0:T(8,128)S(1)} %get-tuple-element.24.hg_ref, f32[512,2048]{1,0:T(8,128)S(1)} %get-tuple-element.25.pg_ref, bf16[2048,512]{1,0:T(8,128)(2,1)S(1)} %get-tuple-element.26.w_ref, f32[2,8,2048]{2,1,0:T(8,128)S(1)} %get-tuple-element.27.ends_ref, ...), custom_call_target="tpu_custom_call" | custom-call | tf_op jit(solution)/shard_map/mix/pallas_call | solution.py:649
  26.8 4.2 %collective-permute-start.4 = (f32[512,512]{1,0:T(8,128)S(1)}, f32[512,512]{1,0:T(8,128)S(1)}, u32[]{:S(2)}, u32[]{:S(2)}) collective-permute-start(f32[512,512]{1,0:T(8,128)S(1)} %get-tuple-element.30.a_ref), channel_id=1, source_target_pairs={{0,1},{1,0},{2,3},{3,2},{4,5},{5,4},{6,7},{7,6},{8,9},{9,8},{10,11... | collective-permute-start | bytes 3145736 | tf_op jit(solution)/shard_map/ppermute | solution.py:39
  31.1 2.3 %collective-permute-done.4.b_ref = f32[512,512]{1,0:T(8,128)S(1)} collective-permute-done((f32[512,512]{1,0:T(8,128)S(1)}, f32[512,512]{1,0:T(8,128)S(1)}, u32[]{:S(2)}, u32[]{:S(2)}) %collective-permute-start.4) | collective-permute-done | bytes 1048608 | tf_op jit(solution)/shard_map/ppermute | solution.py:39
  33.5 1.6 %collective-permute-start.5 = (bf16[512,256]{1,0:T(8,128)(2,1)S(1)}, bf16[512,256]{1,0:T(8,128)(2,1)S(1)}, u32[]{:S(2)}, u32[]{:S(2)}) collective-permute-start(bf16[512,256]{1,0:T(8,128)(2,1)S(1)} %get-tuple-element.31), channel_id=1, source_target_pairs={{0,4},{2,6},{4,8},{6,10},{8,12},{10,14},{12,0},{14,2},{1,5},{3,7},... | collective-permute-start | bytes 786440 | tf_op jit(solution)/shard_map/ppermute | solution.py:30
  35.2 5.9 %collective-permute-done.5.refs_2_ = bf16[512,256]{1,0:T(8,128)(2,1)S(1)} collective-permute-done((bf16[512,256]{1,0:T(8,128)(2,1)S(1)}, bf16[512,256]{1,0:T(8,128)(2,1)S(1)}, u32[]{:S(2)}, u32[]{:S(2)}) %collective-permute-start.5) | collective-permute-done | bytes 262176 | tf_op jit(solution)/shard_map/ppermute | solution.py:30
  41.1 1.6 %collective-permute-start.6 = (bf16[512,256]{1,0:T(8,128)(2,1)S(1)}, bf16[512,256]{1,0:T(8,128)(2,1)S(1)}, u32[]{:S(2)}, u32[]{:S(2)}) collective-permute-start(bf16[512,256]{1,0:T(8,128)(2,1)S(1)} %collective-permute-done.5.refs_2_), channel_id=1, source_target_pairs={{0,4},{2,6},{4,8},{6,10},{8,12},{10,14},{12,0},{14,2},{1,5},{3,7},... | collective-permute-start | bytes 786440 | tf_op jit(solution)/shard_map/ppermute | solution.py:30
  42.7 1.5 %collective-permute-start.13 = (bf16[512,256]{1,0:T(8,128)(2,1)S(1)}, bf16[512,256]{1,0:T(8,128)(2,1)S(1)}, u32[]{:S(2)}, u32[]{:S(2)}) collective-permute-start(bf16[512,256]{1,0:T(8,128)(2,1)S(1)} %collective-permute-done.12.refs_0_), channel_id=1, source_target_pairs={{0,1},{1,0},{2,3},{3,2},{4,5},{5,4},{6,7},{7,6},{8,9},{9,8},{10,11... | collective-permute-start | bytes 786440 | tf_op jit(solution)/shard_map/ppermute | solution.py:39
  44.3 6.2 %attend_own.1 = (f32[512,2048]{1,0:T(8,128)S(1)}, f32[512,1024]{1,0:T(8,128)S(1)}, f32[512,1024]{1,0:T(8,128)S(1)}) custom-call(s32[4]{0:T(128)S(1)} %convert_reduce_fusion.starts_ref, bf16[512,2048]{1,0:T(8,128)(2,1)S(1)} %copy-done, bf16[2,512,256]{2,1,0:T(8,128)(2,1)S(1)} %get-tuple-element.32.refs_0_), custom_call_target="tpu_custom_call" | custom-call | flops 2147483648 | bytes 4194304 | tf_op jit(solution)/shard_map/attend_own/pallas_call | solution.py:706
  50.5 0.5 collective-permute-start.11
  51.0 1.7 %collective-permute-start.7 = (bf16[512,256]{1,0:T(8,128)(2,1)S(1)}, bf16[512,256]{1,0:T(8,128)(2,1)S(1)}, u32[]{:S(2)}, u32[]{:S(2)}) collective-permute-start(bf16[512,256]{1,0:T(8,128)(2,1)S(1)} %collective-permute-done.6.refs_2_), channel_id=1, source_target_pairs={{0,2},{2,0},{4,6},{6,4},{8,10},{10,8},{12,14},{14,12},{1,3},{3,1},... | collective-permute-start | bytes 786440 | tf_op jit(solution)/shard_map/ppermute | solution.py:35
  52.7 0.4 collective-permute-start.10
  53.1 10.5 %attend_mid.2 = (f32[512,2048]{1,0:T(8,128)S(1)}, f32[512,1024]{1,0:T(8,128)S(1)}, f32[512,1024]{1,0:T(8,128)S(1)}) custom-call(s32[4]{0:T(128)S(1)} %convert_reduce_fusion.starts_ref, bf16[512,2048]{1,0:T(8,128)(2,1)S(1)} %copy-done, ...), custom_call_target="tpu_custom_call", output_to_operand_aliasing={{0}: (6, {}), {1}: (7, {}), {2}: (8, {})} | custom-call | flops 4294967296 | bytes 4194304 | tf_op jit(solution)/shard_map/attend_mid/pallas_call | solution.py:706
  63.8 17.7 %attend_mid.3 = (f32[512,2048]{1,0:T(8,128)S(1)}, f32[512,1024]{1,0:T(8,128)S(1)}, f32[512,1024]{1,0:T(8,128)S(1)}) custom-call(s32[4]{0:T(128)S(1)} %convert_reduce_fusion.starts_ref, bf16[512,2048]{1,0:T(8,128)(2,1)S(1)} %copy-done, ...), custom_call_target="tpu_custom_call", output_to_operand_aliasing={{0}: (6, {}), {1}: (7, {}), {2}: (8, {})} | custom-call | flops 4294967296 | bytes 4194304 | tf_op jit(solution)/shard_map/attend_mid/pallas_call | solution.py:706
  81.5 10.9 %attend_end.1 = bf16[512,2048]{1,0:T(8,128)(2,1)} custom-call(s32[4]{0:T(128)S(1)} %convert_reduce_fusion.starts_ref, bf16[512,2048]{1,0:T(8,128)(2,1)S(1)} %copy-done, bf16[512,256]{1,0:T(8,128)(2,1)S(1)} %collective-permute-done.7.refs_0_, bf16[512,256]{1,0:T(8,128)(2,1)S(1)} %collective-permute-done.8.refs_1_, f32[512,2048]{1,0:T(8,128)S(1)} %get-tuple-element.39.refs_2_, ...), custom_call_target="tpu_custom_call" | custom-call | flops 2147483648 | bytes 4194304 | tf_op jit(solution)/shard_map/attend_end/pallas_call | solution.py:706
  (25 shorter events, 0.5 us)
Async XLA Ops:
  1.4 3.5 %collective-permute-start = (bf16[3,2048]{1,0:T(4,128)(2,1)S(1)}, bf16[3,2048]{1,0:T(4,128)(2,1)S(1)}, u32[]{:S(2)}, u32[]{:S(2)}) collective-permute-start(bf16[3,2048]{1,0:T(4,128)(2,1)S(1)} %slice.3), channel_id=1, source_target_pairs={{0,2},{2,4},{4,6},{6,8},{8,10},{10,12},{12,14},{14,0},{1,3},{3,5},... | collective-permute-start | bytes 36872 | tf_op jit(solution)/shard_map/ppermute | solution.py:30
  4.9 16.3 %copy-start.1 = (bf16[512,2048]{1,0:T(8,128)(2,1)S(1)}, bf16[512,2048]{1,0:T(8,128)(2,1)}, u32[]{:S(2)}) copy-start(bf16[512,2048]{1,0:T(8,128)(2,1)} %y_ref.1) | copy-start | bytes 6291460
  4.9 16.3 %copy-start.2 = (bf16[2048,512]{1,0:T(8,128)(2,1)S(1)}, bf16[2048,512]{1,0:T(8,128)(2,1)}, u32[]{:S(2)}) copy-start(bf16[2048,512]{1,0:T(8,128)(2,1)} %panel_ref.1) | copy-start | bytes 6291460
  4.9 16.3 %copy-start.3 = (f32[16,512]{1,0:T(8,128)S(1)}, f32[16,512]{1,0:T(8,128)}, u32[]{:S(2)}) copy-start(f32[16,512]{1,0:T(8,128)} %scale_ref.1) | copy-start | bytes 98308
  16.4 2.7 %collective-permute-start.1 = (f32[2,2048]{1,0:T(2,128)S(1)}, f32[2,2048]{1,0:T(2,128)S(1)}, u32[]{:S(2)}, u32[]{:S(2)}) collective-permute-start(f32[2,2048]{1,0:T(2,128)S(1)} %get-tuple-element.28.tot_ref), channel_id=1, source_target_pairs={{0,2},{2,0},{4,6},{6,4},{8,10},{10,8},{12,14},{14,12},{1,3},{3,1},... | collective-permute-start | bytes 49160 | tf_op jit(solution)/shard_map/ppermute | solution.py:35
  19.1 5.0 %collective-permute-start.2 = (f32[2,2048]{1,0:T(2,128)S(1)}, f32[2,2048]{1,0:T(2,128)S(1)}, u32[]{:S(2)}, u32[]{:S(2)}) collective-permute-start(f32[2,2048]{1,0:T(2,128)S(1)} %level.1), channel_id=1, source_target_pairs={{0,4},{2,6},{4,8},{6,10},{8,12},{10,14},{12,0},{14,2},{1,5},{3,7},... | collective-permute-start | bytes 49160 | tf_op jit(solution)/shard_map/ppermute | solution.py:30
  20.5 3.7 %collective-permute-start.3 = (f32[2,2048]{1,0:T(2,128)S(1)}, f32[2,2048]{1,0:T(2,128)S(1)}, u32[]{:S(2)}, u32[]{:S(2)}) collective-permute-start(f32[2,2048]{1,0:T(2,128)S(1)} %level.1), channel_id=1, source_target_pairs={{0,8},{2,10},{4,12},{6,14},{8,0},{10,2},{12,4},{14,6},{1,9},{3,11}... | collective-permute-start | bytes 49160 | tf_op jit(solution)/shard_map/ppermute | solution.py:30
  26.8 17.5 %copy-start = (bf16[512,2048]{1,0:T(8,128)(2,1)S(1)}, bf16[512,2048]{1,0:T(8,128)(2,1)}, u32[]{:S(2)}) copy-start(bf16[512,2048]{1,0:T(8,128)(2,1)} %q_ref.7) | copy-start | bytes 6291460
  26.8 6.5 %collective-permute-start.4 = (f32[512,512]{1,0:T(8,128)S(1)}, f32[512,512]{1,0:T(8,128)S(1)}, u32[]{:S(2)}, u32[]{:S(2)}) collective-permute-start(f32[512,512]{1,0:T(8,128)S(1)} %get-tuple-element.30.a_ref), channel_id=1, source_target_pairs={{0,1},{1,0},{2,3},{3,2},{4,5},{5,4},{6,7},{7,6},{8,9},{9,8},{10,11... | collective-permute-start | bytes 3145736 | tf_op jit(solution)/shard_map/ppermute | solution.py:39
  33.5 7.5 %collective-permute-start.5 = (bf16[512,256]{1,0:T(8,128)(2,1)S(1)}, bf16[512,256]{1,0:T(8,128)(2,1)S(1)}, u32[]{:S(2)}, u32[]{:S(2)}) collective-permute-start(bf16[512,256]{1,0:T(8,128)(2,1)S(1)} %get-tuple-element.31), channel_id=1, source_target_pairs={{0,4},{2,6},{4,8},{6,10},{8,12},{10,14},{12,0},{14,2},{1,5},{3,7},... | collective-permute-start | bytes 786440 | tf_op jit(solution)/shard_map/ppermute | solution.py:30
  35.2 7.5 %collective-permute-start.12 = (bf16[512,256]{1,0:T(8,128)(2,1)S(1)}, bf16[512,256]{1,0:T(8,128)(2,1)S(1)}, u32[]{:S(2)}, u32[]{:S(2)}) collective-permute-start(bf16[512,256]{1,0:T(8,128)(2,1)S(1)} %get-tuple-element.31), channel_id=1, source_target_pairs={{0,2},{2,0},{4,6},{6,4},{8,10},{10,8},{12,14},{14,12},{1,3},{3,1},... | collective-permute-start | bytes 786440 | tf_op jit(solution)/shard_map/ppermute | solution.py:35
  41.1 9.4 %collective-permute-start.6 = (bf16[512,256]{1,0:T(8,128)(2,1)S(1)}, bf16[512,256]{1,0:T(8,128)(2,1)S(1)}, u32[]{:S(2)}, u32[]{:S(2)}) collective-permute-start(bf16[512,256]{1,0:T(8,128)(2,1)S(1)} %collective-permute-done.5.refs_2_), channel_id=1, source_target_pairs={{0,4},{2,6},{4,8},{6,10},{8,12},{10,14},{12,0},{14,2},{1,5},{3,7},... | collective-permute-start | bytes 786440 | tf_op jit(solution)/shard_map/ppermute | solution.py:30
  42.7 10.0 %collective-permute-start.9 = (bf16[512,256]{1,0:T(8,128)(2,1)S(1)}, bf16[512,256]{1,0:T(8,128)(2,1)S(1)}, u32[]{:S(2)}, u32[]{:S(2)}) collective-permute-start(bf16[512,256]{1,0:T(8,128)(2,1)S(1)} %collective-permute-done.5.refs_2_), channel_id=1, source_target_pairs={{0,2},{2,0},{4,6},{6,4},{8,10},{10,8},{12,14},{14,12},{1,3},{3,1},... | collective-permute-start | bytes 786440 | tf_op jit(solution)/shard_map/ppermute | solution.py:35
  42.7 10.4 %collective-permute-start.13 = (bf16[512,256]{1,0:T(8,128)(2,1)S(1)}, bf16[512,256]{1,0:T(8,128)(2,1)S(1)}, u32[]{:S(2)}, u32[]{:S(2)}) collective-permute-start(bf16[512,256]{1,0:T(8,128)(2,1)S(1)} %collective-permute-done.12.refs_0_), channel_id=1, source_target_pairs={{0,1},{1,0},{2,3},{3,2},{4,5},{5,4},{6,7},{7,6},{8,9},{9,8},{10,11... | collective-permute-start | bytes 786440 | tf_op jit(solution)/shard_map/ppermute | solution.py:39
  44.2 8.9 %collective-permute-start.14 = (bf16[512,256]{1,0:T(8,128)(2,1)S(1)}, bf16[512,256]{1,0:T(8,128)(2,1)S(1)}, u32[]{:S(2)}, u32[]{:S(2)}) collective-permute-start(bf16[512,256]{1,0:T(8,128)(2,1)S(1)} %collective-permute-done.5.refs_2_), channel_id=1, source_target_pairs={{0,1},{1,0},{2,3},{3,2},{4,5},{5,4},{6,7},{7,6},{8,9},{9,8},{10,11... | collective-permute-start | bytes 786440 | tf_op jit(solution)/shard_map/ppermute | solution.py:39
  50.5 13.4 %collective-permute-start.11 = (bf16[512,256]{1,0:T(8,128)(2,1)S(1)}, bf16[512,256]{1,0:T(8,128)(2,1)S(1)}, u32[]{:S(2)}, u32[]{:S(2)}) collective-permute-start(bf16[512,256]{1,0:T(8,128)(2,1)S(1)} %collective-permute-done.6.refs_2_), channel_id=1, source_target_pairs={{0,1},{1,0},{2,3},{3,2},{4,5},{5,4},{6,7},{7,6},{8,9},{9,8},{10,11... | collective-permute-start | bytes 786440 | tf_op jit(solution)/shard_map/ppermute | solution.py:39
  51.0 12.6 %collective-permute-start.7 = (bf16[512,256]{1,0:T(8,128)(2,1)S(1)}, bf16[512,256]{1,0:T(8,128)(2,1)S(1)}, u32[]{:S(2)}, u32[]{:S(2)}) collective-permute-start(bf16[512,256]{1,0:T(8,128)(2,1)S(1)} %collective-permute-done.6.refs_2_), channel_id=1, source_target_pairs={{0,2},{2,0},{4,6},{6,4},{8,10},{10,8},{12,14},{14,12},{1,3},{3,1},... | collective-permute-start | bytes 786440 | tf_op jit(solution)/shard_map/ppermute | solution.py:35
  52.7 11.1 %collective-permute-start.10 = (bf16[512,256]{1,0:T(8,128)(2,1)S(1)}, bf16[512,256]{1,0:T(8,128)(2,1)S(1)}, u32[]{:S(2)}, u32[]{:S(2)}) collective-permute-start(bf16[512,256]{1,0:T(8,128)(2,1)S(1)} %collective-permute-done.9.refs_0_), channel_id=1, source_target_pairs={{0,1},{1,0},{2,3},{3,2},{4,5},{5,4},{6,7},{7,6},{8,9},{9,8},{10,11... | collective-permute-start | bytes 786440 | tf_op jit(solution)/shard_map/ppermute | solution.py:39
  63.6 17.9 %collective-permute-start.8 = (bf16[512,256]{1,0:T(8,128)(2,1)S(1)}, bf16[512,256]{1,0:T(8,128)(2,1)S(1)}, u32[]{:S(2)}, u32[]{:S(2)}) collective-permute-start(bf16[512,256]{1,0:T(8,128)(2,1)S(1)} %collective-permute-done.7.refs_0_), channel_id=1, source_target_pairs={{0,1},{1,0},{2,3},{3,2},{4,5},{5,4},{6,7},{7,6},{8,9},{9,8},{10,11... | collective-permute-start | bytes 786440 | tf_op jit(solution)/shard_map/ppermute | solution.py:39

commit v6 on v5

--- a/solution.py
+++ b/solution.py
@@ -17,10 +17,16 @@
 SEGS = 8
 MIX_GROUPS = 4
 GROUP = 2
+CHUNK = 16
 HIST = 4
 LOG2E = 1.4426950408889634
 LN2 = 0.6931471805599453
-SINH = [-0.5 * LN2 ** (2 * k + 1) / math.factorial(2 * k + 1) for k in range(4)]
+SPAN = 0.16
+SINH = [
+    -0.5 * LN2 * (1.0 + SPAN**3 / (32 * 5040)),
+    -0.5 * LN2**3 * (1.0 / 6 - 9 * SPAN**2 / (16 * 5040)),
+    -0.5 * LN2**5 * (1.0 / 120 + 1.5 * SPAN / 5040),
+]
 F32 = jnp.float32
 BF16 = jnp.bfloat16
 
@@ -110,6 +116,13 @@
     for copy in smalls:
         copy.wait()
 
+    def hit(k):
+        found = False
+        for d in range(DOCS):
+            off = starts_ref[d] - base
+            found = found | ((off >= 0) & (off < rows) & ((off % seg_len) // CHUNK == k))
+        return found
+
     def block(b, z):
         fetch_x(b).wait()
         fetch_panel(b).wait()
@@ -121,6 +134,7 @@
 
         wide = pl.ds(pl.multiple_of(b * width, width), width)
         recur_block(
+            hit,
             b,
             x_buf.at[b % 2],
             halo_all.at[:, wide],
@@ -145,6 +159,7 @@
 
 
 def recur_block(
+    hit,
     b,
     x_ref,
     halo_ref,
@@ -188,30 +203,39 @@
     w = [jnp.broadcast_to(cw_ref[j : j + 1, :], (SEGS, width)) for j in range(CONV)]
     bias = jnp.broadcast_to(cb_ref[...], (SEGS, width))
 
-    def conv_step(i, carry):
-        a, b, c = carry
+    def chunked(step, carry):
+        def chunk(masked, k, carry):
+            for u in range(CHUNK // 2):
+                carry = step(k * (CHUNK // 2) + u, carry, masked)
+            return carry
+
+        def body(k, carry):
+            return lax.cond(hit(k), functools.partial(chunk, True), functools.partial(chunk, False), k, carry)
+
+        return lax.fori_loop(0, seg_len // CHUNK, body, carry)
+
+    def conv_step(i, carry, masked):
+        ka, kb, kc = carry
         x = row(i)
-        m = mask(i)
-        d = w[0] * x + m * c + bias
-        c = w[1] * x + m * b
-        b = w[2] * x + m * a
-        a = w[3] * x
-        return (a, b, c), d
+        if masked:
+            m = mask(i)
+            ka, kb, kc = m * ka, m * kb, m * kc
+        return (w[3] * x, w[2] * x + ka, w[1] * x + kb), w[0] * x + kc + bias
 
     x3, x2, x1 = row(-3), row(-2), row(-1)
     a1 = w[3] * x1
     b1 = w[2] * x1 + mask(-1) * (w[3] * x2)
     c1 = w[1] * x1 + mask(-1) * (w[2] * x2 + mask(-2) * (w[3] * x3))
 
-    def conv_pair(k, carry):
-        carry, d0 = conv_step(2 * k, carry)
-        carry, d1 = conv_step(2 * k + 1, carry)
+    def conv_pair(k, carry, masked):
+        carry, d0 = conv_step(2 * k, carry, masked)
+        carry, d1 = conv_step(2 * k + 1, carry, masked)
         d = jnp.concatenate([d0, d1], 0).astype(BF16)
         for c in range(width // 128):
             co[c, pl.ds(pl.multiple_of(k * 2 * SEGS, 2 * SEGS), 2 * SEGS), :] = d[:, c * 128 : (c + 1) * 128]
         return carry
 
-    lax.fori_loop(0, seg_len // 2, conv_pair, (a1, b1, c1), unroll=8)
+    chunked(conv_pair, (a1, b1, c1))
 
     weight = dequantized(panel, scale) * BF16(0.5)
     conv_out = jnp.concatenate([co[c] for c in range(width // 128)], 1)
@@ -221,19 +245,20 @@
     bias_i = jnp.broadcast_to(gb_ref[1:2, :] * 0.5, (SEGS, width))
     rate4 = jnp.broadcast_to(rate_ref[...] * (-4.0 * LOG2E), (SEGS, width))
 
-    def scan_step(i, conv, carry):
+    def scan_step(i, conv, carry, masked):
         h, p = carry
         at = pl.ds(pl.multiple_of(i * SEGS, SEGS), SEGS)
-        m = mask(i)
         v = rate4 * (1.0 + jnp.tanh(gate[at, :width] + bias_r))
         ti = 1.0 + jnp.tanh(gate[at, width:] + bias_i)
         decay = jnp.exp2(v)
         s = v * v
-        series = ((s * SINH[3] + SINH[2]) * s + SINH[1]) * s + SINH[0]
+        series = (s * SINH[2] + SINH[1]) * s + SINH[0]
         quarter = decay * (v * series)
         half = quarter * lax.rsqrt(jnp.maximum(quarter, 1e-37))
-        half = jnp.where(m > 0.0, half, 0.5)
-        decay = decay * m
+        if masked:
+            m = mask(i)
+            half = jnp.where(m > 0.0, half, 0.5)
+            decay = decay * m
         h = decay * h + ti * (conv * half)
         p = p * decay
         for c in range(width // 128):
@@ -241,19 +266,13 @@
             p_ref[b * (width // 128) + c, at, :] = p[:, c * 128 : (c + 1) * 128]
         return h, p
 
-    def scan_pair(k, carry):
+    def scan_pair(k, carry, masked):
         at = pl.ds(pl.multiple_of(k * 2 * SEGS, 2 * SEGS), 2 * SEGS)
         conv = jnp.concatenate([co[c, at, :].astype(F32) for c in range(width // 128)], 1)
-        carry = scan_step(2 * k, conv[:SEGS], carry)
-        return scan_step(2 * k + 1, conv[SEGS:], carry)
-
-    h, p = lax.fori_loop(
-        0,
-        seg_len // 2,
-        scan_pair,
-        (jnp.zeros((SEGS, width), F32), jnp.ones((SEGS, width), F32)),
-        unroll=8,
-    )
+        carry = scan_step(2 * k, conv[:SEGS], carry, masked)
+        return scan_step(2 * k + 1, conv[SEGS:], carry, masked)
+
+    h, p = chunked(scan_pair, (jnp.zeros((SEGS, width), F32), jnp.ones((SEGS, width), F32)))
     ends_ref[0] = p
     ends_ref[1] = h
     tp, th = p[0:1], h[0:1]
@@ -361,7 +380,7 @@
     low, score, top = take(3)
     if final:
         acc, m_ref, l_ref, stage, sems = take(5)
-    prob, l_new = (None, None) if own else take(2)
+    prob, l_new, flag = (None, None, None) if own else take(3)
     rows = q_ref.shape[0]
     half = rows // 2
     me = lax.axis_index("tm")
@@ -528,10 +547,14 @@
         start_up()
         l_new[...] = prev[2][...]
         loop(exp_all)
-
-    within = jnp.max(l_new[...]) <= 2.0**64
-    fast = any_live & within
-    slow = any_live & jnp.logical_not(within)
+        flag[0] = jnp.where(jnp.max(l_new[...]) <= 2.0**64, 1, 0)
+
+    @pl.when(jnp.logical_not(any_live))
+    def _():
+        flag[0] = 2
+
+    fast = flag[0] == 1
+    slow = flag[0] == 0
 
     if not final:
 
@@ -697,6 +720,7 @@
         scratch += [
             pltpu.VMEM((tiles, heads, rows // 128, rows, 128), BF16),
             pltpu.VMEM((rows, heads * 128), F32),
+            pltpu.SMEM((1,), jnp.int32),
         ]
     if not final:
         out_specs = [vmem] * 3

time: 92.9 us -> 95.3 us (1.026)
  Pallas kernels: 62.5 us -> 64.7 us
    pallas_call x1, Pallas kernels: 11.5 us -> 13.7 us  [recur_call(): pl.pallas_call(recur_kernel, in_specs=[pl.BlockSpec(memory_space=pltpu.SM...]
  transfers between devices with their start and end apart: 15 -> 15, of which waited for: 4 -> 4; matrix products, arithmetic and copies ran while one was open for 1% -> 1% of each run, Pallas kernels for 40% -> 39%
where the time goes in v6:
time: 95.3 us; the launch traced here: 95 us
  Pallas kernels  64.7 us (68%)
  starting transfers between devices  15.7 us (16%)
  waiting for transfers between devices  12 us (13%)
    pallas_call x4, Pallas kernels, attend_call(): pl.pallas_call(functools.partial(attend_kernel, own is not None, lags, fi...  45.3 us
    pallas_call x1, Pallas kernels, recur_call(): pl.pallas_call(recur_kernel, in_specs=[pl.BlockSpec(memory_space=pltpu.SM...  13.7 us
    ppermute x5, waiting for transfers between devices, ring(): return lax.ppermute(x, 'tm', [(i, (i + lag) % n) for i in range(n)])  7.29 us
    ppermute x5, starting transfers between devices, ring(): return lax.ppermute(x, 'tm', [(i, (i + lag) % n) for i in range(n)])  6.99 us
    ppermute x6, starting transfers between devices, partner(): return lax.ppermute(x, 'mp', [(0, 1), (1, 0)])  6.74 us
    pallas_call x1, Pallas kernels, ready_call(): pl.pallas_call(ready_kernel, in_specs=[vmem] * 5, out_specs=[vmem] * 3, o...  2.92 us
    pallas_call x1, Pallas kernels, mix_call(): pl.pallas_call(functools.partial(mix_kernel, len(past)), in_specs=[vmem]...  2.6 us
    ppermute x4, waiting for transfers between devices, swap(): return lax.ppermute(x, 'tm', [(i, i ^ 1) for i in range(n)])  2.44 us
  transfers between devices with their start and end apart: 15, of which 4 were waited for; matrix products, arithmetic and copies ran while one was open for 1% of the time, Pallas kernels for 39%

profile of v6, /device:TPU:17, one launch (start us, length us, event | category | flops | bytes accessed | tf_op | source)
XLA Modules:
  0.0 95.0 jit_solution(6372919021393699956)
XLA Ops:
  0.6 0.8 slice.3
  1.4 1.3 %collective-permute-start = (bf16[3,2048]{1,0:T(4,128)(2,1)S(1)}, bf16[3,2048]{1,0:T(4,128)(2,1)S(1)}, u32[]{:S(2)}, u32[]{:S(2)}) collective-permute-start(bf16[3,2048]{1,0:T(4,128)(2,1)S(1)} %slice.3), channel_id=1, source_target_pairs={{0,2},{2,4},{4,6},{6,8},{8,10},{10,12},{12,14},{14,0},{1,3},{3,5},... | collective-permute-start | bytes 36872 | tf_op jit(solution)/shard_map/ppermute | solution.py:36
  2.7 0.9 convert_reduce_fusion.starts_ref
  3.6 1.4 %collective-permute-done.halo_all = bf16[3,2048]{1,0:T(4,128)(2,1)S(1)} collective-permute-done((bf16[3,2048]{1,0:T(4,128)(2,1)S(1)}, bf16[3,2048]{1,0:T(4,128)(2,1)S(1)}, u32[]{:S(2)}, u32[]{:S(2)}) %collective-permute-start) | collective-permute-done | bytes 12320 | tf_op jit(solution)/shard_map/ppermute | solution.py:36
  5.0 13.7 %recur.1 = (f32[16,512,128]{2,1,0:T(8,128)S(1)}, f32[16,512,128]{2,1,0:T(8,128)S(1)}, f32[2,8,2048]{2,1,0:T(8,128)S(1)}, f32[2,2048]{1,0:T(2,128)S(1)}) custom-call(s32[4]{0:T(128)S(1)} %convert_reduce_fusion.starts_ref, bf16[512,2048]{1,0:T(8,128)(2,1)} %x_hbm.1, bf16[3,2048]{1,0:T(4,128)(2,1)S(1)} %collective-permute-done.halo_all, f32[4,2048]{1,0:T(4,128)} %cw_hbm.1, ...), custom_call_target="tpu_custom_call" | custom-call | tf_op jit(solution)/shard_map/recur/pallas_call | solution.py:618
  18.6 0.2 collective-permute-start.1
  18.9 2.4 %collective-permute-done.1.near_ref = f32[2,2048]{1,0:T(2,128)S(1)} collective-permute-done((f32[2,2048]{1,0:T(2,128)S(1)}, f32[2,2048]{1,0:T(2,128)S(1)}, u32[]{:S(2)}, u32[]{:S(2)}) %collective-permute-start.1) | collective-permute-done | bytes 16416 | tf_op jit(solution)/shard_map/ppermute | solution.py:41
  21.3 1.3 %collective-permute-start.2 = (f32[2,2048]{1,0:T(2,128)S(1)}, f32[2,2048]{1,0:T(2,128)S(1)}, u32[]{:S(2)}, u32[]{:S(2)}) collective-permute-start(f32[2,2048]{1,0:T(2,128)S(1)} %level.1), channel_id=1, source_target_pairs={{0,4},{2,6},{4,8},{6,10},{8,12},{10,14},{12,0},{14,2},{1,5},{3,7},... | collective-permute-start | bytes 49160 | tf_op jit(solution)/shard_map/ppermute | solution.py:36
  22.6 0.9 collective-permute-start.3
  23.6 2.9 %ready.1 = (f32[512,2048]{1,0:T(8,128)S(1)}, f32[512,2048]{1,0:T(8,128)S(1)}, bf16[2048,512]{1,0:T(8,128)(2,1)S(1)}) custom-call(f32[16,512,128]{2,1,0:T(8,128)S(1)} %get-tuple-element.22.h_ref, f32[16,512,128]{2,1,0:T(8,128)S(1)} %get-tuple-element.23.p_ref, bf16[512,2048]{1,0:T(8,128)(2,1)S(1)} %copy-done.1, bf16[2048,512]{1,0:T(8,128)(2,1)S(1)} %copy-done.2, ...), custom_call_target="tpu_custom_call" | custom-call | flops 16777216 | bytes 4194304 | tf_op jit(solution)/shard_map/ready/pallas_call | solution.py:656
  26.5 2.6 %mix.1 = (bf16[512,2048]{1,0:T(8,128)(2,1)}, f32[512,512]{1,0:T(8,128)S(1)}) custom-call(f32[512,2048]{1,0:T(8,128)S(1)} %get-tuple-element.24.hg_ref, f32[512,2048]{1,0:T(8,128)S(1)} %get-tuple-element.25.pg_ref, bf16[2048,512]{1,0:T(8,128)(2,1)S(1)} %get-tuple-element.26.w_ref, f32[2,8,2048]{2,1,0:T(8,128)S(1)} %get-tuple-element.27.ends_ref, ...), custom_call_target="tpu_custom_call" | custom-call | tf_op jit(solution)/shard_map/mix/pallas_call | solution.py:672
  29.2 4.1 %collective-permute-start.4 = (f32[512,512]{1,0:T(8,128)S(1)}, f32[512,512]{1,0:T(8,128)S(1)}, u32[]{:S(2)}, u32[]{:S(2)}) collective-permute-start(f32[512,512]{1,0:T(8,128)S(1)} %get-tuple-element.30.a_ref), channel_id=1, source_target_pairs={{0,1},{1,0},{2,3},{3,2},{4,5},{5,4},{6,7},{7,6},{8,9},{9,8},{10,11... | collective-permute-start | bytes 3145736 | tf_op jit(solution)/shard_map/ppermute | solution.py:45
  33.2 2.3 %collective-permute-done.4.b_ref = f32[512,512]{1,0:T(8,128)S(1)} collective-permute-done((f32[512,512]{1,0:T(8,128)S(1)}, f32[512,512]{1,0:T(8,128)S(1)}, u32[]{:S(2)}, u32[]{:S(2)}) %collective-permute-start.4) | collective-permute-done | bytes 1048608 | tf_op jit(solution)/shard_map/ppermute | solution.py:45
  35.7 1.8 %collective-permute-start.5 = (bf16[512,256]{1,0:T(8,128)(2,1)S(1)}, bf16[512,256]{1,0:T(8,128)(2,1)S(1)}, u32[]{:S(2)}, u32[]{:S(2)}) collective-permute-start(bf16[512,256]{1,0:T(8,128)(2,1)S(1)} %get-tuple-element.31), channel_id=1, source_target_pairs={{0,4},{2,6},{4,8},{6,10},{8,12},{10,14},{12,0},{14,2},{1,5},{3,7},... | collective-permute-start | bytes 786440 | tf_op jit(solution)/shard_map/ppermute | solution.py:36
  37.5 5.9 %collective-permute-done.5.refs_2_ = bf16[512,256]{1,0:T(8,128)(2,1)S(1)} collective-permute-done((bf16[512,256]{1,0:T(8,128)(2,1)S(1)}, bf16[512,256]{1,0:T(8,128)(2,1)S(1)}, u32[]{:S(2)}, u32[]{:S(2)}) %collective-permute-start.5) | collective-permute-done | bytes 262176 | tf_op jit(solution)/shard_map/ppermute | solution.py:36
  43.4 1.6 %collective-permute-start.6 = (bf16[512,256]{1,0:T(8,128)(2,1)S(1)}, bf16[512,256]{1,0:T(8,128)(2,1)S(1)}, u32[]{:S(2)}, u32[]{:S(2)}) collective-permute-start(bf16[512,256]{1,0:T(8,128)(2,1)S(1)} %collective-permute-done.5.refs_2_), channel_id=1, source_target_pairs={{0,4},{2,6},{4,8},{6,10},{8,12},{10,14},{12,0},{14,2},{1,5},{3,7},... | collective-permute-start | bytes 786440 | tf_op jit(solution)/shard_map/ppermute | solution.py:36
  45.0 1.5 %collective-permute-start.13 = (bf16[512,256]{1,0:T(8,128)(2,1)S(1)}, bf16[512,256]{1,0:T(8,128)(2,1)S(1)}, u32[]{:S(2)}, u32[]{:S(2)}) collective-permute-start(bf16[512,256]{1,0:T(8,128)(2,1)S(1)} %collective-permute-done.12.refs_0_), channel_id=1, source_target_pairs={{0,1},{1,0},{2,3},{3,2},{4,5},{5,4},{6,7},{7,6},{8,9},{9,8},{10,11... | collective-permute-start | bytes 786440 | tf_op jit(solution)/shard_map/ppermute | solution.py:45
  46.6 6.2 %attend_own.1 = (f32[512,2048]{1,0:T(8,128)S(1)}, f32[512,1024]{1,0:T(8,128)S(1)}, f32[512,1024]{1,0:T(8,128)S(1)}) custom-call(s32[4]{0:T(128)S(1)} %convert_reduce_fusion.starts_ref, bf16[512,2048]{1,0:T(8,128)(2,1)S(1)} %copy-done, bf16[2,512,256]{2,1,0:T(8,128)(2,1)S(1)} %get-tuple-element.32.refs_0_), custom_call_target="tpu_custom_call" | custom-call | flops 2147483648 | bytes 4194304 | tf_op jit(solution)/shard_map/attend_own/pallas_call | solution.py:730
  52.8 0.5 collective-permute-start.11
  53.3 1.7 %collective-permute-start.7 = (bf16[512,256]{1,0:T(8,128)(2,1)S(1)}, bf16[512,256]{1,0:T(8,128)(2,1)S(1)}, u32[]{:S(2)}, u32[]{:S(2)}) collective-permute-start(bf16[512,256]{1,0:T(8,128)(2,1)S(1)} %collective-permute-done.6.refs_2_), channel_id=1, source_target_pairs={{0,2},{2,0},{4,6},{6,4},{8,10},{10,8},{12,14},{14,12},{1,3},{3,1},... | collective-permute-start | bytes 786440 | tf_op jit(solution)/shard_map/ppermute | solution.py:41
  55.1 0.4 collective-permute-start.10
  55.4 10.5 %attend_mid.2 = (f32[512,2048]{1,0:T(8,128)S(1)}, f32[512,1024]{1,0:T(8,128)S(1)}, f32[512,1024]{1,0:T(8,128)S(1)}) custom-call(s32[4]{0:T(128)S(1)} %convert_reduce_fusion.starts_ref, bf16[512,2048]{1,0:T(8,128)(2,1)S(1)} %copy-done, ...), custom_call_target="tpu_custom_call", output_to_operand_aliasing={{0}: (6, {}), {1}: (7, {}), {2}: (8, {})} | custom-call | flops 4294967296 | bytes 4194304 | tf_op jit(solution)/shard_map/attend_mid/pallas_call | solution.py:730
  66.2 17.7 %attend_mid.3 = (f32[512,2048]{1,0:T(8,128)S(1)}, f32[512,1024]{1,0:T(8,128)S(1)}, f32[512,1024]{1,0:T(8,128)S(1)}) custom-call(s32[4]{0:T(128)S(1)} %convert_reduce_fusion.starts_ref, bf16[512,2048]{1,0:T(8,128)(2,1)S(1)} %copy-done, ...), custom_call_target="tpu_custom_call", output_to_operand_aliasing={{0}: (6, {}), {1}: (7, {}), {2}: (8, {})} | custom-call | flops 4294967296 | bytes 4194304 | tf_op jit(solution)/shard_map/attend_mid/pallas_call | solution.py:730
  83.9 10.9 %attend_end.1 = bf16[512,2048]{1,0:T(8,128)(2,1)} custom-call(s32[4]{0:T(128)S(1)} %convert_reduce_fusion.starts_ref, bf16[512,2048]{1,0:T(8,128)(2,1)S(1)} %copy-done, bf16[512,256]{1,0:T(8,128)(2,1)S(1)} %collective-permute-done.7.refs_0_, bf16[512,256]{1,0:T(8,128)(2,1)S(1)} %collective-permute-done.8.refs_1_, f32[512,2048]{1,0:T(8,128)S(1)} %get-tuple-element.39.refs_2_, ...), custom_call_target="tpu_custom_call" | custom-call | flops 2147483648 | bytes 4194304 | tf_op jit(solution)/shard_map/attend_end/pallas_call | solution.py:730
  (25 shorter events, 0.5 us)
Async XLA Ops:
  1.4 3.5 %collective-permute-start = (bf16[3,2048]{1,0:T(4,128)(2,1)S(1)}, bf16[3,2048]{1,0:T(4,128)(2,1)S(1)}, u32[]{:S(2)}, u32[]{:S(2)}) collective-permute-start(bf16[3,2048]{1,0:T(4,128)(2,1)S(1)} %slice.3), channel_id=1, source_target_pairs={{0,2},{2,4},{4,6},{6,8},{8,10},{10,12},{12,14},{14,0},{1,3},{3,5},... | collective-permute-start | bytes 36872 | tf_op jit(solution)/shard_map/ppermute | solution.py:36
  4.9 18.6 %copy-start.1 = (bf16[512,2048]{1,0:T(8,128)(2,1)S(1)}, bf16[512,2048]{1,0:T(8,128)(2,1)}, u32[]{:S(2)}) copy-start(bf16[512,2048]{1,0:T(8,128)(2,1)} %y_ref.1) | copy-start | bytes 6291460
  4.9 18.6 %copy-start.2 = (bf16[2048,512]{1,0:T(8,128)(2,1)S(1)}, bf16[2048,512]{1,0:T(8,128)(2,1)}, u32[]{:S(2)}) copy-start(bf16[2048,512]{1,0:T(8,128)(2,1)} %panel_ref.1) | copy-start | bytes 6291460
  4.9 18.6 %copy-start.3 = (f32[16,512]{1,0:T(8,128)S(1)}, f32[16,512]{1,0:T(8,128)}, u32[]{:S(2)}) copy-start(f32[16,512]{1,0:T(8,128)} %scale_ref.1) | copy-start | bytes 98308
  18.6 2.7 %collective-permute-start.1 = (f32[2,2048]{1,0:T(2,128)S(1)}, f32[2,2048]{1,0:T(2,128)S(1)}, u32[]{:S(2)}, u32[]{:S(2)}) collective-permute-start(f32[2,2048]{1,0:T(2,128)S(1)} %get-tuple-element.28.tot_ref), channel_id=1, source_target_pairs={{0,2},{2,0},{4,6},{6,4},{8,10},{10,8},{12,14},{14,12},{1,3},{3,1},... | collective-permute-start | bytes 49160 | tf_op jit(solution)/shard_map/ppermute | solution.py:41
  21.3 5.2 %collective-permute-start.2 = (f32[2,2048]{1,0:T(2,128)S(1)}, f32[2,2048]{1,0:T(2,128)S(1)}, u32[]{:S(2)}, u32[]{:S(2)}) collective-permute-start(f32[2,2048]{1,0:T(2,128)S(1)} %level.1), channel_id=1, source_target_pairs={{0,4},{2,6},{4,8},{6,10},{8,12},{10,14},{12,0},{14,2},{1,5},{3,7},... | collective-permute-start | bytes 49160 | tf_op jit(solution)/shard_map/ppermute | solution.py:36
  22.6 3.9 %collective-permute-start.3 = (f32[2,2048]{1,0:T(2,128)S(1)}, f32[2,2048]{1,0:T(2,128)S(1)}, u32[]{:S(2)}, u32[]{:S(2)}) collective-permute-start(f32[2,2048]{1,0:T(2,128)S(1)} %level.1), channel_id=1, source_target_pairs={{0,8},{2,10},{4,12},{6,14},{8,0},{10,2},{12,4},{14,6},{1,9},{3,11}... | collective-permute-start | bytes 49160 | tf_op jit(solution)/shard_map/ppermute | solution.py:36
  29.1 17.5 %copy-start = (bf16[512,2048]{1,0:T(8,128)(2,1)S(1)}, bf16[512,2048]{1,0:T(8,128)(2,1)}, u32[]{:S(2)}) copy-start(bf16[512,2048]{1,0:T(8,128)(2,1)} %q_ref.7) | copy-start | bytes 6291460
  29.2 6.3 %collective-permute-start.4 = (f32[512,512]{1,0:T(8,128)S(1)}, f32[512,512]{1,0:T(8,128)S(1)}, u32[]{:S(2)}, u32[]{:S(2)}) collective-permute-start(f32[512,512]{1,0:T(8,128)S(1)} %get-tuple-element.30.a_ref), channel_id=1, source_target_pairs={{0,1},{1,0},{2,3},{3,2},{4,5},{5,4},{6,7},{7,6},{8,9},{9,8},{10,11... | collective-permute-start | bytes 3145736 | tf_op jit(solution)/shard_map/ppermute | solution.py:45
  35.7 7.7 %collective-permute-start.5 = (bf16[512,256]{1,0:T(8,128)(2,1)S(1)}, bf16[512,256]{1,0:T(8,128)(2,1)S(1)}, u32[]{:S(2)}, u32[]{:S(2)}) collective-permute-start(bf16[512,256]{1,0:T(8,128)(2,1)S(1)} %get-tuple-element.31), channel_id=1, source_target_pairs={{0,4},{2,6},{4,8},{6,10},{8,12},{10,14},{12,0},{14,2},{1,5},{3,7},... | collective-permute-start | bytes 786440 | tf_op jit(solution)/shard_map/ppermute | solution.py:36
  37.5 7.5 %collective-permute-start.12 = (bf16[512,256]{1,0:T(8,128)(2,1)S(1)}, bf16[512,256]{1,0:T(8,128)(2,1)S(1)}, u32[]{:S(2)}, u32[]{:S(2)}) collective-permute-start(bf16[512,256]{1,0:T(8,128)(2,1)S(1)} %get-tuple-element.31), channel_id=1, source_target_pairs={{0,2},{2,0},{4,6},{6,4},{8,10},{10,8},{12,14},{14,12},{1,3},{3,1},... | collective-permute-start | bytes 786440 | tf_op jit(solution)/shard_map/ppermute | solution.py:41
  43.4 9.4 %collective-permute-start.6 = (bf16[512,256]{1,0:T(8,128)(2,1)S(1)}, bf16[512,256]{1,0:T(8,128)(2,1)S(1)}, u32[]{:S(2)}, u32[]{:S(2)}) collective-permute-start(bf16[512,256]{1,0:T(8,128)(2,1)S(1)} %collective-permute-done.5.refs_2_), channel_id=1, source_target_pairs={{0,4},{2,6},{4,8},{6,10},{8,12},{10,14},{12,0},{14,2},{1,5},{3,7},... | collective-permute-start | bytes 786440 | tf_op jit(solution)/shard_map/ppermute | solution.py:36
  45.0 10.0 %collective-permute-start.9 = (bf16[512,256]{1,0:T(8,128)(2,1)S(1)}, bf16[512,256]{1,0:T(8,128)(2,1)S(1)}, u32[]{:S(2)}, u32[]{:S(2)}) collective-permute-start(bf16[512,256]{1,0:T(8,128)(2,1)S(1)} %collective-permute-done.5.refs_2_), channel_id=1, source_target_pairs={{0,2},{2,0},{4,6},{6,4},{8,10},{10,8},{12,14},{14,12},{1,3},{3,1},... | collective-permute-start | bytes 786440 | tf_op jit(solution)/shard_map/ppermute | solution.py:41
  45.0 10.4 %collective-permute-start.13 = (bf16[512,256]{1,0:T(8,128)(2,1)S(1)}, bf16[512,256]{1,0:T(8,128)(2,1)S(1)}, u32[]{:S(2)}, u32[]{:S(2)}) collective-permute-start(bf16[512,256]{1,0:T(8,128)(2,1)S(1)} %collective-permute-done.12.refs_0_), channel_id=1, source_target_pairs={{0,1},{1,0},{2,3},{3,2},{4,5},{5,4},{6,7},{7,6},{8,9},{9,8},{10,11... | collective-permute-start | bytes 786440 | tf_op jit(solution)/shard_map/ppermute | solution.py:45
  46.6 8.9 %collective-permute-start.14 = (bf16[512,256]{1,0:T(8,128)(2,1)S(1)}, bf16[512,256]{1,0:T(8,128)(2,1)S(1)}, u32[]{:S(2)}, u32[]{:S(2)}) collective-permute-start(bf16[512,256]{1,0:T(8,128)(2,1)S(1)} %collective-permute-done.5.refs_2_), channel_id=1, source_target_pairs={{0,1},{1,0},{2,3},{3,2},{4,5},{5,4},{6,7},{7,6},{8,9},{9,8},{10,11... | collective-permute-start | bytes 786440 | tf_op jit(solution)/shard_map/ppermute | solution.py:45
  52.8 13.4 %collective-permute-start.11 = (bf16[512,256]{1,0:T(8,128)(2,1)S(1)}, bf16[512,256]{1,0:T(8,128)(2,1)S(1)}, u32[]{:S(2)}, u32[]{:S(2)}) collective-permute-start(bf16[512,256]{1,0:T(8,128)(2,1)S(1)} %collective-permute-done.6.refs_2_), channel_id=1, source_target_pairs={{0,1},{1,0},{2,3},{3,2},{4,5},{5,4},{6,7},{7,6},{8,9},{9,8},{10,11... | collective-permute-start | bytes 786440 | tf_op jit(solution)/shard_map/ppermute | solution.py:45
  53.3 12.6 %collective-permute-start.7 = (bf16[512,256]{1,0:T(8,128)(2,1)S(1)}, bf16[512,256]{1,0:T(8,128)(2,1)S(1)}, u32[]{:S(2)}, u32[]{:S(2)}) collective-permute-start(bf16[512,256]{1,0:T(8,128)(2,1)S(1)} %collective-permute-done.6.refs_2_), channel_id=1, source_target_pairs={{0,2},{2,0},{4,6},{6,4},{8,10},{10,8},{12,14},{14,12},{1,3},{3,1},... | collective-permute-start | bytes 786440 | tf_op jit(solution)/shard_map/ppermute | solution.py:41
  55.1 11.1 %collective-permute-start.10 = (bf16[512,256]{1,0:T(8,128)(2,1)S(1)}, bf16[512,256]{1,0:T(8,128)(2,1)S(1)}, u32[]{:S(2)}, u32[]{:S(2)}) collective-permute-start(bf16[512,256]{1,0:T(8,128)(2,1)S(1)} %collective-permute-done.9.refs_0_), channel_id=1, source_target_pairs={{0,1},{1,0},{2,3},{3,2},{4,5},{5,4},{6,7},{7,6},{8,9},{9,8},{10,11... | collective-permute-start | bytes 786440 | tf_op jit(solution)/shard_map/ppermute | solution.py:45
  66.0 17.9 %collective-permute-start.8 = (bf16[512,256]{1,0:T(8,128)(2,1)S(1)}, bf16[512,256]{1,0:T(8,128)(2,1)S(1)}, u32[]{:S(2)}, u32[]{:S(2)}) collective-permute-start(bf16[512,256]{1,0:T(8,128)(2,1)S(1)} %collective-permute-done.7.refs_0_), channel_id=1, source_target_pairs={{0,1},{1,0},{2,3},{3,2},{4,5},{5,4},{6,7},{7,6},{8,9},{9,8},{10,11... | collective-permute-start | bytes 786440 | tf_op jit(solution)/shard_map/ppermute | solution.py:45

commit v7 on v6

--- a/solution.py
+++ b/solution.py
@@ -79,6 +79,7 @@
     scale_all,
     gb_all,
     rate_all,
+    hits,
     sems,
     small_sems,
 ):
@@ -116,12 +117,17 @@
     for copy in smalls:
         copy.wait()
 
+    for k in range(seg_len // CHUNK):
+        hits[k] = 0
+    for d in range(DOCS):
+        off = starts_ref[d] - base
+
+        @pl.when((off >= 0) & (off < rows))
+        def _(off=off):
+            hits[lax.rem(off, seg_len) // CHUNK] = 1
+
     def hit(k):
-        found = False
-        for d in range(DOCS):
-            off = starts_ref[d] - base
-            found = found | ((off >= 0) & (off < rows) & ((off % seg_len) // CHUNK == k))
-        return found
+        return hits[k] > 0
 
     def block(b, z):
         fetch_x(b).wait()
@@ -628,6 +634,7 @@
             pltpu.VMEM((2, width, 2 * width), BF16),
         ]
         + [pltpu.VMEM(a.shape, F32) for a in (conv_weight, conv_bias, gate_scale, gate_bias, decay_rate)]
+        + [pltpu.SMEM((rows // SEGS // CHUNK,), jnp.int32)]
         + [pltpu.SemaphoreType.DMA((2, 2)), pltpu.SemaphoreType.DMA((5,))],
         out_shape=[
             jax.ShapeDtypeStruct((channels // 128, rows, 128), F32),

time: 95.3 us -> 92.9 us (0.975)
  Pallas kernels: 64.7 us -> 62.4 us
    pallas_call x1, Pallas kernels: 13.7 us -> 11.3 us  [recur_call(): pl.pallas_call(recur_kernel, in_specs=[pl.BlockSpec(memory_space=pltpu.SM...]
  transfers between devices with their start and end apart: 15 -> 15, of which waited for: 4 -> 4; matrix products, arithmetic and copies ran while one was open for 1% -> 1% of each run, Pallas kernels for 39% -> 40%
where the time goes in v7:
time: 92.9 us; the launch traced here: 92.6 us
  Pallas kernels  62.4 us (67%)
  starting transfers between devices  15.7 us (17%)
  waiting for transfers between devices  12 us (13%)
    pallas_call x4, Pallas kernels, attend_call(): pl.pallas_call(functools.partial(attend_kernel, own is not None, lags, fi...  45.3 us
    pallas_call x1, Pallas kernels, recur_call(): pl.pallas_call(recur_kernel, in_specs=[pl.BlockSpec(memory_space=pltpu.SM...  11.3 us
    ppermute x5, waiting for transfers between devices, ring(): return lax.ppermute(x, 'tm', [(i, (i + lag) % n) for i in range(n)])  7.28 us
    ppermute x5, starting transfers between devices, ring(): return lax.ppermute(x, 'tm', [(i, (i + lag) % n) for i in range(n)])  6.99 us
    ppermute x6, starting transfers between devices, partner(): return lax.ppermute(x, 'mp', [(0, 1), (1, 0)])  6.75 us
    pallas_call x1, Pallas kernels, ready_call(): pl.pallas_call(ready_kernel, in_specs=[vmem] * 5, out_specs=[vmem] * 3, o...  2.92 us
    pallas_call x1, Pallas kernels, mix_call(): pl.pallas_call(functools.partial(mix_kernel, len(past)), in_specs=[vmem]...  2.6 us
    ppermute x4, waiting for transfers between devices, swap(): return lax.ppermute(x, 'tm', [(i, i ^ 1) for i in range(n)])  2.44 us
  transfers between devices with their start and end apart: 15, of which 4 were waited for; matrix products, arithmetic and copies ran while one was open for 1% of the time, Pallas kernels for 40%

profile of v7, /device:TPU:17, one launch (start us, length us, event | category | flops | bytes accessed | tf_op | source)
XLA Modules:
  0.0 92.6 jit_solution(16935878088032447231)
XLA Ops:
  0.6 0.8 slice.3
  1.4 1.3 %collective-permute-start = (bf16[3,2048]{1,0:T(4,128)(2,1)S(1)}, bf16[3,2048]{1,0:T(4,128)(2,1)S(1)}, u32[]{:S(2)}, u32[]{:S(2)}) collective-permute-start(bf16[3,2048]{1,0:T(4,128)(2,1)S(1)} %slice.3), channel_id=1, source_target_pairs={{0,2},{2,4},{4,6},{6,8},{8,10},{10,12},{12,14},{14,0},{1,3},{3,5},... | collective-permute-start | bytes 36872 | tf_op jit(solution)/shard_map/ppermute | solution.py:36
  2.7 0.9 convert_reduce_fusion.starts_ref
  3.6 1.4 %collective-permute-done.halo_all = bf16[3,2048]{1,0:T(4,128)(2,1)S(1)} collective-permute-done((bf16[3,2048]{1,0:T(4,128)(2,1)S(1)}, bf16[3,2048]{1,0:T(4,128)(2,1)S(1)}, u32[]{:S(2)}, u32[]{:S(2)}) %collective-permute-start) | collective-permute-done | bytes 12320 | tf_op jit(solution)/shard_map/ppermute | solution.py:36
  5.0 11.3 %recur.1 = (f32[16,512,128]{2,1,0:T(8,128)S(1)}, f32[16,512,128]{2,1,0:T(8,128)S(1)}, f32[2,8,2048]{2,1,0:T(8,128)S(1)}, f32[2,2048]{1,0:T(2,128)S(1)}) custom-call(s32[4]{0:T(128)S(1)} %convert_reduce_fusion.starts_ref, bf16[512,2048]{1,0:T(8,128)(2,1)} %x_hbm.1, bf16[3,2048]{1,0:T(4,128)(2,1)S(1)} %collective-permute-done.halo_all, f32[4,2048]{1,0:T(4,128)} %cw_hbm.1, ...), custom_call_target="tpu_custom_call" | custom-call | tf_op jit(solution)/shard_map/recur/pallas_call | solution.py:624
  16.3 0.2 collective-permute-start.1
  16.5 2.4 %collective-permute-done.1.near_ref = f32[2,2048]{1,0:T(2,128)S(1)} collective-permute-done((f32[2,2048]{1,0:T(2,128)S(1)}, f32[2,2048]{1,0:T(2,128)S(1)}, u32[]{:S(2)}, u32[]{:S(2)}) %collective-permute-start.1) | collective-permute-done | bytes 16416 | tf_op jit(solution)/shard_map/ppermute | solution.py:41
  18.9 1.3 %collective-permute-start.2 = (f32[2,2048]{1,0:T(2,128)S(1)}, f32[2,2048]{1,0:T(2,128)S(1)}, u32[]{:S(2)}, u32[]{:S(2)}) collective-permute-start(f32[2,2048]{1,0:T(2,128)S(1)} %level.1), channel_id=1, source_target_pairs={{0,4},{2,6},{4,8},{6,10},{8,12},{10,14},{12,0},{14,2},{1,5},{3,7},... | collective-permute-start | bytes 49160 | tf_op jit(solution)/shard_map/ppermute | solution.py:36
  20.3 0.9 %collective-permute-start.3 = (f32[2,2048]{1,0:T(2,128)S(1)}, f32[2,2048]{1,0:T(2,128)S(1)}, u32[]{:S(2)}, u32[]{:S(2)}) collective-permute-start(f32[2,2048]{1,0:T(2,128)S(1)} %level.1), channel_id=1, source_target_pairs={{0,8},{2,10},{4,12},{6,14},{8,0},{10,2},{12,4},{14,6},{1,9},{3,11}... | collective-permute-start | bytes 49160 | tf_op jit(solution)/shard_map/ppermute | solution.py:36
  21.2 2.9 %ready.1 = (f32[512,2048]{1,0:T(8,128)S(1)}, f32[512,2048]{1,0:T(8,128)S(1)}, bf16[2048,512]{1,0:T(8,128)(2,1)S(1)}) custom-call(f32[16,512,128]{2,1,0:T(8,128)S(1)} %get-tuple-element.22.h_ref, f32[16,512,128]{2,1,0:T(8,128)S(1)} %get-tuple-element.23.p_ref, bf16[512,2048]{1,0:T(8,128)(2,1)S(1)} %copy-done.1, bf16[2048,512]{1,0:T(8,128)(2,1)S(1)} %copy-done.2, ...), custom_call_target="tpu_custom_call" | custom-call | flops 16777216 | bytes 4194304 | tf_op jit(solution)/shard_map/ready/pallas_call | solution.py:663
  24.2 2.6 %mix.1 = (bf16[512,2048]{1,0:T(8,128)(2,1)}, f32[512,512]{1,0:T(8,128)S(1)}) custom-call(f32[512,2048]{1,0:T(8,128)S(1)} %get-tuple-element.24.hg_ref, f32[512,2048]{1,0:T(8,128)S(1)} %get-tuple-element.25.pg_ref, bf16[2048,512]{1,0:T(8,128)(2,1)S(1)} %get-tuple-element.26.w_ref, f32[2,8,2048]{2,1,0:T(8,128)S(1)} %get-tuple-element.27.ends_ref, ...), custom_call_target="tpu_custom_call" | custom-call | tf_op jit(solution)/shard_map/mix/pallas_call | solution.py:679
  26.8 4.1 %collective-permute-start.4 = (f32[512,512]{1,0:T(8,128)S(1)}, f32[512,512]{1,0:T(8,128)S(1)}, u32[]{:S(2)}, u32[]{:S(2)}) collective-permute-start(f32[512,512]{1,0:T(8,128)S(1)} %get-tuple-element.30.a_ref), channel_id=1, source_target_pairs={{0,1},{1,0},{2,3},{3,2},{4,5},{5,4},{6,7},{7,6},{8,9},{9,8},{10,11... | collective-permute-start | bytes 3145736 | tf_op jit(solution)/shard_map/ppermute | solution.py:45
  30.9 2.3 %collective-permute-done.4.b_ref = f32[512,512]{1,0:T(8,128)S(1)} collective-permute-done((f32[512,512]{1,0:T(8,128)S(1)}, f32[512,512]{1,0:T(8,128)S(1)}, u32[]{:S(2)}, u32[]{:S(2)}) %collective-permute-start.4) | collective-permute-done | bytes 1048608 | tf_op jit(solution)/shard_map/ppermute | solution.py:45
  33.4 1.8 %collective-permute-start.5 = (bf16[512,256]{1,0:T(8,128)(2,1)S(1)}, bf16[512,256]{1,0:T(8,128)(2,1)S(1)}, u32[]{:S(2)}, u32[]{:S(2)}) collective-permute-start(bf16[512,256]{1,0:T(8,128)(2,1)S(1)} %get-tuple-element.31), channel_id=1, source_target_pairs={{0,4},{2,6},{4,8},{6,10},{8,12},{10,14},{12,0},{14,2},{1,5},{3,7},... | collective-permute-start | bytes 786440 | tf_op jit(solution)/shard_map/ppermute | solution.py:36
  35.2 5.9 %collective-permute-done.5.refs_2_ = bf16[512,256]{1,0:T(8,128)(2,1)S(1)} collective-permute-done((bf16[512,256]{1,0:T(8,128)(2,1)S(1)}, bf16[512,256]{1,0:T(8,128)(2,1)S(1)}, u32[]{:S(2)}, u32[]{:S(2)}) %collective-permute-start.5) | collective-permute-done | bytes 262176 | tf_op jit(solution)/shard_map/ppermute | solution.py:36
  41.1 1.6 %collective-permute-start.6 = (bf16[512,256]{1,0:T(8,128)(2,1)S(1)}, bf16[512,256]{1,0:T(8,128)(2,1)S(1)}, u32[]{:S(2)}, u32[]{:S(2)}) collective-permute-start(bf16[512,256]{1,0:T(8,128)(2,1)S(1)} %collective-permute-done.5.refs_2_), channel_id=1, source_target_pairs={{0,4},{2,6},{4,8},{6,10},{8,12},{10,14},{12,0},{14,2},{1,5},{3,7},... | collective-permute-start | bytes 786440 | tf_op jit(solution)/shard_map/ppermute | solution.py:36
  42.7 1.5 %collective-permute-start.13 = (bf16[512,256]{1,0:T(8,128)(2,1)S(1)}, bf16[512,256]{1,0:T(8,128)(2,1)S(1)}, u32[]{:S(2)}, u32[]{:S(2)}) collective-permute-start(bf16[512,256]{1,0:T(8,128)(2,1)S(1)} %collective-permute-done.12.refs_0_), channel_id=1, source_target_pairs={{0,1},{1,0},{2,3},{3,2},{4,5},{5,4},{6,7},{7,6},{8,9},{9,8},{10,11... | collective-permute-start | bytes 786440 | tf_op jit(solution)/shard_map/ppermute | solution.py:45
  44.3 6.2 %attend_own.1 = (f32[512,2048]{1,0:T(8,128)S(1)}, f32[512,1024]{1,0:T(8,128)S(1)}, f32[512,1024]{1,0:T(8,128)S(1)}) custom-call(s32[4]{0:T(128)S(1)} %convert_reduce_fusion.starts_ref, bf16[512,2048]{1,0:T(8,128)(2,1)S(1)} %copy-done, bf16[2,512,256]{2,1,0:T(8,128)(2,1)S(1)} %get-tuple-element.32.refs_0_), custom_call_target="tpu_custom_call" | custom-call | flops 2147483648 | bytes 4194304 | tf_op jit(solution)/shard_map/attend_own/pallas_call | solution.py:737
  50.5 0.5 collective-permute-start.11
  51.0 1.7 %collective-permute-start.7 = (bf16[512,256]{1,0:T(8,128)(2,1)S(1)}, bf16[512,256]{1,0:T(8,128)(2,1)S(1)}, u32[]{:S(2)}, u32[]{:S(2)}) collective-permute-start(bf16[512,256]{1,0:T(8,128)(2,1)S(1)} %collective-permute-done.6.refs_2_), channel_id=1, source_target_pairs={{0,2},{2,0},{4,6},{6,4},{8,10},{10,8},{12,14},{14,12},{1,3},{3,1},... | collective-permute-start | bytes 786440 | tf_op jit(solution)/shard_map/ppermute | solution.py:41
  52.7 0.4 collective-permute-start.10
  53.1 10.5 %attend_mid.2 = (f32[512,2048]{1,0:T(8,128)S(1)}, f32[512,1024]{1,0:T(8,128)S(1)}, f32[512,1024]{1,0:T(8,128)S(1)}) custom-call(s32[4]{0:T(128)S(1)} %convert_reduce_fusion.starts_ref, bf16[512,2048]{1,0:T(8,128)(2,1)S(1)} %copy-done, ...), custom_call_target="tpu_custom_call", output_to_operand_aliasing={{0}: (6, {}), {1}: (7, {}), {2}: (8, {})} | custom-call | flops 4294967296 | bytes 4194304 | tf_op jit(solution)/shard_map/attend_mid/pallas_call | solution.py:737
  63.8 17.7 %attend_mid.3 = (f32[512,2048]{1,0:T(8,128)S(1)}, f32[512,1024]{1,0:T(8,128)S(1)}, f32[512,1024]{1,0:T(8,128)S(1)}) custom-call(s32[4]{0:T(128)S(1)} %convert_reduce_fusion.starts_ref, bf16[512,2048]{1,0:T(8,128)(2,1)S(1)} %copy-done, ...), custom_call_target="tpu_custom_call", output_to_operand_aliasing={{0}: (6, {}), {1}: (7, {}), {2}: (8, {})} | custom-call | flops 4294967296 | bytes 4194304 | tf_op jit(solution)/shard_map/attend_mid/pallas_call | solution.py:737
  81.5 10.9 %attend_end.1 = bf16[512,2048]{1,0:T(8,128)(2,1)} custom-call(s32[4]{0:T(128)S(1)} %convert_reduce_fusion.starts_ref, bf16[512,2048]{1,0:T(8,128)(2,1)S(1)} %copy-done, bf16[512,256]{1,0:T(8,128)(2,1)S(1)} %collective-permute-done.7.refs_0_, bf16[512,256]{1,0:T(8,128)(2,1)S(1)} %collective-permute-done.8.refs_1_, f32[512,2048]{1,0:T(8,128)S(1)} %get-tuple-element.39.refs_2_, ...), custom_call_target="tpu_custom_call" | custom-call | flops 2147483648 | bytes 4194304 | tf_op jit(solution)/shard_map/attend_end/pallas_call | solution.py:737
  (25 shorter events, 0.5 us)
Async XLA Ops:
  1.4 3.5 %collective-permute-start = (bf16[3,2048]{1,0:T(4,128)(2,1)S(1)}, bf16[3,2048]{1,0:T(4,128)(2,1)S(1)}, u32[]{:S(2)}, u32[]{:S(2)}) collective-permute-start(bf16[3,2048]{1,0:T(4,128)(2,1)S(1)} %slice.3), channel_id=1, source_target_pairs={{0,2},{2,4},{4,6},{6,8},{8,10},{10,12},{12,14},{14,0},{1,3},{3,5},... | collective-permute-start | bytes 36872 | tf_op jit(solution)/shard_map/ppermute | solution.py:36
  4.9 16.3 %copy-start.1 = (bf16[512,2048]{1,0:T(8,128)(2,1)S(1)}, bf16[512,2048]{1,0:T(8,128)(2,1)}, u32[]{:S(2)}) copy-start(bf16[512,2048]{1,0:T(8,128)(2,1)} %y_ref.1) | copy-start | bytes 6291460
  4.9 16.3 %copy-start.2 = (bf16[2048,512]{1,0:T(8,128)(2,1)S(1)}, bf16[2048,512]{1,0:T(8,128)(2,1)}, u32[]{:S(2)}) copy-start(bf16[2048,512]{1,0:T(8,128)(2,1)} %panel_ref.1) | copy-start | bytes 6291460
  4.9 16.3 %copy-start.3 = (f32[16,512]{1,0:T(8,128)S(1)}, f32[16,512]{1,0:T(8,128)}, u32[]{:S(2)}) copy-start(f32[16,512]{1,0:T(8,128)} %scale_ref.1) | copy-start | bytes 98308
  16.3 2.7 %collective-permute-start.1 = (f32[2,2048]{1,0:T(2,128)S(1)}, f32[2,2048]{1,0:T(2,128)S(1)}, u32[]{:S(2)}, u32[]{:S(2)}) collective-permute-start(f32[2,2048]{1,0:T(2,128)S(1)} %get-tuple-element.28.tot_ref), channel_id=1, source_target_pairs={{0,2},{2,0},{4,6},{6,4},{8,10},{10,8},{12,14},{14,12},{1,3},{3,1},... | collective-permute-start | bytes 49160 | tf_op jit(solution)/shard_map/ppermute | solution.py:41
  18.9 5.2 %collective-permute-start.2 = (f32[2,2048]{1,0:T(2,128)S(1)}, f32[2,2048]{1,0:T(2,128)S(1)}, u32[]{:S(2)}, u32[]{:S(2)}) collective-permute-start(f32[2,2048]{1,0:T(2,128)S(1)} %level.1), channel_id=1, source_target_pairs={{0,4},{2,6},{4,8},{6,10},{8,12},{10,14},{12,0},{14,2},{1,5},{3,7},... | collective-permute-start | bytes 49160 | tf_op jit(solution)/shard_map/ppermute | solution.py:36
  20.3 3.9 %collective-permute-start.3 = (f32[2,2048]{1,0:T(2,128)S(1)}, f32[2,2048]{1,0:T(2,128)S(1)}, u32[]{:S(2)}, u32[]{:S(2)}) collective-permute-start(f32[2,2048]{1,0:T(2,128)S(1)} %level.1), channel_id=1, source_target_pairs={{0,8},{2,10},{4,12},{6,14},{8,0},{10,2},{12,4},{14,6},{1,9},{3,11}... | collective-permute-start | bytes 49160 | tf_op jit(solution)/shard_map/ppermute | solution.py:36
  26.8 17.5 %copy-start = (bf16[512,2048]{1,0:T(8,128)(2,1)S(1)}, bf16[512,2048]{1,0:T(8,128)(2,1)}, u32[]{:S(2)}) copy-start(bf16[512,2048]{1,0:T(8,128)(2,1)} %q_ref.7) | copy-start | bytes 6291460
  26.8 6.3 %collective-permute-start.4 = (f32[512,512]{1,0:T(8,128)S(1)}, f32[512,512]{1,0:T(8,128)S(1)}, u32[]{:S(2)}, u32[]{:S(2)}) collective-permute-start(f32[512,512]{1,0:T(8,128)S(1)} %get-tuple-element.30.a_ref), channel_id=1, source_target_pairs={{0,1},{1,0},{2,3},{3,2},{4,5},{5,4},{6,7},{7,6},{8,9},{9,8},{10,11... | collective-permute-start | bytes 3145736 | tf_op jit(solution)/shard_map/ppermute | solution.py:45
  33.4 7.7 %collective-permute-start.5 = (bf16[512,256]{1,0:T(8,128)(2,1)S(1)}, bf16[512,256]{1,0:T(8,128)(2,1)S(1)}, u32[]{:S(2)}, u32[]{:S(2)}) collective-permute-start(bf16[512,256]{1,0:T(8,128)(2,1)S(1)} %get-tuple-element.31), channel_id=1, source_target_pairs={{0,4},{2,6},{4,8},{6,10},{8,12},{10,14},{12,0},{14,2},{1,5},{3,7},... | collective-permute-start | bytes 786440 | tf_op jit(solution)/shard_map/ppermute | solution.py:36
  35.2 7.5 %collective-permute-start.12 = (bf16[512,256]{1,0:T(8,128)(2,1)S(1)}, bf16[512,256]{1,0:T(8,128)(2,1)S(1)}, u32[]{:S(2)}, u32[]{:S(2)}) collective-permute-start(bf16[512,256]{1,0:T(8,128)(2,1)S(1)} %get-tuple-element.31), channel_id=1, source_target_pairs={{0,2},{2,0},{4,6},{6,4},{8,10},{10,8},{12,14},{14,12},{1,3},{3,1},... | collective-permute-start | bytes 786440 | tf_op jit(solution)/shard_map/ppermute | solution.py:41
  41.1 9.4 %collective-permute-start.6 = (bf16[512,256]{1,0:T(8,128)(2,1)S(1)}, bf16[512,256]{1,0:T(8,128)(2,1)S(1)}, u32[]{:S(2)}, u32[]{:S(2)}) collective-permute-start(bf16[512,256]{1,0:T(8,128)(2,1)S(1)} %collective-permute-done.5.refs_2_), channel_id=1, source_target_pairs={{0,4},{2,6},{4,8},{6,10},{8,12},{10,14},{12,0},{14,2},{1,5},{3,7},... | collective-permute-start | bytes 786440 | tf_op jit(solution)/shard_map/ppermute | solution.py:36
  42.7 10.0 %collective-permute-start.9 = (bf16[512,256]{1,0:T(8,128)(2,1)S(1)}, bf16[512,256]{1,0:T(8,128)(2,1)S(1)}, u32[]{:S(2)}, u32[]{:S(2)}) collective-permute-start(bf16[512,256]{1,0:T(8,128)(2,1)S(1)} %collective-permute-done.5.refs_2_), channel_id=1, source_target_pairs={{0,2},{2,0},{4,6},{6,4},{8,10},{10,8},{12,14},{14,12},{1,3},{3,1},... | collective-permute-start | bytes 786440 | tf_op jit(solution)/shard_map/ppermute | solution.py:41
  42.7 10.4 %collective-permute-start.13 = (bf16[512,256]{1,0:T(8,128)(2,1)S(1)}, bf16[512,256]{1,0:T(8,128)(2,1)S(1)}, u32[]{:S(2)}, u32[]{:S(2)}) collective-permute-start(bf16[512,256]{1,0:T(8,128)(2,1)S(1)} %collective-permute-done.12.refs_0_), channel_id=1, source_target_pairs={{0,1},{1,0},{2,3},{3,2},{4,5},{5,4},{6,7},{7,6},{8,9},{9,8},{10,11... | collective-permute-start | bytes 786440 | tf_op jit(solution)/shard_map/ppermute | solution.py:45
  44.2 8.9 %collective-permute-start.14 = (bf16[512,256]{1,0:T(8,128)(2,1)S(1)}, bf16[512,256]{1,0:T(8,128)(2,1)S(1)}, u32[]{:S(2)}, u32[]{:S(2)}) collective-permute-start(bf16[512,256]{1,0:T(8,128)(2,1)S(1)} %collective-permute-done.5.refs_2_), channel_id=1, source_target_pairs={{0,1},{1,0},{2,3},{3,2},{4,5},{5,4},{6,7},{7,6},{8,9},{9,8},{10,11... | collective-permute-start | bytes 786440 | tf_op jit(solution)/shard_map/ppermute | solution.py:45
  50.5 13.4 %collective-permute-start.11 = (bf16[512,256]{1,0:T(8,128)(2,1)S(1)}, bf16[512,256]{1,0:T(8,128)(2,1)S(1)}, u32[]{:S(2)}, u32[]{:S(2)}) collective-permute-start(bf16[512,256]{1,0:T(8,128)(2,1)S(1)} %collective-permute-done.6.refs_2_), channel_id=1, source_target_pairs={{0,1},{1,0},{2,3},{3,2},{4,5},{5,4},{6,7},{7,6},{8,9},{9,8},{10,11... | collective-permute-start | bytes 786440 | tf_op jit(solution)/shard_map/ppermute | solution.py:45
  51.0 12.6 %collective-permute-start.7 = (bf16[512,256]{1,0:T(8,128)(2,1)S(1)}, bf16[512,256]{1,0:T(8,128)(2,1)S(1)}, u32[]{:S(2)}, u32[]{:S(2)}) collective-permute-start(bf16[512,256]{1,0:T(8,128)(2,1)S(1)} %collective-permute-done.6.refs_2_), channel_id=1, source_target_pairs={{0,2},{2,0},{4,6},{6,4},{8,10},{10,8},{12,14},{14,12},{1,3},{3,1},... | collective-permute-start | bytes 786440 | tf_op jit(solution)/shard_map/ppermute | solution.py:41
  52.7 11.1 %collective-permute-start.10 = (bf16[512,256]{1,0:T(8,128)(2,1)S(1)}, bf16[512,256]{1,0:T(8,128)(2,1)S(1)}, u32[]{:S(2)}, u32[]{:S(2)}) collective-permute-start(bf16[512,256]{1,0:T(8,128)(2,1)S(1)} %collective-permute-done.9.refs_0_), channel_id=1, source_target_pairs={{0,1},{1,0},{2,3},{3,2},{4,5},{5,4},{6,7},{7,6},{8,9},{9,8},{10,11... | collective-permute-start | bytes 786440 | tf_op jit(solution)/shard_map/ppermute | solution.py:45
  63.6 17.9 %collective-permute-start.8 = (bf16[512,256]{1,0:T(8,128)(2,1)S(1)}, bf16[512,256]{1,0:T(8,128)(2,1)S(1)}, u32[]{:S(2)}, u32[]{:S(2)}) collective-permute-start(bf16[512,256]{1,0:T(8,128)(2,1)S(1)} %collective-permute-done.7.refs_0_), channel_id=1, source_target_pairs={{0,1},{1,0},{2,3},{3,2},{4,5},{5,4},{6,7},{7,6},{8,9},{9,8},{10,11... | collective-permute-start | bytes 786440 | tf_op jit(solution)/shard_map/ppermute | solution.py:45

commit v8 on v7

--- a/solution.py
+++ b/solution.py
@@ -792,7 +792,7 @@
     own, half = sum_call(partial_kv, partner(partial_kv))
 
     levels = -(-WINDOW // rows) // 2
-    straight, attended = half, None
+    straight, attended, held, held_lags = half, None, [], []
     for k in range(levels + 1):
         last = k == levels
         beyond = None if last else ring(straight, 2)
@@ -801,10 +801,14 @@
             attended = attend_call(starts, queries, own, [], [], None, False)
         else:
             attended = attend_call(starts, queries, None, tiles, lags, attended, False)
-        tiles, lags = [crossed, partner(crossed)], [(2 * k, 1)]
-        if not last:
-            tiles += [beyond, partner(beyond)]
-            lags.append((2 * k + 2, 0))
+        near_tiles, near_lags = [crossed, partner(crossed)], [(2 * k, 1)]
+        if last:
+            tiles, lags = near_tiles, near_lags
+        else:
+            tiles, lags = [beyond, partner(beyond)], [(2 * k + 2, 0)]
+            held, held_lags = held + near_tiles, held_lags + near_lags
+            if k > 0:
+                tiles, lags, held, held_lags = tiles + held, lags + held_lags, [], []
         straight = beyond
     attended = attend_call(starts, queries, None, tiles, lags, attended, True)
     return mixed, attended

time: 92.9 us -> 97.4 us (1.048)
  waiting for transfers between devices: 12 us -> 15.5 us
    ppermute x5, waiting for transfers between devices: 7.28 us -> 10.8 us  [ring(): return lax.ppermute(x, 'tm', [(i, (i + lag) % n) for i in range(n)])]
    ppermute x6, starting transfers between devices: 6.75 us -> 9.31 us  [partner(): return lax.ppermute(x, 'mp', [(0, 1), (1, 0)])]
    ppermute x4, starting transfers between devices: 1.94 us -> 0.23 us  [swap(): return lax.ppermute(x, 'tm', [(i, i ^ 1) for i in range(n)])]
  transfers between devices with their start and end apart: 15 -> 15, of which waited for: 4 -> 5; matrix products, arithmetic and copies ran while one was open for 1% -> 1% of each run, Pallas kernels for 40% -> 39%
where the time goes in v8:
time: 97.4 us; the launch traced here: 97.1 us
  Pallas kernels  62.5 us (64%)
  starting transfers between devices  16.5 us (17%)
  waiting for transfers between devices  15.5 us (16%)
    pallas_call x4, Pallas kernels, attend_call(): pl.pallas_call(functools.partial(attend_kernel, own is not None, lags, fi...  45.4 us
    pallas_call x1, Pallas kernels, recur_call(): pl.pallas_call(recur_kernel, in_specs=[pl.BlockSpec(memory_space=pltpu.SM...  11.3 us
    ppermute x5, waiting for transfers between devices, ring(): return lax.ppermute(x, 'tm', [(i, (i + lag) % n) for i in range(n)])  10.8 us
    ppermute x6, starting transfers between devices, partner(): return lax.ppermute(x, 'mp', [(0, 1), (1, 0)])  9.31 us
    ppermute x5, starting transfers between devices, ring(): return lax.ppermute(x, 'tm', [(i, (i + lag) % n) for i in range(n)])  6.99 us
    pallas_call x1, Pallas kernels, ready_call(): pl.pallas_call(ready_kernel, in_specs=[vmem] * 5, out_specs=[vmem] * 3, o...  2.92 us
    pallas_call x1, Pallas kernels, mix_call(): pl.pallas_call(functools.partial(mix_kernel, len(past)), in_specs=[vmem]...  2.6 us
    ppermute x4, waiting for transfers between devices, swap(): return lax.ppermute(x, 'tm', [(i, i ^ 1) for i in range(n)])  2.44 us
  transfers between devices with their start and end apart: 15, of which 5 were waited for; matrix products, arithmetic and copies ran while one was open for 1% of the time, Pallas kernels for 39%

profile of v8, /device:TPU:17, one launch (start us, length us, event | category | flops | bytes accessed | tf_op | source)
XLA Modules:
  0.0 97.1 jit_solution(7042296909617286981)
XLA Ops:
  0.6 0.8 slice.3
  1.4 1.3 %collective-permute-start = (bf16[3,2048]{1,0:T(4,128)(2,1)S(1)}, bf16[3,2048]{1,0:T(4,128)(2,1)S(1)}, u32[]{:S(2)}, u32[]{:S(2)}) collective-permute-start(bf16[3,2048]{1,0:T(4,128)(2,1)S(1)} %slice.3), channel_id=1, source_target_pairs={{0,2},{2,4},{4,6},{6,8},{8,10},{10,12},{12,14},{14,0},{1,3},{3,5},... | collective-permute-start | bytes 36872 | tf_op jit(solution)/shard_map/ppermute | solution.py:36
  2.7 0.9 convert_reduce_fusion.starts_ref
  3.6 1.4 %collective-permute-done.halo_all = bf16[3,2048]{1,0:T(4,128)(2,1)S(1)} collective-permute-done((bf16[3,2048]{1,0:T(4,128)(2,1)S(1)}, bf16[3,2048]{1,0:T(4,128)(2,1)S(1)}, u32[]{:S(2)}, u32[]{:S(2)}) %collective-permute-start) | collective-permute-done | bytes 12320 | tf_op jit(solution)/shard_map/ppermute | solution.py:36
  5.0 11.3 %recur.1 = (f32[16,512,128]{2,1,0:T(8,128)S(1)}, f32[16,512,128]{2,1,0:T(8,128)S(1)}, f32[2,8,2048]{2,1,0:T(8,128)S(1)}, f32[2,2048]{1,0:T(2,128)S(1)}) custom-call(s32[4]{0:T(128)S(1)} %convert_reduce_fusion.starts_ref, bf16[512,2048]{1,0:T(8,128)(2,1)} %x_hbm.1, bf16[3,2048]{1,0:T(4,128)(2,1)S(1)} %collective-permute-done.halo_all, f32[4,2048]{1,0:T(4,128)} %cw_hbm.1, ...), custom_call_target="tpu_custom_call" | custom-call | tf_op jit(solution)/shard_map/recur/pallas_call | solution.py:624
  16.3 0.2 collective-permute-start.1
  16.5 2.4 %collective-permute-done.1.near_ref = f32[2,2048]{1,0:T(2,128)S(1)} collective-permute-done((f32[2,2048]{1,0:T(2,128)S(1)}, f32[2,2048]{1,0:T(2,128)S(1)}, u32[]{:S(2)}, u32[]{:S(2)}) %collective-permute-start.1) | collective-permute-done | bytes 16416 | tf_op jit(solution)/shard_map/ppermute | solution.py:41
  18.9 1.3 %collective-permute-start.2 = (f32[2,2048]{1,0:T(2,128)S(1)}, f32[2,2048]{1,0:T(2,128)S(1)}, u32[]{:S(2)}, u32[]{:S(2)}) collective-permute-start(f32[2,2048]{1,0:T(2,128)S(1)} %level.1), channel_id=1, source_target_pairs={{0,4},{2,6},{4,8},{6,10},{8,12},{10,14},{12,0},{14,2},{1,5},{3,7},... | collective-permute-start | bytes 49160 | tf_op jit(solution)/shard_map/ppermute | solution.py:36
  20.3 0.9 collective-permute-start.3
  21.2 2.9 %ready.1 = (f32[512,2048]{1,0:T(8,128)S(1)}, f32[512,2048]{1,0:T(8,128)S(1)}, bf16[2048,512]{1,0:T(8,128)(2,1)S(1)}) custom-call(f32[16,512,128]{2,1,0:T(8,128)S(1)} %get-tuple-element.22.h_ref, f32[16,512,128]{2,1,0:T(8,128)S(1)} %get-tuple-element.23.p_ref, bf16[512,2048]{1,0:T(8,128)(2,1)S(1)} %copy-done.1, bf16[2048,512]{1,0:T(8,128)(2,1)S(1)} %copy-done.2, ...), custom_call_target="tpu_custom_call" | custom-call | flops 16777216 | bytes 4194304 | tf_op jit(solution)/shard_map/ready/pallas_call | solution.py:663
  24.2 2.6 %mix.1 = (bf16[512,2048]{1,0:T(8,128)(2,1)}, f32[512,512]{1,0:T(8,128)S(1)}) custom-call(f32[512,2048]{1,0:T(8,128)S(1)} %get-tuple-element.24.hg_ref, f32[512,2048]{1,0:T(8,128)S(1)} %get-tuple-element.25.pg_ref, bf16[2048,512]{1,0:T(8,128)(2,1)S(1)} %get-tuple-element.26.w_ref, f32[2,8,2048]{2,1,0:T(8,128)S(1)} %get-tuple-element.27.ends_ref, ...), custom_call_target="tpu_custom_call" | custom-call | tf_op jit(solution)/shard_map/mix/pallas_call | solution.py:679
  26.8 4.1 %collective-permute-start.4 = (f32[512,512]{1,0:T(8,128)S(1)}, f32[512,512]{1,0:T(8,128)S(1)}, u32[]{:S(2)}, u32[]{:S(2)}) collective-permute-start(f32[512,512]{1,0:T(8,128)S(1)} %get-tuple-element.30.a_ref), channel_id=1, source_target_pairs={{0,1},{1,0},{2,3},{3,2},{4,5},{5,4},{6,7},{7,6},{8,9},{9,8},{10,11... | collective-permute-start | bytes 3145736 | tf_op jit(solution)/shard_map/ppermute | solution.py:45
  30.9 2.3 %collective-permute-done.4.b_ref = f32[512,512]{1,0:T(8,128)S(1)} collective-permute-done((f32[512,512]{1,0:T(8,128)S(1)}, f32[512,512]{1,0:T(8,128)S(1)}, u32[]{:S(2)}, u32[]{:S(2)}) %collective-permute-start.4) | collective-permute-done | bytes 1048608 | tf_op jit(solution)/shard_map/ppermute | solution.py:45
  33.4 1.8 %collective-permute-start.5 = (bf16[512,256]{1,0:T(8,128)(2,1)S(1)}, bf16[512,256]{1,0:T(8,128)(2,1)S(1)}, u32[]{:S(2)}, u32[]{:S(2)}) collective-permute-start(bf16[512,256]{1,0:T(8,128)(2,1)S(1)} %get-tuple-element.31), channel_id=1, source_target_pairs={{0,4},{2,6},{4,8},{6,10},{8,12},{10,14},{12,0},{14,2},{1,5},{3,7},... | collective-permute-start | bytes 786440 | tf_op jit(solution)/shard_map/ppermute | solution.py:36
  35.2 5.9 %collective-permute-done.5.refs_0_ = bf16[512,256]{1,0:T(8,128)(2,1)S(1)} collective-permute-done((bf16[512,256]{1,0:T(8,128)(2,1)S(1)}, bf16[512,256]{1,0:T(8,128)(2,1)S(1)}, u32[]{:S(2)}, u32[]{:S(2)}) %collective-permute-start.5) | collective-permute-done | bytes 262176 | tf_op jit(solution)/shard_map/ppermute | solution.py:36
  41.1 1.6 %collective-permute-start.6 = (bf16[512,256]{1,0:T(8,128)(2,1)S(1)}, bf16[512,256]{1,0:T(8,128)(2,1)S(1)}, u32[]{:S(2)}, u32[]{:S(2)}) collective-permute-start(bf16[512,256]{1,0:T(8,128)(2,1)S(1)} %collective-permute-done.5.refs_0_), channel_id=1, source_target_pairs={{0,4},{2,6},{4,8},{6,10},{8,12},{10,14},{12,0},{14,2},{1,5},{3,7},... | collective-permute-start | bytes 786440 | tf_op jit(solution)/shard_map/ppermute | solution.py:36
  42.7 1.5 %collective-permute-start.14 = (bf16[512,256]{1,0:T(8,128)(2,1)S(1)}, bf16[512,256]{1,0:T(8,128)(2,1)S(1)}, u32[]{:S(2)}, u32[]{:S(2)}) collective-permute-start(bf16[512,256]{1,0:T(8,128)(2,1)S(1)} %collective-permute-done.5.refs_0_), channel_id=1, source_target_pairs={{0,1},{1,0},{2,3},{3,2},{4,5},{5,4},{6,7},{7,6},{8,9},{9,8},{10,11... | collective-permute-start | bytes 786440 | tf_op jit(solution)/shard_map/ppermute | solution.py:45
  44.3 3.5 %collective-permute-done.6.refs_0_ = bf16[512,256]{1,0:T(8,128)(2,1)S(1)} collective-permute-done((bf16[512,256]{1,0:T(8,128)(2,1)S(1)}, bf16[512,256]{1,0:T(8,128)(2,1)S(1)}, u32[]{:S(2)}, u32[]{:S(2)}) %collective-permute-start.6) | collective-permute-done | bytes 262176 | tf_op jit(solution)/shard_map/ppermute | solution.py:36
  47.8 2.0 %collective-permute-start.9 = (bf16[512,256]{1,0:T(8,128)(2,1)S(1)}, bf16[512,256]{1,0:T(8,128)(2,1)S(1)}, u32[]{:S(2)}, u32[]{:S(2)}) collective-permute-start(bf16[512,256]{1,0:T(8,128)(2,1)S(1)} %collective-permute-done.6.refs_0_), channel_id=1, source_target_pairs={{0,1},{1,0},{2,3},{3,2},{4,5},{5,4},{6,7},{7,6},{8,9},{9,8},{10,11... | collective-permute-start | bytes 786440 | tf_op jit(solution)/shard_map/ppermute | solution.py:45
  49.8 1.6 %collective-permute-start.13 = (bf16[512,256]{1,0:T(8,128)(2,1)S(1)}, bf16[512,256]{1,0:T(8,128)(2,1)S(1)}, u32[]{:S(2)}, u32[]{:S(2)}) collective-permute-start(bf16[512,256]{1,0:T(8,128)(2,1)S(1)} %collective-permute-done.12.refs_4_), channel_id=1, source_target_pairs={{0,1},{1,0},{2,3},{3,2},{4,5},{5,4},{6,7},{7,6},{8,9},{9,8},{10,11... | collective-permute-start | bytes 786440 | tf_op jit(solution)/shard_map/ppermute | solution.py:45
  51.4 6.3 %attend_own.1 = (f32[512,2048]{1,0:T(8,128)S(1)}, f32[512,1024]{1,0:T(8,128)S(1)}, f32[512,1024]{1,0:T(8,128)S(1)}) custom-call(s32[4]{0:T(128)S(1)} %convert_reduce_fusion.starts_ref, bf16[512,2048]{1,0:T(8,128)(2,1)S(1)} %copy-done, bf16[2,512,256]{2,1,0:T(8,128)(2,1)S(1)} %get-tuple-element.32.refs_0_), custom_call_target="tpu_custom_call" | custom-call | flops 2147483648 | bytes 4194304 | tf_op jit(solution)/shard_map/attend_own/pallas_call | solution.py:737
  57.7 10.4 %attend_mid.2 = (f32[512,2048]{1,0:T(8,128)S(1)}, f32[512,1024]{1,0:T(8,128)S(1)}, f32[512,1024]{1,0:T(8,128)S(1)}) custom-call(s32[4]{0:T(128)S(1)} %convert_reduce_fusion.starts_ref, bf16[512,2048]{1,0:T(8,128)(2,1)S(1)} %copy-done, ...), custom_call_target="tpu_custom_call", output_to_operand_aliasing={{0}: (4, {}), {1}: (5, {}), {2}: (6, {})} | custom-call | flops 2147483648 | bytes 4194304 | tf_op jit(solution)/shard_map/attend_mid/pallas_call | solution.py:737
  68.2 17.8 %attend_mid.3 = (f32[512,2048]{1,0:T(8,128)S(1)}, f32[512,1024]{1,0:T(8,128)S(1)}, f32[512,1024]{1,0:T(8,128)S(1)}) custom-call(s32[4]{0:T(128)S(1)} %convert_reduce_fusion.starts_ref, bf16[512,2048]{1,0:T(8,128)(2,1)S(1)} %copy-done, ...), custom_call_target="tpu_custom_call", output_to_operand_aliasing={{0}: (8, {}), {1}: (9, {}), {2}: (10, {})} | custom-call | flops 6442450944 | bytes 4194304 | tf_op jit(solution)/shard_map/attend_mid/pallas_call | solution.py:737
  86.1 10.9 %attend_end.1 = bf16[512,2048]{1,0:T(8,128)(2,1)} custom-call(s32[4]{0:T(128)S(1)} %convert_reduce_fusion.starts_ref, bf16[512,2048]{1,0:T(8,128)(2,1)S(1)} %copy-done, bf16[512,256]{1,0:T(8,128)(2,1)S(1)} %collective-permute-done.7.refs_0_, bf16[512,256]{1,0:T(8,128)(2,1)S(1)} %collective-permute-done.8.refs_1_, f32[512,2048]{1,0:T(8,128)S(1)} %get-tuple-element.39.refs_2_, ...), custom_call_target="tpu_custom_call" | custom-call | flops 2147483648 | bytes 4194304 | tf_op jit(solution)/shard_map/attend_end/pallas_call | solution.py:737
  (25 shorter events, 0.4 us)
Async XLA Ops:
  1.4 3.5 %collective-permute-start = (bf16[3,2048]{1,0:T(4,128)(2,1)S(1)}, bf16[3,2048]{1,0:T(4,128)(2,1)S(1)}, u32[]{:S(2)}, u32[]{:S(2)}) collective-permute-start(bf16[3,2048]{1,0:T(4,128)(2,1)S(1)} %slice.3), channel_id=1, source_target_pairs={{0,2},{2,4},{4,6},{6,8},{8,10},{10,12},{12,14},{14,0},{1,3},{3,5},... | collective-permute-start | bytes 36872 | tf_op jit(solution)/shard_map/ppermute | solution.py:36
  4.9 16.3 %copy-start.1 = (bf16[512,2048]{1,0:T(8,128)(2,1)S(1)}, bf16[512,2048]{1,0:T(8,128)(2,1)}, u32[]{:S(2)}) copy-start(bf16[512,2048]{1,0:T(8,128)(2,1)} %y_ref.1) | copy-start | bytes 6291460
  4.9 16.3 %copy-start.2 = (bf16[2048,512]{1,0:T(8,128)(2,1)S(1)}, bf16[2048,512]{1,0:T(8,128)(2,1)}, u32[]{:S(2)}) copy-start(bf16[2048,512]{1,0:T(8,128)(2,1)} %panel_ref.1) | copy-start | bytes 6291460
  4.9 16.3 %copy-start.3 = (f32[16,512]{1,0:T(8,128)S(1)}, f32[16,512]{1,0:T(8,128)}, u32[]{:S(2)}) copy-start(f32[16,512]{1,0:T(8,128)} %scale_ref.1) | copy-start | bytes 98308
  16.3 2.7 %collective-permute-start.1 = (f32[2,2048]{1,0:T(2,128)S(1)}, f32[2,2048]{1,0:T(2,128)S(1)}, u32[]{:S(2)}, u32[]{:S(2)}) collective-permute-start(f32[2,2048]{1,0:T(2,128)S(1)} %get-tuple-element.28.tot_ref), channel_id=1, source_target_pairs={{0,2},{2,0},{4,6},{6,4},{8,10},{10,8},{12,14},{14,12},{1,3},{3,1},... | collective-permute-start | bytes 49160 | tf_op jit(solution)/shard_map/ppermute | solution.py:41
  18.9 5.2 %collective-permute-start.2 = (f32[2,2048]{1,0:T(2,128)S(1)}, f32[2,2048]{1,0:T(2,128)S(1)}, u32[]{:S(2)}, u32[]{:S(2)}) collective-permute-start(f32[2,2048]{1,0:T(2,128)S(1)} %level.1), channel_id=1, source_target_pairs={{0,4},{2,6},{4,8},{6,10},{8,12},{10,14},{12,0},{14,2},{1,5},{3,7},... | collective-permute-start | bytes 49160 | tf_op jit(solution)/shard_map/ppermute | solution.py:36
  20.3 3.9 %collective-permute-start.3 = (f32[2,2048]{1,0:T(2,128)S(1)}, f32[2,2048]{1,0:T(2,128)S(1)}, u32[]{:S(2)}, u32[]{:S(2)}) collective-permute-start(f32[2,2048]{1,0:T(2,128)S(1)} %level.1), channel_id=1, source_target_pairs={{0,8},{2,10},{4,12},{6,14},{8,0},{10,2},{12,4},{14,6},{1,9},{3,11}... | collective-permute-start | bytes 49160 | tf_op jit(solution)/shard_map/ppermute | solution.py:36
  26.8 24.6 %copy-start = (bf16[512,2048]{1,0:T(8,128)(2,1)S(1)}, bf16[512,2048]{1,0:T(8,128)(2,1)}, u32[]{:S(2)}) copy-start(bf16[512,2048]{1,0:T(8,128)(2,1)} %q_ref.7) | copy-start | bytes 6291460
  26.8 6.3 %collective-permute-start.4 = (f32[512,512]{1,0:T(8,128)S(1)}, f32[512,512]{1,0:T(8,128)S(1)}, u32[]{:S(2)}, u32[]{:S(2)}) collective-permute-start(f32[512,512]{1,0:T(8,128)S(1)} %get-tuple-element.30.a_ref), channel_id=1, source_target_pairs={{0,1},{1,0},{2,3},{3,2},{4,5},{5,4},{6,7},{7,6},{8,9},{9,8},{10,11... | collective-permute-start | bytes 3145736 | tf_op jit(solution)/shard_map/ppermute | solution.py:45
  33.4 7.7 %collective-permute-start.5 = (bf16[512,256]{1,0:T(8,128)(2,1)S(1)}, bf16[512,256]{1,0:T(8,128)(2,1)S(1)}, u32[]{:S(2)}, u32[]{:S(2)}) collective-permute-start(bf16[512,256]{1,0:T(8,128)(2,1)S(1)} %get-tuple-element.31), channel_id=1, source_target_pairs={{0,4},{2,6},{4,8},{6,10},{8,12},{10,14},{12,0},{14,2},{1,5},{3,7},... | collective-permute-start | bytes 786440 | tf_op jit(solution)/shard_map/ppermute | solution.py:36
  35.2 9.0 %collective-permute-start.10 = (bf16[512,256]{1,0:T(8,128)(2,1)S(1)}, bf16[512,256]{1,0:T(8,128)(2,1)S(1)}, u32[]{:S(2)}, u32[]{:S(2)}) collective-permute-start(bf16[512,256]{1,0:T(8,128)(2,1)S(1)} %get-tuple-element.31), channel_id=1, source_target_pairs={{0,2},{2,0},{4,6},{6,4},{8,10},{10,8},{12,14},{14,12},{1,3},{3,1},... | collective-permute-start | bytes 786440 | tf_op jit(solution)/shard_map/ppermute | solution.py:41
  41.1 6.7 %collective-permute-start.6 = (bf16[512,256]{1,0:T(8,128)(2,1)S(1)}, bf16[512,256]{1,0:T(8,128)(2,1)S(1)}, u32[]{:S(2)}, u32[]{:S(2)}) collective-permute-start(bf16[512,256]{1,0:T(8,128)(2,1)S(1)} %collective-permute-done.5.refs_0_), channel_id=1, source_target_pairs={{0,4},{2,6},{4,8},{6,10},{8,12},{10,14},{12,0},{14,2},{1,5},{3,7},... | collective-permute-start | bytes 786440 | tf_op jit(solution)/shard_map/ppermute | solution.py:36
  42.7 7.1 %collective-permute-start.12 = (bf16[512,256]{1,0:T(8,128)(2,1)S(1)}, bf16[512,256]{1,0:T(8,128)(2,1)S(1)}, u32[]{:S(2)}, u32[]{:S(2)}) collective-permute-start(bf16[512,256]{1,0:T(8,128)(2,1)S(1)} %collective-permute-done.5.refs_0_), channel_id=1, source_target_pairs={{0,2},{2,0},{4,6},{6,4},{8,10},{10,8},{12,14},{14,12},{1,3},{3,1},... | collective-permute-start | bytes 786440 | tf_op jit(solution)/shard_map/ppermute | solution.py:41
  42.7 15.0 %collective-permute-start.14 = (bf16[512,256]{1,0:T(8,128)(2,1)S(1)}, bf16[512,256]{1,0:T(8,128)(2,1)S(1)}, u32[]{:S(2)}, u32[]{:S(2)}) collective-permute-start(bf16[512,256]{1,0:T(8,128)(2,1)S(1)} %collective-permute-done.5.refs_0_), channel_id=1, source_target_pairs={{0,1},{1,0},{2,3},{3,2},{4,5},{5,4},{6,7},{7,6},{8,9},{9,8},{10,11... | collective-permute-start | bytes 786440 | tf_op jit(solution)/shard_map/ppermute | solution.py:45
  44.2 24.0 %collective-permute-start.11 = (bf16[512,256]{1,0:T(8,128)(2,1)S(1)}, bf16[512,256]{1,0:T(8,128)(2,1)S(1)}, u32[]{:S(2)}, u32[]{:S(2)}) collective-permute-start(bf16[512,256]{1,0:T(8,128)(2,1)S(1)} %collective-permute-done.10.refs_2_), channel_id=1, source_target_pairs={{0,1},{1,0},{2,3},{3,2},{4,5},{5,4},{6,7},{7,6},{8,9},{9,8},{10,11... | collective-permute-start | bytes 786440 | tf_op jit(solution)/shard_map/ppermute | solution.py:45
  47.8 20.4 %collective-permute-start.9 = (bf16[512,256]{1,0:T(8,128)(2,1)S(1)}, bf16[512,256]{1,0:T(8,128)(2,1)S(1)}, u32[]{:S(2)}, u32[]{:S(2)}) collective-permute-start(bf16[512,256]{1,0:T(8,128)(2,1)S(1)} %collective-permute-done.6.refs_0_), channel_id=1, source_target_pairs={{0,1},{1,0},{2,3},{3,2},{4,5},{5,4},{6,7},{7,6},{8,9},{9,8},{10,11... | collective-permute-start | bytes 786440 | tf_op jit(solution)/shard_map/ppermute | solution.py:45
  49.8 18.3 %collective-permute-start.7 = (bf16[512,256]{1,0:T(8,128)(2,1)S(1)}, bf16[512,256]{1,0:T(8,128)(2,1)S(1)}, u32[]{:S(2)}, u32[]{:S(2)}) collective-permute-start(bf16[512,256]{1,0:T(8,128)(2,1)S(1)} %collective-permute-done.6.refs_0_), channel_id=1, source_target_pairs={{0,2},{2,0},{4,6},{6,4},{8,10},{10,8},{12,14},{14,12},{1,3},{3,1},... | collective-permute-start | bytes 786440 | tf_op jit(solution)/shard_map/ppermute | solution.py:41
  49.8 18.4 %collective-permute-start.13 = (bf16[512,256]{1,0:T(8,128)(2,1)S(1)}, bf16[512,256]{1,0:T(8,128)(2,1)S(1)}, u32[]{:S(2)}, u32[]{:S(2)}) collective-permute-start(bf16[512,256]{1,0:T(8,128)(2,1)S(1)} %collective-permute-done.12.refs_4_), channel_id=1, source_target_pairs={{0,1},{1,0},{2,3},{3,2},{4,5},{5,4},{6,7},{7,6},{8,9},{9,8},{10,11... | collective-permute-start | bytes 786440 | tf_op jit(solution)/shard_map/ppermute | solution.py:45
  68.1 17.9 %collective-permute-start.8 = (bf16[512,256]{1,0:T(8,128)(2,1)S(1)}, bf16[512,256]{1,0:T(8,128)(2,1)S(1)}, u32[]{:S(2)}, u32[]{:S(2)}) collective-permute-start(bf16[512,256]{1,0:T(8,128)(2,1)S(1)} %collective-permute-done.7.refs_0_), channel_id=1, source_target_pairs={{0,1},{1,0},{2,3},{3,2},{4,5},{5,4},{6,7},{7,6},{8,9},{9,8},{10,11... | collective-permute-start | bytes 786440 | tf_op jit(solution)/shard_map/ppermute | solution.py:45
